TPU v7x, 32 devices: a whole 2x2x4 slice. The times are simulated.
32 devices in a mesh: section: 2 (over core), dp: 4 (over z), tensor: 4 (over y, x).
Axes of the slice: x: 2, y: 2, z: 4, core: 2. Of those that a mesh axis runs over, the one named last changes fastest.
Arguments:
- block_input: bfloat16 [2, 8, 1024, 768], P('section', 'dp', 'tensor'), may hold values from -6 to 6
- w_self: bfloat16 [2, 768, 3, 768], P('section', 'dp', None, 'tensor'), may hold values from -0.21875 to 0.21875
- w_self_out: bfloat16 [2, 768, 768], P('section', 'tensor', 'dp'), may hold values from -3 to 3
- w_cross: bfloat16 [2, 768, 2, 768], P('section', 'dp', None, 'tensor')
- w_up: bfloat16 [2, 768, 3072], P('section', 'dp', 'tensor'), may hold values from -0.21875 to 0.21875
- w_down: bfloat16 [2, 3072, 768], P('section', 'tensor', 'dp'), may hold values from -0.109375 to 0.109375
- norm_gains: bfloat16 [2, 3, 768], P('section'), may hold values from 0.5 to 1.5
- lengths: int32 [2, 8], P(None, 'dp'), may hold values from 128 to 1024, as said below
- task_mask: int32 [8, 1024], P('dp'), may hold values from 0 to 1, as said below
- out_grad: bfloat16 [8, 1024, 768], P('dp', 'tensor'), may hold values from -6 to 6
Outputs:
- block_output: bfloat16 [2, 8, 1024, 768], P('section', 'dp', 'tensor')
- input_grad: float32 [2, 8, 1024, 768], P('section', 'dp', 'tensor')
- w_self_grad: float32 [2, 768, 3, 768], P('section', 'dp', None, 'tensor')
- w_self_out_grad: float32 [2, 768, 768], P('section', 'tensor', 'dp')
- w_cross_grad: float32 [2, 768, 2, 768], P('section', 'dp', None, 'tensor')
- w_up_grad: float32 [2, 768, 3072], P('section', 'dp', 'tensor')
- w_down_grad: float32 [2, 3072, 768], P('section', 'tensor', 'dp')
- gains_grad: float32 [2, 2, 768], P('section')
- last_gain_grad: float32 [2, 768], P('section')
Inputs may be any that keep to these rules, and one draw needn't show every extreme that they name: Row 0 holds encoder lengths and row 1 decoder lengths; the first sequence has length 1024 in both rows. `task_mask`: position 0 of every sequence is 1.
All inputs are finite; a program needn't handle non-finite values.
Results may differ from a plain program's by a relative error of at most 0.02.
Values may be sent and summed in bfloat16 or wider, within the bound.
A program may use at most 320 MiB of HBM per device.

v0:
```python
import jax
import jax.numpy as jnp
from jax import lax
from jax.sharding import PartitionSpec as P

HEAD = 64
MICRO = 2


EPSILON = 1e-05
SCORE_SCALE = 0.125
NEG_FILL = -1000000000.0


def from_behind(shard, axis, by):
    size = lax.axis_size(axis)
    pairs = [(i, i + by) for i in range(size) if 0 <= i + by < size]
    return lax.ppermute(shard, axis, pairs)


def layer_norm(values, gain_row):
    centred = values - jnp.mean(values, axis=-1, keepdims=True)
    spread = jnp.mean(centred * centred, axis=-1, keepdims=True)
    return centred * lax.rsqrt(spread + EPSILON) * gain_row


def norm_back(values, gain_row, grad_rows):
    _, pullback = jax.vjp(layer_norm, values, gain_row)
    return pullback(grad_rows)


def spread_rows(normed):
    return lax.all_gather(normed, "tensor", axis=1, tiled=True)


def collect_rows(partial_value):
    return lax.psum_scatter(
        partial_value.astype(jnp.bfloat16), "tensor", scatter_dimension=1, tiled=True
    ).astype(jnp.float32)


def spread_grads(grad_low):
    return lax.all_gather(grad_low, "tensor", axis=1, tiled=True)


def return_rows(partial_value):
    return lax.psum_scatter(
        partial_value.astype(jnp.bfloat16), "tensor", scatter_dimension=1, tiled=True
    ).astype(jnp.float32)


def fetch_weights(w_self, w_self_out, w_cross, w_up, w_down):
    gathered = (
        lax.all_gather(w_self, "dp", axis=1, tiled=True),
        lax.all_gather(w_self_out, "dp", axis=2, tiled=True),
        lax.all_gather(w_cross, "dp", axis=1, tiled=True),
        lax.all_gather(w_up, "dp", axis=1, tiled=True),
        lax.all_gather(w_down, "dp", axis=2, tiled=True),
    )
    return tuple((gathered_piece[0] for gathered_piece in gathered))


def reduce_grads(grad_terms):
    weight_terms = tuple((grad_piece[None] for grad_piece in grad_terms[:5]))
    shares = (
        lax.psum_scatter(
            weight_terms[0].astype(jnp.bfloat16), "dp", scatter_dimension=1, tiled=True
        ).astype(jnp.float32),
        lax.psum_scatter(
            weight_terms[1].astype(jnp.bfloat16), "dp", scatter_dimension=2, tiled=True
        ).astype(jnp.float32),
        lax.psum_scatter(
            weight_terms[2].astype(jnp.bfloat16), "dp", scatter_dimension=1, tiled=True
        ).astype(jnp.float32),
        lax.psum_scatter(
            weight_terms[3].astype(jnp.bfloat16), "dp", scatter_dimension=1, tiled=True
        ).astype(jnp.float32),
        lax.psum_scatter(
            weight_terms[4].astype(jnp.bfloat16), "dp", scatter_dimension=2, tiled=True
        ).astype(jnp.float32),
    )
    gain_total = lax.psum(grad_terms[5][None], ("dp", "tensor"))
    return tuple(shares) + (gain_total,)


def make_masks(lengths_now, task_rows, is_decoder, slot_rows):
    positions = jnp.arange(slot_rows)
    own_length = jnp.where(is_decoder, lengths_now[1], lengths_now[0])

    def self_allowed(sequence, query_pos):
        inside = positions[None, :] < own_length[sequence]
        earlier = positions[None, :] <= query_pos[:, None]
        return inside & (earlier | jnp.logical_not(is_decoder))

    def cross_allowed(sequence, query_pos):
        inside = (positions < lengths_now[0][sequence]) & (task_rows[sequence] == 1)
        return jnp.broadcast_to(inside[None, :], (query_pos.shape[0], slot_rows))

    return (self_allowed, cross_allowed)


def attend(queries, key_rows, value_rows, allowed):
    seq_count, slot_rows, head_width = queries.shape
    head_count = head_width // HEAD
    block_rows = min(512, slot_rows)
    per_seq = slot_rows // block_rows

    def one_block(block_index):
        sequence = block_index // per_seq
        first_row = block_index % per_seq * block_rows
        query_block = lax.dynamic_slice(
            queries, (sequence, first_row, 0), (1, block_rows, head_width)
        ).reshape(block_rows, head_count, HEAD)
        key_seq = lax.dynamic_index_in_dim(key_rows, sequence, 0, keepdims=False).reshape(
            slot_rows, head_count, HEAD
        )
        value_seq = lax.dynamic_index_in_dim(value_rows, sequence, 0, keepdims=False).reshape(
            slot_rows, head_count, HEAD
        )
        scores = (
            jnp.einsum("qhd,khd->hqk", query_block, key_seq, preferred_element_type=jnp.float32)
            * SCORE_SCALE
        )
        allowed_now = allowed(sequence, first_row + jnp.arange(block_rows))
        scores = jnp.where(allowed_now[None], scores, NEG_FILL)
        row_top = jnp.max(scores, axis=-1, keepdims=True)
        exponent = jnp.exp(scores - row_top)
        row_total = jnp.sum(exponent, axis=-1, keepdims=True)
        attn_probs = (exponent / row_total).astype(jnp.bfloat16)
        result = jnp.einsum(
            "hqk,khd->qhd", attn_probs, value_seq, preferred_element_type=jnp.float32
        )
        return (
            result.astype(jnp.bfloat16).reshape(block_rows, head_width),
            (row_top + jnp.log(row_total))[..., 0],
        )

    outputs, log_sums = lax.map(one_block, jnp.arange(seq_count * per_seq))
    return (outputs.reshape(seq_count, slot_rows, head_width), log_sums)


def attend_back(queries, key_rows, value_rows, log_sums, d_attended, allowed):
    seq_count, slot_rows, head_width = queries.shape
    head_count = head_width // HEAD
    block_rows = min(512, slot_rows)
    per_seq = slot_rows // block_rows
    zero_grad = jnp.zeros((seq_count, slot_rows, head_count, HEAD), jnp.float32)

    def one_block(carry, block_index):
        d_keys, d_values = carry
        sequence = block_index // per_seq
        first_row = block_index % per_seq * block_rows
        query_block = lax.dynamic_slice(
            queries, (sequence, first_row, 0), (1, block_rows, head_width)
        ).reshape(block_rows, head_count, HEAD)
        grad_block = lax.dynamic_slice(
            d_attended, (sequence, first_row, 0), (1, block_rows, head_width)
        ).reshape(block_rows, head_count, HEAD)
        key_seq = lax.dynamic_index_in_dim(key_rows, sequence, 0, keepdims=False).reshape(
            slot_rows, head_count, HEAD
        )
        value_seq = lax.dynamic_index_in_dim(value_rows, sequence, 0, keepdims=False).reshape(
            slot_rows, head_count, HEAD
        )
        scores = (
            jnp.einsum("qhd,khd->hqk", query_block, key_seq, preferred_element_type=jnp.float32)
            * SCORE_SCALE
        )
        allowed_now = allowed(sequence, first_row + jnp.arange(block_rows))
        scores = jnp.where(allowed_now[None], scores, NEG_FILL)
        lse_block = lax.dynamic_index_in_dim(log_sums, block_index, 0, keepdims=False)
        attn_probs = jnp.exp(scores - lse_block[:, :, None])
        low_probs = attn_probs.astype(jnp.bfloat16)
        d_probs = jnp.einsum(
            "qhd,khd->hqk", grad_block, value_seq, preferred_element_type=jnp.float32
        )
        value_part = jnp.einsum(
            "hqk,qhd->khd", low_probs, grad_block, preferred_element_type=jnp.float32
        )
        inner_sum = jnp.sum(attn_probs * d_probs, axis=-1, keepdims=True)
        d_scores = (attn_probs * (d_probs - inner_sum)).astype(jnp.bfloat16)
        d_query = (
            jnp.einsum("hqk,khd->qhd", d_scores, key_seq, preferred_element_type=jnp.float32)
            * SCORE_SCALE
        )
        key_part = (
            jnp.einsum("hqk,qhd->khd", d_scores, query_block, preferred_element_type=jnp.float32)
            * SCORE_SCALE
        )
        key_now = lax.dynamic_index_in_dim(d_keys, sequence, 0, keepdims=False)
        value_now = lax.dynamic_index_in_dim(d_values, sequence, 0, keepdims=False)
        d_keys = lax.dynamic_update_index_in_dim(d_keys, key_now + key_part, sequence, 0)
        d_values = lax.dynamic_update_index_in_dim(d_values, value_now + value_part, sequence, 0)
        return ((d_keys, d_values), d_query.astype(jnp.bfloat16).reshape(block_rows, head_width))

    (d_keys, d_values), d_queries = lax.scan(
        one_block, (zero_grad, zero_grad), jnp.arange(seq_count * per_seq)
    )
    shape_out = (seq_count, slot_rows, head_width)
    return (
        d_queries.reshape(shape_out),
        d_keys.astype(jnp.bfloat16).reshape(shape_out),
        d_values.astype(jnp.bfloat16).reshape(shape_out),
    )


def feed_forward(full_rows, w_up, w_down):
    pre_act = jnp.dot(full_rows, w_up, preferred_element_type=jnp.float32)
    activation = jax.nn.gelu(pre_act).astype(jnp.bfloat16)
    branch = jnp.dot(activation, w_down, preferred_element_type=jnp.float32)
    return (branch, pre_act, activation)


def feed_back(full_rows, pre_act, activation, grad_full, w_up, w_down):
    d_activation = jnp.einsum("rd,fd->rf", grad_full, w_down, preferred_element_type=jnp.float32)
    _, gelu_pull = jax.vjp(jax.nn.gelu, pre_act)
    d_pre = gelu_pull(d_activation)[0].astype(jnp.bfloat16)
    d_down = jnp.einsum("rf,rd->fd", activation, grad_full, preferred_element_type=jnp.float32)
    d_up = jnp.einsum("rd,rf->df", full_rows, d_pre, preferred_element_type=jnp.float32)
    d_rows = jnp.einsum("rf,df->rd", d_pre, w_up, preferred_element_type=jnp.float32)
    return (d_rows, d_up, d_down)


def block_forward(x_rows, weights, lengths_now, task_rows, is_decoder, kv_in):
    w_self, w_self_out, w_cross, w_up, w_down, gain_rows = weights
    seq_count, slot_local, model_width = x_rows.shape
    slot_rows = task_rows.shape[1]
    head_width = w_self.shape[2]
    hidden_width = w_up.shape[1]
    total_rows = seq_count * slot_rows
    self_allowed, cross_allowed = make_masks(lengths_now, task_rows, is_decoder, slot_rows)
    normed_first = layer_norm(x_rows, gain_rows[0]).astype(jnp.bfloat16)
    full_first = spread_rows(normed_first).reshape(total_rows, model_width)
    projected = jnp.einsum(
        "rd,dkh->krh", full_first, w_self, preferred_element_type=jnp.float32
    ).astype(jnp.bfloat16)
    queries = projected[0].reshape(seq_count, slot_rows, head_width)
    key_rows = projected[1].reshape(seq_count, slot_rows, head_width)
    value_rows = projected[2].reshape(seq_count, slot_rows, head_width)
    attended, self_lse = attend(queries, key_rows, value_rows, self_allowed)
    partial_value = jnp.dot(
        attended.reshape(total_rows, head_width), w_self_out, preferred_element_type=jnp.float32
    )
    x_mid = x_rows + collect_rows(partial_value.reshape(seq_count, slot_rows, model_width))
    normed_second = layer_norm(x_mid, gain_rows[1]).astype(jnp.bfloat16)
    full_second = spread_rows(normed_second).reshape(total_rows, model_width)

    def cross_branch(full_rows):
        cross_queries = jnp.dot(
            full_rows, w_cross[:, 0, :], preferred_element_type=jnp.float32
        ).astype(jnp.bfloat16)
        cross_queries = cross_queries.reshape(seq_count, slot_rows, head_width)
        cross_attended, cross_lse = attend(cross_queries, kv_in[0], kv_in[1], cross_allowed)
        branch = jnp.einsum(
            "rh,dh->rd",
            cross_attended.reshape(total_rows, head_width),
            w_cross[:, 1, :],
            preferred_element_type=jnp.float32,
        )
        return (
            branch,
            cross_queries,
            cross_attended,
            cross_lse,
            jnp.zeros((total_rows, hidden_width), jnp.float32),
            jnp.zeros((total_rows, hidden_width), jnp.bfloat16),
        )

    def encoder_ffn(full_rows):
        branch, pre_act, activation = feed_forward(full_rows, w_up, w_down)
        blank = jnp.zeros((seq_count, slot_rows, head_width), jnp.bfloat16)
        return (branch, blank, blank, jnp.zeros(self_lse.shape, jnp.float32), pre_act, activation)

    branch_mid, cross_queries, cross_attended, cross_lse, pre_mid, act_mid = lax.cond(
        is_decoder, cross_branch, encoder_ffn, full_second
    )
    x_late = x_mid + collect_rows(branch_mid.reshape(seq_count, slot_rows, model_width))
    normed_third = layer_norm(x_late, gain_rows[2]).astype(jnp.bfloat16)
    full_third = spread_rows(normed_third).reshape(total_rows, model_width)

    def decoder_ffn(full_rows):
        branch, pre_act, activation = feed_forward(full_rows, w_up, w_down)
        return (
            branch,
            pre_act,
            activation,
            jnp.zeros((2, seq_count, slot_rows, head_width), jnp.bfloat16),
        )

    def memory_branch(full_rows):
        memory_kv = jnp.einsum(
            "rd,dkh->krh", full_rows, w_cross, preferred_element_type=jnp.float32
        ).astype(jnp.bfloat16)
        return (
            jnp.zeros((total_rows, model_width), jnp.float32),
            jnp.zeros((total_rows, hidden_width), jnp.float32),
            jnp.zeros((total_rows, hidden_width), jnp.bfloat16),
            memory_kv.reshape(2, seq_count, slot_rows, head_width),
        )

    branch_last, pre_last, act_last, kv_out = lax.cond(
        is_decoder, decoder_ffn, memory_branch, full_third
    )
    x_out = x_late + collect_rows(branch_last.reshape(seq_count, slot_rows, model_width))
    result = jnp.where(is_decoder, x_out.astype(jnp.bfloat16), normed_third)
    saved_state = {
        "x_rows": x_rows,
        "x_mid": x_mid,
        "x_late": x_late,
        "full_first": full_first,
        "queries": queries,
        "key_rows": key_rows,
        "value_rows": value_rows,
        "attended": attended,
        "self_lse": self_lse,
        "full_second": full_second,
        "cross_queries": cross_queries,
        "cross_attended": cross_attended,
        "cross_lse": cross_lse,
        "pre_mid": pre_mid,
        "act_mid": act_mid,
        "full_third": full_third,
        "pre_last": pre_last,
        "act_last": act_last,
        "kv_in": kv_in,
    }
    return (result, kv_out, saved_state)


def block_backward(saved_state, grad_rows, kv_grads, weights, lengths_now, task_rows, is_decoder):
    w_self, w_self_out, w_cross, w_up, w_down, gain_rows = weights
    seq_count, slot_local, model_width = grad_rows.shape
    slot_rows = task_rows.shape[1]
    head_width = w_self.shape[2]
    total_rows = seq_count * slot_rows
    self_allowed, cross_allowed = make_masks(lengths_now, task_rows, is_decoder, slot_rows)
    kv_in = saved_state["kv_in"]
    grad_third = spread_grads(grad_rows.astype(jnp.bfloat16)).reshape(total_rows, model_width)

    def decoder_ffn_back(grad_full):
        d_rows, d_up, d_down = feed_back(
            saved_state["full_third"],
            saved_state["pre_last"],
            saved_state["act_last"],
            grad_full,
            w_up,
            w_down,
        )
        return (d_rows, d_up, d_down, jnp.zeros(w_cross.shape, jnp.float32))

    def memory_back(grad_full):
        pieces = kv_grads.reshape(2, total_rows, head_width)
        d_rows = jnp.einsum("krh,dkh->rd", pieces, w_cross, preferred_element_type=jnp.float32)
        d_cross = jnp.einsum(
            "rd,krh->dkh", saved_state["full_third"], pieces, preferred_element_type=jnp.float32
        )
        return (
            d_rows,
            jnp.zeros(w_up.shape, jnp.float32),
            jnp.zeros(w_down.shape, jnp.float32),
            d_cross,
        )

    d_rows_last, d_up_last, d_down_last, d_cross_last = lax.cond(
        is_decoder, decoder_ffn_back, memory_back, grad_third
    )
    d_normed = return_rows(d_rows_last.reshape(seq_count, slot_rows, model_width))
    d_from_norm, d_gain_third = norm_back(saved_state["x_late"], gain_rows[2], d_normed)
    d_late = grad_rows + d_from_norm
    grad_second = spread_grads(d_late.astype(jnp.bfloat16)).reshape(total_rows, model_width)

    def cross_back(grad_full):
        d_attended = jnp.dot(
            grad_full, w_cross[:, 1, :], preferred_element_type=jnp.float32
        ).astype(jnp.bfloat16)
        d_output = jnp.einsum(
            "rd,rh->dh",
            grad_full,
            saved_state["cross_attended"].reshape(total_rows, head_width),
            preferred_element_type=jnp.float32,
        )
        d_queries, d_key_c, d_value_c = attend_back(
            saved_state["cross_queries"],
            kv_in[0],
            kv_in[1],
            saved_state["cross_lse"],
            d_attended.reshape(seq_count, slot_rows, head_width),
            cross_allowed,
        )
        flat_queries = d_queries.reshape(total_rows, head_width)
        d_input = jnp.einsum(
            "rd,rh->dh",
            saved_state["full_second"],
            flat_queries,
            preferred_element_type=jnp.float32,
        )
        d_rows = jnp.einsum(
            "rh,dh->rd", flat_queries, w_cross[:, 0, :], preferred_element_type=jnp.float32
        )
        return (
            d_rows,
            jnp.zeros(w_up.shape, jnp.float32),
            jnp.zeros(w_down.shape, jnp.float32),
            jnp.stack([d_input, d_output], axis=1),
            jnp.stack([d_key_c, d_value_c]),
        )

    def encoder_ffn_back(grad_full):
        d_rows, d_up, d_down = feed_back(
            saved_state["full_second"],
            saved_state["pre_mid"],
            saved_state["act_mid"],
            grad_full,
            w_up,
            w_down,
        )
        return (
            d_rows,
            d_up,
            d_down,
            jnp.zeros(w_cross.shape, jnp.float32),
            jnp.zeros((2, seq_count, slot_rows, head_width), jnp.bfloat16),
        )

    d_rows_mid, d_up_mid, d_down_mid, d_cross_mid, kv_grad_out = lax.cond(
        is_decoder, cross_back, encoder_ffn_back, grad_second
    )
    d_normed = return_rows(d_rows_mid.reshape(seq_count, slot_rows, model_width))
    d_from_norm, d_gain_second = norm_back(saved_state["x_mid"], gain_rows[1], d_normed)
    d_mid = d_late + d_from_norm
    grad_first = spread_grads(d_mid.astype(jnp.bfloat16)).reshape(total_rows, model_width)
    d_attended = jnp.einsum(
        "rd,hd->rh", grad_first, w_self_out, preferred_element_type=jnp.float32
    ).astype(jnp.bfloat16)
    d_self_out = jnp.einsum(
        "rh,rd->hd",
        saved_state["attended"].reshape(total_rows, head_width),
        grad_first,
        preferred_element_type=jnp.float32,
    )
    d_query, d_key, d_value = attend_back(
        saved_state["queries"],
        saved_state["key_rows"],
        saved_state["value_rows"],
        saved_state["self_lse"],
        d_attended.reshape(seq_count, slot_rows, head_width),
        self_allowed,
    )
    stacked = jnp.stack([d_query, d_key, d_value]).reshape(3, total_rows, head_width)
    d_self = jnp.einsum(
        "rd,krh->dkh", saved_state["full_first"], stacked, preferred_element_type=jnp.float32
    )
    d_rows_first = jnp.einsum("krh,dkh->rd", stacked, w_self, preferred_element_type=jnp.float32)
    d_normed = return_rows(d_rows_first.reshape(seq_count, slot_rows, model_width))
    d_from_norm, d_gain_first = norm_back(saved_state["x_rows"], gain_rows[0], d_normed)
    d_input_rows = d_mid + d_from_norm
    grad_terms = (
        d_self,
        d_self_out,
        d_cross_mid + d_cross_last,
        d_up_mid + d_up_last,
        d_down_mid + d_down_last,
        jnp.stack([d_gain_first, d_gain_second, d_gain_third]),
    )
    return (d_input_rows, grad_terms, kv_grad_out)


def body(
    block_input, w_self, w_self_out, w_cross, w_up, w_down, norm_gains, lengths, task_mask, out_grad
):
    section_index = lax.axis_index("section")
    is_decoder = section_index == 1
    micro_count = MICRO
    local_seqs, slot_local, model_width = block_input.shape[1:]
    per_micro = local_seqs // micro_count
    slot_rows = task_mask.shape[1]
    head_width = w_self.shape[3]
    inputs = block_input[0].reshape(micro_count, per_micro, slot_local, model_width)
    cotangents = out_grad.reshape(micro_count, per_micro, slot_local, model_width)
    lengths_all = lengths.reshape(2, micro_count, per_micro)
    tasks_all = task_mask.reshape(micro_count, per_micro, slot_rows)
    gain_rows = norm_gains[0].astype(jnp.float32)
    kv_held = jnp.zeros((2, per_micro, slot_rows, head_width), jnp.bfloat16)
    outputs = jnp.zeros((micro_count, per_micro, slot_local, model_width), jnp.bfloat16)
    records = []
    for tick_index in range(micro_count + 1):
        fetched = fetch_weights(w_self, w_self_out, w_cross, w_up, w_down)
        weights = fetched + (gain_rows,)
        offset = tick_index - section_index
        is_live = (offset >= 0) & (offset < micro_count)
        micro_index = jnp.clip(offset, 0, micro_count - 1)
        x_rows = lax.dynamic_index_in_dim(inputs, micro_index, 0, keepdims=False).astype(
            jnp.float32
        )
        lengths_now = lax.dynamic_index_in_dim(lengths_all, micro_index, 1, keepdims=False)
        tasks_now = lax.dynamic_index_in_dim(tasks_all, micro_index, 0, keepdims=False)
        result, kv_out, saved_state = block_forward(
            x_rows, weights, lengths_now, tasks_now, is_decoder, kv_held
        )
        previous = lax.dynamic_index_in_dim(outputs, micro_index, 0, keepdims=False)
        outputs = lax.dynamic_update_index_in_dim(
            outputs, jnp.where(is_live, result, previous), micro_index, 0
        )
        kept_state = saved_state
        records.append((kept_state, micro_index, is_live, lengths_now, tasks_now))
        kv_held = from_behind(kv_out, "section", 1)
    kv_grads = jnp.zeros((2, per_micro, slot_rows, head_width), jnp.bfloat16)
    input_grads = jnp.zeros((micro_count, per_micro, slot_local, model_width), jnp.float32)
    grad_totals = None
    for back_index in range(micro_count + 1):
        kept_state, micro_index, is_live, lengths_now, tasks_now = records[micro_count - back_index]
        fetched = fetch_weights(w_self, w_self_out, w_cross, w_up, w_down)
        weights = fetched + (gain_rows,)
        saved_state = kept_state
        cot_rows = lax.dynamic_index_in_dim(cotangents, micro_index, 0, keepdims=False).astype(
            jnp.float32
        )
        cot_rows = jnp.where(is_decoder, cot_rows, 0.0)
        d_input_rows, grad_terms, kv_grad_out = block_backward(
            saved_state, cot_rows, kv_grads, weights, lengths_now, tasks_now, is_decoder
        )
        kv_grads = from_behind(kv_grad_out, "section", -1)
        previous = lax.dynamic_index_in_dim(input_grads, micro_index, 0, keepdims=False)
        input_grads = lax.dynamic_update_index_in_dim(
            input_grads, jnp.where(is_live, d_input_rows, previous), micro_index, 0
        )
        live_scale = is_live.astype(jnp.float32)
        grad_terms = tuple((grad_piece * live_scale for grad_piece in grad_terms))
        shares = reduce_grads(grad_terms)
        grad_totals = (
            shares
            if grad_totals is None
            else tuple((first + second for first, second in zip(grad_totals, shares)))
        )
    gain_totals = grad_totals[5]
    return (
        outputs.reshape(1, local_seqs, slot_local, model_width),
        input_grads.reshape(1, local_seqs, slot_local, model_width),
        grad_totals[0],
        grad_totals[1],
        grad_totals[2],
        grad_totals[3],
        grad_totals[4],
        gain_totals[:, :2],
        gain_totals[:, 2],
    )


def solution(mesh):
    placed = (
        P("section", "dp", "tensor", None),
        P("section", "dp", None, "tensor"),
        P("section", "tensor", "dp"),
        P("section", "dp", None, "tensor"),
        P("section", "dp", "tensor"),
        P("section", "tensor", "dp"),
        P("section", None, None),
        P(None, "dp"),
        P("dp", None),
        P("dp", "tensor", None),
    )
    return jax.shard_map(
        body,
        mesh=mesh,
        in_specs=placed,
        out_specs=(
            P("section", "dp", "tensor", None),
            P("section", "dp", "tensor", None),
            P("section", "dp", None, "tensor"),
            P("section", "tensor", "dp"),
            P("section", "dp", None, "tensor"),
            P("section", "dp", "tensor"),
            P("section", "tensor", "dp"),
            P("section", None, None),
            P("section", None),
        ),
        check_vma=False,
    )
```

profile of v0, /device:TPU:2, one launch (start us, length us, event | category | flops | bytes accessed | tf_op | source)
XLA Modules:
  0.0 2012.4 jit_solution(5622114597771258653)
XLA Ops:
  15.8 30.1 %all_gather.47 = bf16[1,768,3,192]{3,2,0,1:T(4,128)(2,1)S(1)} all-gather(bf16[1,192,3,192]{3,2,0,1:T(4,128)(2,1)S(1)} %copy.240), channel_id=1, replica_groups=mesh['section'=2,'dp'=4,'tensor'=4] {'dp'}, dimensions={1}, use_global_device_ids=true | all-gather | bytes 1105920 | tf_op jit(solution)/shard_map/all_gather | solution.py:54
  100.6 30.4 %reduce-scatter.70.cloned.1.call-done = bf16[1,256,768]{2,1,0:T(8,128)(2,1)} async-done(((bf16[1,1024,768]{2,1,0:T(8,128)(2,1)}), bf16[1,256,768]{2,1,0:T(8,128)(2,1)}) %reduce-scatter.70.cloned.1.call-update) | async-done | bytes 393232 | tf_op jit(solution)/shard_map/reduce_scatter | solution.py:37
  232.9 33.8 %reduce-scatter.58.cloned.1.call-done = bf16[1,256,768]{2,1,0:T(8,128)(2,1)} async-done(((bf16[1,1024,768]{2,1,0:T(8,128)(2,1)}), bf16[1,256,768]{2,1,0:T(8,128)(2,1)}) %reduce-scatter.58.cloned.1.call-update) | async-done | bytes 393232 | tf_op jit(solution)/shard_map/reduce_scatter | solution.py:37
  337.3 44.8 %reduce-scatter.60.cloned.1.call-done = bf16[1,256,768]{2,1,0:T(8,128)(2,1)} async-done(((bf16[1,1024,768]{2,1,0:T(8,128)(2,1)}), bf16[1,256,768]{2,1,0:T(8,128)(2,1)}) %reduce-scatter.60.cloned.1.call-update) | async-done | bytes 393232 | tf_op jit(solution)/shard_map/reduce_scatter | solution.py:37
  385.9 30.2 %all-gather.29.cloned.1.call-done = bf16[1,1024,768]{2,1,0:T(8,128)(2,1)} async-done(((bf16[1,256,768]{2,1,0:T(8,128)(2,1)}), bf16[1,1024,768]{2,1,0:T(8,128)(2,1)}) %all-gather.29.cloned.1.call-update) | async-done | bytes 1572880 | tf_op jit(solution)/shard_map/all_gather | solution.py:33
  462.2 51.4 %reduce-scatter.66.cloned.1.call-done = bf16[1,256,768]{2,1,0:T(8,128)(2,1)} async-done(((bf16[1,1024,768]{2,1,0:T(8,128)(2,1)}), bf16[1,256,768]{2,1,0:T(8,128)(2,1)}) %reduce-scatter.66.cloned.1.call-update) | async-done | bytes 393232 | tf_op jit(solution)/shard_map/reduce_scatter | solution.py:37
  517.5 30.4 %all-gather.35.cloned.1.call-done = bf16[1,1024,768]{2,1,0:T(8,128)(2,1)} async-done(((bf16[1,256,768]{2,1,0:T(8,128)(2,1)}), bf16[1,1024,768]{2,1,0:T(8,128)(2,1)}) %all-gather.35.cloned.1.call-update) | async-done | bytes 1572880 | tf_op jit(solution)/shard_map/all_gather | solution.py:33
  594.5 51.4 %reduce-scatter.72.cloned.1.call-done = bf16[1,256,768]{2,1,0:T(8,128)(2,1)} async-done(((bf16[1,1024,768]{2,1,0:T(8,128)(2,1)}), bf16[1,256,768]{2,1,0:T(8,128)(2,1)}) %reduce-scatter.72.cloned.1.call-update) | async-done | bytes 393232 | tf_op jit(solution)/shard_map/reduce_scatter | solution.py:37
  720.6 39.1 %reduce-scatter.76.cloned.1.call-done = bf16[1,256,768]{2,1,0:T(8,128)(2,1)} async-done(((bf16[1,1024,768]{2,1,0:T(8,128)(2,1)}), bf16[1,256,768]{2,1,0:T(8,128)(2,1)}) %reduce-scatter.76.cloned.1.call-update) | async-done | bytes 393232 | tf_op jit(solution)/shard_map/reduce_scatter | solution.py:47
  765.6 30.4 %all-gather.45.cloned.1.call-done = bf16[1,1024,768]{2,1,0:T(8,128)(2,1)} async-done(((bf16[1,256,768]{2,1,0:T(8,128)(2,1)}), bf16[1,1024,768]{2,1,0:T(8,128)(2,1)}) %all-gather.45.cloned.1.call-update) | async-done | bytes 1572880 | tf_op jit(solution)/shard_map/all_gather | solution.py:43
  828.8 40.5 %collective-permute-done.2 = bf16[2,1,1024,192]{2,3,0,1:T(8,128)(2,1)S(1)} collective-permute-done((bf16[2,1,1024,192]{2,3,0,1:T(8,128)(2,1)S(1)}, bf16[2,1,1024,192]{2,3,0,1:T(8,128)(2,1)S(1)}, u32[]{:S(2)}, u32[]{:S(2)}) %collective-permute-start.2) | collective-permute-done | bytes 786464 | tf_op jit(solution)/shard_map/ppermute | solution.py:18
  889.3 38.2 %reduce-scatter.82.cloned.1.call-done = bf16[1,256,768]{2,1,0:T(8,128)(2,1)} async-done(((bf16[1,1024,768]{2,1,0:T(8,128)(2,1)}), bf16[1,256,768]{2,1,0:T(8,128)(2,1)}) %reduce-scatter.82.cloned.1.call-update) | async-done | bytes 393232 | tf_op jit(solution)/shard_map/reduce_scatter | solution.py:47
  933.2 30.3 %all-gather.51.cloned.1.call-done = bf16[1,1024,768]{2,1,0:T(8,128)(2,1)} async-done(((bf16[1,256,768]{2,1,0:T(8,128)(2,1)}), bf16[1,1024,768]{2,1,0:T(8,128)(2,1)}) %all-gather.51.cloned.1.call-update) | async-done | bytes 1572880 | tf_op jit(solution)/shard_map/all_gather | solution.py:43
  996.1 35.9 %collective-permute-done.3 = bf16[2,1,1024,192]{2,3,0,1:T(8,128)(2,1)} collective-permute-done((bf16[2,1,1024,192]{2,3,0,1:T(8,128)(2,1)S(1)}, bf16[2,1,1024,192]{2,3,0,1:T(8,128)(2,1)}, u32[]{:S(2)}, u32[]{:S(2)}) %collective-permute-start.3) | collective-permute-done | bytes 786464 | tf_op jit(solution)/shard_map/ppermute | solution.py:18
  1045.3 34.7 %reduce-scatter.88.cloned.1.call-done = bf16[1,256,768]{2,1,0:T(8,128)(2,1)} async-done(((bf16[1,1024,768]{2,1,0:T(8,128)(2,1)}), bf16[1,256,768]{2,1,0:T(8,128)(2,1)}) %reduce-scatter.88.cloned.1.call-update) | async-done | bytes 393232 | tf_op jit(solution)/shard_map/reduce_scatter | solution.py:47
  1085.9 31.2 %all-gather.57.cloned.1.call-done = bf16[1,1024,768]{2,1,0:T(8,128)(2,1)} async-done(((bf16[1,256,768]{2,1,0:T(8,128)(2,1)}), bf16[1,1024,768]{2,1,0:T(8,128)(2,1)}) %all-gather.57.cloned.1.call-update) | async-done | bytes 1572880 | tf_op jit(solution)/shard_map/all_gather | solution.py:43
  1135.5 54.5 %reduce-scatter.90.cloned.1.call-done = bf16[1,256,768]{2,1,0:T(8,128)(2,1)} async-done(((bf16[1,1024,768]{2,1,0:T(8,128)(2,1)}), bf16[1,256,768]{2,1,0:T(8,128)(2,1)}) %reduce-scatter.90.cloned.1.call-update) | async-done | bytes 393232 | tf_op jit(solution)/shard_map/reduce_scatter | solution.py:47
  1301.0 37.2 %while.193 = (s32[]{:T(128)}, f32[1,1024,3,64]{1,3,2,0:T(8,128)S(1)}, f32[1,1024,3,64]{1,3,2,0:T(8,128)}, bf16[2,512,192]{1,2,0:T(8,128)(2,1)S(1)}, s32[2]{0:T(1...) while((s32[]{:T(128)}, ...), condition=%wide.region_116.117_spmd.clone.clone, body=%wide.region_114.116_spmd.clone.clone.sunk | while | flops 1032585216 | bytes 80986592 | solution.py:196
  1353.4 37.8 %while.192 = (s32[]{:T(128)}, f32[1,1024,3,64]{1,3,2,0:T(8,128)S(1)}, f32[1,1024,3,64]{1,3,2,0:T(8,128)}, bf16[2,512,192]{1,2,0:T(8,128)(2,1)S(1)}, s32[2]{0:T(1...) while((s32[]{:T(128)}, ...), condition=%wide.region_97.98_spmd.clone.clone, body=%wide.region_95.97_spmd.clone.clone.sunk | while | flops 1032585216 | bytes 80986592 | solution.py:196
  1400.6 44.0 %while.191 = (s32[]{:T(128)}, f32[1,1024,3,64]{1,3,2,0:T(8,128)S(1)}, f32[1,1024,3,64]{1,3,2,0:T(8,128)S(1)}, bf16[2,512,192]{1,2,0:T(8,128)(2,1)S(1)}, s32[2]{0...) while((s32[]{:T(128)}, ...), condition=%wide.region_78.79_spmd.clone.clone, body=%wide.region_76.78_spmd.clone.clone.sunk | while | flops 1032585216 | bytes 74695072 | solution.py:196
  1649.7 30.2 %reduce-scatter.98.cloned.1.call-done = bf16[1,768,192]{1,2,0:T(8,128)(2,1)} async-done(((bf16[1,768,768]{1,2,0:T(8,128)(2,1)}), bf16[1,768,192]{1,2,0:T(8,128)(2,1)}) %reduce-scatter.98.cloned.1.call-update) | async-done | bytes 294928 | tf_op jit(solution)/shard_map/reduce_scatter | solution.py:78
  1857.3 33.8 %reduce-scatter.92.cloned.1.call-done = bf16[1,256,768]{2,1,0:T(8,128)(2,1)} async-done(((bf16[1,1024,768]{2,1,0:T(8,128)(2,1)}), bf16[1,256,768]{2,1,0:T(8,128)(2,1)}) %reduce-scatter.92.cloned.1.call-update) | async-done | bytes 393232 | tf_op jit(solution)/shard_map/reduce_scatter | solution.py:47
  1891.1 33.8 %reduce-scatter.86.cloned.1.call-done = bf16[1,256,768]{2,1,0:T(8,128)(2,1)} async-done(((bf16[1,1024,768]{2,1,0:T(8,128)(2,1)}), bf16[1,256,768]{2,1,0:T(8,128)(2,1)}) %reduce-scatter.86.cloned.1.call-update) | async-done | bytes 393232 | tf_op jit(solution)/shard_map/reduce_scatter | solution.py:47
  1928.5 70.5 %psum.25 = f32[1,3,768]{2,1,0:T(4,128)S(1)} all-reduce(f32[1,3,768]{2,1,0:T(4,128)S(1)} %fusion.516), channel_id=1, replica_groups=mesh['section'=2,'dp'=4,'tensor'=4] {'dp','tensor'}, use_global_device_ids=true, to_apply=%region_138.139 | all-reduce | flops 2304 | bytes 18432 | tf_op jit(solution)/shard_map/psum | solution.py:82
  (1024 shorter events, 1354.2 us)
Async XLA Ops:
  765.5 162.0 %reduce-scatter.82.cloned.1.call-start = ((), (), s32[]{:S(2)}) async-start(), calls=%async_computation.60 | async-start | bytes 1966080 | tf_op jit(solution)/shard_map/reduce_scatter | solution.py:47
  933.2 146.8 %reduce-scatter.88.cloned.1.call-start = ((), (), s32[]{:S(2)}) async-start(), calls=%async_computation.66 | async-start | bytes 1966080 | tf_op jit(solution)/shard_map/reduce_scatter | solution.py:47
  1135.4 155.1 %all-gather.59.cloned.1.call-start = ((), (), s32[]{:S(2)}) async-start(), calls=%async_computation.69 | async-start | bytes 1966080 | tf_op jit(solution)/shard_map/all_gather | solution.py:43
  1237.3 225.2 %reduce-scatter.62.cloned.1.call-start = ((), (), s32[]{:S(2)}) async-start(), calls=%async_computation.40 | async-start | bytes 1966080 | tf_op jit(solution)/shard_map/reduce_scatter | solution.py:37
  1240.7 224.2 %reduce-scatter.68.cloned.1.call-start = ((), (), s32[]{:S(2)}) async-start(), calls=%async_computation.46 | async-start | bytes 1966080 | tf_op jit(solution)/shard_map/reduce_scatter | solution.py:37
  1244.0 223.0 %reduce-scatter.74.cloned.1.call-start = ((), (), s32[]{:S(2)}) async-start(), calls=%async_computation.52 | async-start | bytes 1966080 | tf_op jit(solution)/shard_map/reduce_scatter | solution.py:37
  1247.2 221.1 %reduce-scatter.112.cloned.1.call-start = ((), (), s32[]{:S(2)}) async-start(), calls=%async_computation.80 | async-start | bytes 737280
  1251.3 231.5 %reduce-scatter.118.cloned.1.call-start = ((), (), s32[]{:S(2)}) async-start(), calls=%async_computation.83 | async-start | bytes 1474560
  1258.0 248.4 %reduce-scatter.114.cloned.1.call-start = ((), (), s32[]{:S(2)}) async-start(), calls=%async_computation.81 | async-start | bytes 737280
  1262.0 274.2 %reduce-scatter.120.cloned.1.call-start = ((), (), s32[]{:S(2)}) async-start(), calls=%async_computation.84 | async-start | bytes 1474560
  1268.4 291.2 %reduce-scatter.116.cloned.1.call-start = ((), (), s32[]{:S(2)}) async-start(), calls=%async_computation.82 | async-start | bytes 737280
  1272.6 316.9 %reduce-scatter.122.cloned.1.call-start = ((), (), s32[]{:S(2)}) async-start(), calls=%async_computation.85 | async-start | bytes 1474560
  1279.0 340.6 %reduce-scatter.94.cloned.1.call-start = ((), (), s32[]{:S(2)}) async-start(), calls=%async_computation.71 | async-start | bytes 1474560 | tf_op jit(solution)/shard_map/reduce_scatter | solution.py:78
  1282.8 366.9 %reduce-scatter.96.cloned.1.call-start = ((), (), s32[]{:S(2)}) async-start(), calls=%async_computation.72 | async-start | bytes 1474560 | tf_op jit(solution)/shard_map/reduce_scatter | solution.py:78
  1286.6 393.3 %reduce-scatter.98.cloned.1.call-start = ((), (), s32[]{:S(2)}) async-start(), calls=%async_computation.73 | async-start | bytes 1474560 | tf_op jit(solution)/shard_map/reduce_scatter | solution.py:78
  1290.4 411.1 %reduce-scatter.110.cloned.1.call-start = ((), (), s32[]{:S(2)}) async-start(), calls=%async_computation.79 | async-start | bytes 491520
  1293.9 428.8 %reduce-scatter.108.cloned.1.call-start = ((), (), s32[]{:S(2)}) async-start(), calls=%async_computation.78 | async-start | bytes 491520
  1297.4 446.5 %reduce-scatter.106.cloned.1.call-start = ((), (), s32[]{:S(2)}) async-start(), calls=%async_computation.77 | async-start | bytes 491520
  1343.8 427.0 %reduce-scatter.104.cloned.1.call-start = ((), (), s32[]{:S(2)}) async-start(), calls=%async_computation.76 | async-start | bytes 1228800
  1349.8 447.8 %reduce-scatter.102.cloned.1.call-start = ((), (), s32[]{:S(2)}) async-start(), calls=%async_computation.75 | async-start | bytes 1228800
  1399.2 425.6 %reduce-scatter.100.cloned.1.call-start = ((), (), s32[]{:S(2)}) async-start(), calls=%async_computation.74 | async-start | bytes 1228800
  1451.6 405.8 %reduce-scatter.80.cloned.1.call-start = ((), (), s32[]{:S(2)}) async-start(), calls=%async_computation.58 | async-start | bytes 1966080 | tf_op jit(solution)/shard_map/reduce_scatter | solution.py:47
  1455.6 435.6 %reduce-scatter.92.cloned.1.call-start = ((), (), s32[]{:S(2)}) async-start(), calls=%async_computation.70 | async-start | bytes 1966080 | tf_op jit(solution)/shard_map/reduce_scatter | solution.py:47
  1459.7 465.2 %reduce-scatter.86.cloned.1.call-start = ((), (), s32[]{:S(2)}) async-start(), calls=%async_computation.64 | async-start | bytes 1966080 | tf_op jit(solution)/shard_map/reduce_scatter | solution.py:47
  (238 other events, 8530.8 us)
Sparse Core Ops, SparseCore 0:
  14.9 32.1 all-gather.36
  100.6 30.3 reduce-scatter.69
  134.3 30.9 all-gather.30
  167.6 30.9 all-gather.20
  202.0 30.8 reduce-scatter.63
  235.8 30.8 reduce-scatter.57
  516.9 30.9 all-gather.34
  550.3 30.9 all-gather.38
  720.7 38.9 reduce-scatter.75
  764.9 30.9 all-gather.44
  797.8 30.9 all-gather.48
  1045.3 34.5 reduce-scatter.87
  1085.3 31.7 all-gather.56
  1229.6 30.9 all-gather.58
  1262.3 30.9 all-gather.52
  1295.0 30.9 all-gather.46
  1329.5 30.8 reduce-scatter.61
  1363.2 30.9 reduce-scatter.67
  1397.2 30.8 reduce-scatter.73
  1591.7 27.8 reduce-scatter.93
  1652.0 27.8 reduce-scatter.97
  1827.8 29.4 reduce-scatter.79
  1860.2 30.8 reduce-scatter.91
  1894.0 30.8 reduce-scatter.85
  (13 shorter events, 303.9 us)
Sparse Core Ops, SparseCore 1:
  223.6 30.2 all-gather.24
  255.3 37.7 all-gather.26
  295.3 31.5 all-gather.22
  337.3 44.7 reduce-scatter.59
  385.2 30.8 all-gather.28
  418.5 30.8 all-gather.32
  462.3 51.3 reduce-scatter.65
  594.6 51.3 reduce-scatter.71
  648.5 30.8 all-gather.40
  681.2 30.8 all-gather.42
  889.3 38.1 reduce-scatter.81
  932.7 30.8 all-gather.50
  965.2 30.8 all-gather.54
  1088.9 37.3 reduce-scatter.77
  1134.7 55.2 reduce-scatter.89
  1193.0 30.8 reduce-scatter.83
where the time goes:
time: 2030 us; the launch traced here: 2010 us
  waiting for transfers between devices  1270 us (63%)
  matrix products  240 us (12%)
  blocking collectives  147 us (7%)
  local copies, waits for them, and re-layouts  144 us (7%)
  other arithmetic  134 us (7%)
  loops' own time  43.4 us (2%)
  between operations  23.6 us (1%)
    reduce_scatter x9, waiting for transfers between devices, return_rows(): lax.psum_scatter(partial_value.astype(jnp.bfloat16), 'tensor', scatter_di...  294 us
    unnamed x65, waiting for transfers between devices  255 us
    reduce_scatter x9, waiting for transfers between devices, collect_rows(): lax.psum_scatter(partial_value.astype(jnp.bfloat16), 'tensor', scatter_di...  221 us
    all_gather x9, waiting for transfers between devices, spread_rows(): return lax.all_gather(normed, 'tensor', axis=1, tiled=True)  195 us
    all_gather x9, waiting for transfers between devices, spread_grads(): return lax.all_gather(grad_low, 'tensor', axis=1, tiled=True)  142 us
    reduce_scatter x3, waiting for transfers between devices, reduce_grads(): lax.psum_scatter(weight_terms[4].astype(jnp.bfloat16), 'dp', scatter_dime...  87.4 us
    ppermute x4, waiting for transfers between devices, from_behind(): return lax.ppermute(shard, axis, pairs)  76.4 us
    psum x1, blocking collectives, reduce_grads(): gain_total = lax.psum(grad_terms[5][None], ('dp', 'tensor'))  70.5 us
  transfers between devices with their start and end apart: 57, of which 44 were waited for; matrix products, arithmetic and copies ran while one was open for 18% of the time, Pallas kernels for 0%

commit v1 on v0

v1 whole, which is shorter than its diff:
```python
import jax
import jax.numpy as jnp
from jax import lax
from jax.sharding import PartitionSpec as P

HEAD = 64
TILE = 128
EPSILON = 1e-05
SCORE_SCALE = 0.125
NEG_FILL = -1000000000.0
AXES = ("section", "dp", "tensor")
LOW = jnp.bfloat16
WIDE = jnp.float32


class Layout:
    def __init__(self):
        self.cores = lax.axis_size("section")
        self.planes = lax.axis_size("dp")
        self.chips = lax.axis_size("tensor")
        self.core = lax.axis_index("section")
        self.plane = lax.axis_index("dp")
        self.chip = lax.axis_index("tensor")
        self.role = self.chip % 2
        self.item = self.chip // 2
        self.is_decoder = self.role == 1
        self.relays = self.core == self.item

    def route(self, value, target):
        pairs = []
        for core in range(self.cores):
            for plane in range(self.planes):
                for chip in range(self.chips):
                    to = target(core, plane, chip)
                    if to is None:
                        continue
                    source = (core * self.planes + plane) * self.chips + chip
                    goal = (to[0] * self.planes + to[1]) * self.chips + to[2]
                    pairs.append((source, goal))
        return lax.ppermute(value, AXES, pairs)

    def other_core(self, value):
        return self.route(value, lambda c, z, t: (1 - c, z, t))


def normalize(values):
    centred = values - jnp.mean(values, axis=-1, keepdims=True)
    spread = jnp.mean(centred * centred, axis=-1, keepdims=True)
    scale = lax.rsqrt(spread + EPSILON)
    return centred * scale, scale


def layer_norm(values, gain):
    return normalize(values)[0] * gain


def norm_back(values, gain, grad):
    normal, scale = normalize(values)
    scaled = grad * gain
    first = jnp.mean(scaled, axis=-1, keepdims=True)
    second = jnp.mean(scaled * normal, axis=-1, keepdims=True)
    return (scaled - first - normal * second) * scale, jnp.sum(grad * normal, axis=0)


ORDER = (("q", 0), ("q", 1), ("k", 0), ("k", 1), ("v", 0), ("v", 1), ("q", 2), ("v", 2), ("k", 2), ("o", 2), ("o", 0), ("o", 1))


def pack_heads(parts):
    return jnp.concatenate([parts[n][:, HEAD * h : HEAD * (h + 1)] for n, h in ORDER], axis=1)


def unpack_heads(block, name):
    where = {(n, h): i for i, (n, h) in enumerate(ORDER)}
    return jnp.concatenate(
        [block[:, HEAD * where[(name, h)] : HEAD * (where[(name, h)] + 1)] for h in range(3)], axis=1
    )


def mm(left, right):
    return jnp.dot(left, right, preferred_element_type=WIDE)


def mm_nt(left, right):
    return lax.dot_general(left, right, (((1,), (1,)), ((), ())), preferred_element_type=WIDE)


def mm_tn(left, right):
    return lax.dot_general(left, right, (((0,), (0,)), ((), ())), preferred_element_type=WIDE)


def split_heads(value):
    return value.reshape(value.shape[0], -1, HEAD)


def attend(q, k, v, allowed):
    scores = jnp.einsum("qhd,khd->hqk", split_heads(q), split_heads(k), preferred_element_type=WIDE) * SCORE_SCALE
    scores = jnp.where(allowed[None], scores, NEG_FILL)
    top = jnp.max(scores, axis=-1, keepdims=True)
    power = jnp.exp(scores - top)
    total = jnp.sum(power, axis=-1, keepdims=True)
    probs = (power / total).astype(LOW)
    out = jnp.einsum("hqk,khd->qhd", probs, split_heads(v), preferred_element_type=WIDE)
    return out.astype(LOW).reshape(q.shape), top + jnp.log(total)


def attend_back(q, k, v, log_sum, d_out, allowed):
    scores = jnp.einsum("qhd,khd->hqk", split_heads(q), split_heads(k), preferred_element_type=WIDE) * SCORE_SCALE
    scores = jnp.where(allowed[None], scores, NEG_FILL)
    probs = jnp.exp(scores - log_sum)
    d_probs = jnp.einsum("qhd,khd->hqk", split_heads(d_out), split_heads(v), preferred_element_type=WIDE)
    inner = jnp.sum(probs * d_probs, axis=-1, keepdims=True)
    d_scores = (probs * (d_probs - inner)).astype(LOW)
    d_v = jnp.einsum("hqk,qhd->khd", probs.astype(LOW), split_heads(d_out), preferred_element_type=WIDE)
    d_q = jnp.einsum("hqk,khd->qhd", d_scores, split_heads(k), preferred_element_type=WIDE) * SCORE_SCALE
    d_k = jnp.einsum("hqk,qhd->khd", d_scores, split_heads(q), preferred_element_type=WIDE) * SCORE_SCALE
    return tuple(g.astype(LOW).reshape(q.shape) for g in (d_q, d_k, d_v))


def gelu_parts(value):
    coef = 0.7978845608028654
    cube = 0.044715
    inner = coef * (value + cube * value * value * value)
    soft = jnp.tanh(inner)
    slope = 0.5 * (1.0 + soft) + 0.5 * value * (1.0 - soft * soft) * coef * (1.0 + 3.0 * cube * value * value)
    return 0.5 * value * (1.0 + soft), slope


def ring_gather(lay, shard):
    planes = lay.planes
    rows = shard.shape[1]
    relay = lambda c, z, t: (c, (z + 1) % planes, t) if c == t // 2 else None
    whole = jnp.zeros((shard.shape[0], planes * rows, shard.shape[2]), shard.dtype)
    piece = shard
    for step in range(planes):
        across = lay.route(piece, lambda c, z, t: (c, z, (t + 2) % 4) if c == t // 2 else None)
        chosen = jnp.where(lay.relays, piece, across)
        whole = lax.dynamic_update_slice(whole, chosen, (0, ((lay.plane - step) % planes) * rows, 0))
        if step + 1 < planes:
            piece = lay.route(piece, relay)
    return whole


def ring_scatter(lay, total, holder):
    planes = lay.planes
    rows = total.shape[1] // planes
    low = total.astype(LOW)
    across = lay.route(
        low, lambda c, z, t: (c, z, (t + 2) % 4) if (c != t // 2 and t % 2 == holder) else None
    )
    summed = low.astype(WIDE) + across.astype(WIDE)
    relay = lambda c, z, t: (c, (z + 1) % planes, t) if (c == t // 2 and t % 2 == holder) else None
    take = lambda j: lax.dynamic_slice_in_dim(summed, (j % planes) * rows, rows, 1)
    running = take(lay.plane - 1)
    for step in range(1, planes):
        running = lay.route(running.astype(LOW), relay).astype(WIDE) + take(lay.plane - 1 - step)
    return running.astype(LOW)


def hand_back(lay, value, holder, section):
    same = lay.route(
        value[0], lambda c, z, t: (section, z, t) if (c == t // 2 and t % 2 == holder) else None
    )
    beside = lay.route(
        value[1], lambda c, z, t: (section, z, t ^ 1) if (c == t // 2 and t % 2 == holder) else None
    )
    return same.astype(WIDE) + beside.astype(WIDE)


def body(block_input, w_self, w_self_out, w_cross, w_up, w_down, norm_gains, lengths, task_mask, out_grad):
    lay = Layout()
    seqs, rows, width = block_input.shape[1:]
    slot = rows * lay.chips
    sec = lay.core
    item = lay.item

    def spread(value, first):
        pick = value[jnp.where(first, lay.chip % 2, 1 - lay.chip % 2)]
        flip = 0 if first else 1
        return lay.route(pick, lambda c, z, t: (t // 2, z, 2 * ((t % 2) ^ flip) + c))

    def merge_rows(mine, theirs):
        low_half = jnp.where(lay.core == 0, mine, theirs)
        high_half = jnp.where(lay.core == 0, theirs, mine)
        return jnp.concatenate([low_half[0], low_half[1], high_half[0], high_half[1]], axis=0)

    first = spread(block_input[0], True)
    second = spread(block_input[0], False)
    mine = jnp.where(item == 0, jnp.stack([first, second]), jnp.stack([second, first]))
    x_rows = merge_rows(mine, lay.other_core(mine)).astype(WIDE)

    picked = out_grad[lay.core]
    even = lay.route(picked, lambda c, z, t: (t // 2, z, 2 * c + 1) if t % 2 == 0 else None)
    odd = lay.route(picked, lambda c, z, t: (t // 2, z, 2 * c + 1) if t % 2 == 1 else None)
    mine = jnp.stack([even, odd])
    cotangent = merge_rows(mine, lay.other_core(mine))

    gains_here = norm_gains[0].astype(WIDE)
    gains = jnp.where(sec == lay.role, gains_here, lay.other_core(norm_gains[0]).astype(WIDE))

    depth = w_self.shape[1]
    wide = w_self.shape[3]
    self_block = pack_heads(
        {"q": w_self[0, :, 0], "k": w_self[0, :, 1], "v": w_self[0, :, 2], "o": w_self_out[0].T}
    )
    feed_block = jnp.concatenate([w_up[0], w_down[0].T], axis=1)
    cross_block = w_cross[0].reshape(depth, 2 * wide)

    def collect(block):
        same = lay.route(block, lambda c, z, t: (t // 2, z, t) if c == t % 2 else None)
        beside = lay.route(block, lambda c, z, t: (t // 2, z, t ^ 1) if c != t % 2 else None)
        return jnp.stack([same, beside])

    def collect_cross(block, section):
        same = lay.route(block, lambda c, z, t: (t // 2, z, t) if (c == section and t % 2 == 1) else None)
        beside = lay.route(block, lambda c, z, t: (t // 2, z, t ^ 1) if (c == section and t % 2 == 0) else None)
        return same, beside

    w_att = ring_gather(lay, collect(self_block))
    w_ffn = ring_gather(lay, collect(feed_block))
    memory_side = collect_cross(cross_block, 0)
    query_side = collect_cross(cross_block, 1)
    w_crs = ring_gather(
        lay,
        jnp.stack(
            [
                pack_heads({"q": q[:, :wide], "k": m[:, :wide], "v": m[:, wide:], "o": q[:, wide:]})
                for m, q in zip(memory_side, query_side)
            ]
        ),
    )
    hidden = w_up.shape[2]
    part = lambda w, name: jnp.concatenate([unpack_heads(w[0], name), unpack_heads(w[1], name)], axis=1)
    att = {n: part(w_att, n) for n in "qkvo"}
    crs = {n: part(w_crs, n) for n in "qkvo"}
    up = jnp.concatenate([w_ffn[0, :, :hidden], w_ffn[1, :, :hidden]], axis=1)
    down_t = jnp.concatenate([w_ffn[0, :, hidden:], w_ffn[1, :, hidden:]], axis=1)

    positions = jnp.arange(slot)
    own_length = jnp.where(lay.is_decoder, lengths[1, item], lengths[0, item])
    self_allowed = (positions[None, :] < own_length) & (
        (positions[None, :] <= positions[:, None]) | jnp.logical_not(lay.is_decoder)
    )
    cross_allowed = jnp.broadcast_to(
        ((positions < lengths[0, item]) & (task_mask[item] == 1))[None], (slot, slot)
    )

    def joined(partial):
        low = partial.astype(LOW)
        return low.astype(WIDE) + lay.other_core(low).astype(WIDE)

    normed0 = layer_norm(x_rows, gains[0]).astype(LOW)
    q, k, v = (mm(normed0, att[n]).astype(LOW) for n in "qkv")
    out_self, lse_self = attend(q, k, v, self_allowed)
    x_mid = x_rows + joined(mm_nt(out_self, att["o"]))
    normed1 = layer_norm(x_mid, gains[1]).astype(LOW)

    pre_enc = mm(normed1, up)
    act_enc, slope_enc = gelu_parts(pre_enc)
    act_enc = act_enc.astype(LOW)
    x_late_enc = x_mid + joined(mm_nt(act_enc, down_t))
    memory_enc = layer_norm(x_late_enc, gains[2]).astype(LOW)
    memory = lay.route(memory_enc, lambda c, z, t: (c, z, t ^ 1) if t % 2 == 0 else None)

    cq = mm(normed1, crs["q"]).astype(LOW)
    ck, cv = (mm(memory, crs[n]).astype(LOW) for n in "kv")
    out_cross, lse_cross = attend(cq, ck, cv, cross_allowed)
    x_late = x_mid + joined(mm_nt(out_cross, crs["o"]))
    normed2 = layer_norm(x_late, gains[2]).astype(LOW)
    pre_dec = mm(normed2, up)
    act_dec, slope_dec = gelu_parts(pre_dec)
    act_dec = act_dec.astype(LOW)
    result_dec = (x_late + joined(mm_nt(act_dec, down_t))).astype(LOW)

    d_out = cotangent.astype(WIDE)
    d_pre = (slope_dec * mm(cotangent, down_t)).astype(LOW)
    d_ffn_dec = jnp.concatenate([mm_tn(normed2, d_pre), mm_tn(cotangent, act_dec)], axis=1)
    d_late_norm, d_gain2_dec = norm_back(x_late, gains[2], joined(mm_nt(d_pre, up)))
    d_late = d_out + d_late_norm
    grad_late = d_late.astype(LOW)
    d_att = mm(grad_late, crs["o"]).astype(LOW)
    d_cq, d_ck, d_cv = attend_back(cq, ck, cv, lse_cross, d_att, cross_allowed)
    d_memory = joined(mm_nt(d_ck, crs["k"]) + mm_nt(d_cv, crs["v"]))
    d_crs = {
        "q": mm_tn(normed1, d_cq),
        "k": mm_tn(memory, d_ck),
        "v": mm_tn(memory, d_cv),
        "o": mm_tn(grad_late, out_cross),
    }
    d_mid_norm, d_gain1_dec = norm_back(x_mid, gains[1], joined(mm_nt(d_cq, crs["q"])))
    d_mid_dec = d_late + d_mid_norm

    d_memory = lay.route(d_memory.astype(LOW), lambda c, z, t: (c, z, t ^ 1) if t % 2 == 1 else None).astype(WIDE)
    d_late_enc, d_gain2_enc = norm_back(x_late_enc, gains[2], d_memory)
    grad_late_enc = d_late_enc.astype(LOW)
    d_pre = (slope_enc * mm(grad_late_enc, down_t)).astype(LOW)
    d_ffn_enc = jnp.concatenate([mm_tn(normed1, d_pre), mm_tn(grad_late_enc, act_enc)], axis=1)
    d_mid_norm, d_gain1_enc = norm_back(x_mid, gains[1], joined(mm_nt(d_pre, up)))
    d_mid_enc = d_late_enc + d_mid_norm

    d_mid = jnp.where(lay.is_decoder, d_mid_dec, d_mid_enc)
    grad_mid = d_mid.astype(LOW)
    d_att = mm(grad_mid, att["o"]).astype(LOW)
    d_q, d_k, d_v = attend_back(q, k, v, lse_self, d_att, self_allowed)
    d_norm = joined(mm_nt(d_q, att["q"]) + mm_nt(d_k, att["k"]) + mm_nt(d_v, att["v"]))
    d_att_w = {
        "q": mm_tn(normed0, d_q),
        "k": mm_tn(normed0, d_k),
        "v": mm_tn(normed0, d_v),
        "o": mm_tn(grad_mid, out_self),
    }
    d_first, d_gain0 = norm_back(x_rows, gains[0], d_norm)
    d_rows = d_mid + d_first

    half = 3 * HEAD

    def blocks(parts):
        return jnp.stack(
            [pack_heads({n: parts[n][:, half * b : half * (b + 1)] for n in parts}) for b in range(2)]
        )

    def feed_blocks(both):
        total = both.shape[1] // 2
        return jnp.stack(
            [
                jnp.concatenate(
                    [both[:, hidden * b : hidden * (b + 1)], both[:, total + hidden * b : total + hidden * (b + 1)]],
                    axis=1,
                )
                for b in range(2)
            ]
        )

    self_total = blocks(d_att_w)
    home_self = hand_back(lay, ring_scatter(lay, self_total, 0), 0, 0) + hand_back(
        lay, ring_scatter(lay, self_total, 1), 1, 1
    )
    home_feed = hand_back(lay, ring_scatter(lay, feed_blocks(d_ffn_enc), 0), 0, 0) + hand_back(
        lay, ring_scatter(lay, feed_blocks(d_ffn_dec), 1), 1, 1
    )
    cross_total = ring_scatter(lay, blocks(d_crs), 1)
    side = lambda names: jnp.stack(
        [jnp.concatenate([unpack_heads(cross_total[b], n) for n in names], axis=1) for b in range(2)]
    )
    home_cross = hand_back(lay, side("kv"), 1, 0) + hand_back(lay, side("qo"), 1, 1)

    g_self = jnp.stack([unpack_heads(home_self, n) for n in "qkv"], axis=1)[None]
    g_self_out = unpack_heads(home_self, "o").T[None]
    g_cross = home_cross.reshape(1, depth, 2, wide)
    g_up = home_feed[:, :hidden][None]
    g_down = home_feed[:, hidden:].T[None]

    gain2 = jnp.where(lay.is_decoder, d_gain2_dec, d_gain2_enc)
    gain1 = jnp.where(lay.is_decoder, d_gain1_dec, d_gain1_enc)
    gain_rows = jnp.stack([d_gain0, gain1, gain2])
    slots = jnp.stack(
        [
            jnp.where((lay.role == r) & (lay.core == 0), gain_rows, 0.0)
            for r in range(2)
        ]
    )
    gain_total = lax.psum(slots, AXES)[sec][None]

    def rows_home(value):
        mine = lax.dynamic_slice_in_dim(value, lay.core * 2 * rows, 2 * rows, 0).reshape(2, rows, width)
        a = lay.route(mine[item], lambda c, z, t: (t % 2, z, 2 * c + t // 2))
        b = lay.route(mine[1 - item], lambda c, z, t: (t % 2, z, 2 * c + 1 - t // 2))
        even = lay.chip % 2 == 0
        return jnp.where(even, jnp.stack([a, b]), jnp.stack([b, a]))[None]

    block_output = rows_home(jnp.where(lay.is_decoder, result_dec, memory_enc))
    input_grad = rows_home(d_rows.astype(LOW)).astype(WIDE)
    return (
        block_output,
        input_grad,
        g_self,
        g_self_out,
        g_cross,
        g_up,
        g_down,
        gain_total[:, :2],
        gain_total[:, 2],
    )


def solution(mesh):
    placed = (
        P("section", "dp", "tensor", None),
        P("section", "dp", None, "tensor"),
        P("section", "tensor", "dp"),
        P("section", "dp", None, "tensor"),
        P("section", "dp", "tensor"),
        P("section", "tensor", "dp"),
        P("section", None, None),
        P(None, "dp"),
        P("dp", None),
        P("dp", "tensor", None),
    )
    return jax.shard_map(
        body,
        mesh=mesh,
        in_specs=placed,
        out_specs=(
            P("section", "dp", "tensor", None),
            P("section", "dp", "tensor", None),
            P("section", "dp", None, "tensor"),
            P("section", "tensor", "dp"),
            P("section", "dp", None, "tensor"),
            P("section", "dp", "tensor"),
            P("section", "tensor", "dp"),
            P("section", None, None),
            P("section", None),
        ),
        check_vma=False,
    )
```

time: 2030 us -> 866 us (0.43)
  waiting for transfers between devices: 1270 us -> 175 us
  starting transfers between devices: 11.1 us -> 203 us
  blocking collectives: 147 us -> 41.3 us
  local copies, waits for them, and re-layouts: 144 us -> 67.4 us
  loops' own time: 43.4 us -> 0 us
  matrix products: 240 us -> 199 us
  other arithmetic: 134 us -> 163 us
    reduce_scatter x21 -> x0, waiting for transfers between devices: 602 us -> none  [the longest x9 294 us: return_rows(): lax.psum_scatter(partial_value.astype(jnp.bfloat16), 'tensor', scatter_di...]
    all_gather x20 -> x0, waiting for transfers between devices: 337 us -> none  [the longest x9 195 us: spread_rows(): return lax.all_gather(normed, 'tensor', axis=1, tiled=True)]
    unnamed x65 -> x0, waiting for transfers between devices: 255 us -> none
    ppermute x4 -> x83, starting transfers between devices: 6.9 us -> 203 us  [route(): return lax.ppermute(value, AXES, pairs)]
    ppermute x4 -> x83, waiting for transfers between devices: 76.4 us -> 175 us  [route(): return lax.ppermute(value, AXES, pairs)]
    all_gather x3 -> x0, blocking collectives: 76.4 us -> none  [the longest x1 30.1 us: fetch_weights(): lax.all_gather(w_self, 'dp', axis=1, tiled=True)]
    another operation x64 -> x6, local copies, waits for them, and re-layouts: 51.7 us -> 2.19 us  [the longest x1 1.87 us: body(): cross_block = w_cross[0].reshape(depth, 2 * wide)]
    unnamed x389 -> x402, local copies, waits for them, and re-layouts: 62.4 us -> 14.4 us
  transfers between devices with their start and end apart: 57 -> 83, of which waited for: 44 -> 21; matrix products, arithmetic and copies ran while one was open for 18% -> 46% of each run, Pallas kernels for 0% -> 0%
where the time goes in v1:
time: 866 us; the launch traced here: 855 us
  starting transfers between devices  203 us (23%)
  matrix products  199 us (23%)
  waiting for transfers between devices  175 us (20%)
  other arithmetic  163 us (19%)
  local copies, waits for them, and re-layouts  67.4 us (8%)
  blocking collectives  41.3 us (5%)
    ppermute x83, starting transfers between devices, route(): return lax.ppermute(value, AXES, pairs)  203 us
    ppermute x83, waiting for transfers between devices, route(): return lax.ppermute(value, AXES, pairs)  175 us
    psum x1, blocking collectives, body(): gain_total = lax.psum(slots, AXES)[sec][None]  41.3 us
    dot_general x2, matrix products, attend_back(): jnp.einsum('qhd,khd->hqk', split_heads(d_out), split_heads(v), preferred_...  34.4 us
    convert_element_type x2, other arithmetic, attend_back(): d_scores = (probs * (d_probs - inner)).astype(LOW)  34.2 us
    dot_general x12, matrix products, mm_nt(): lax.dot_general(left, right, (((1,), (1,)), ((), ())), preferred_element_...  30.8 us
    dot_general x12, matrix products, mm_tn(): lax.dot_general(left, right, (((0,), (0,)), ((), ())), preferred_element_...  29.4 us
    dot_general x12, matrix products, mm(): return jnp.dot(left, right, preferred_element_type=WIDE)  26.8 us
  transfers between devices with their start and end apart: 83, of which 21 were waited for; matrix products, arithmetic and copies ran while one was open for 46% of the time, Pallas kernels for 0%

profile of v1, /device:TPU:2, one launch (start us, length us, event | category | flops | bytes accessed | tf_op | source)
XLA Modules:
  0.0 855.2 jit_solution(5905409913780738239)
XLA Ops:
  41.9 10.8 %collective-permute-start = (bf16[256,768]{1,0:T(8,128)(2,1)}, bf16[256,768]{1,0:T(8,128)(2,1)S(1)}, u32[]{:S(2)}, u32[]{:S(2)}) collective-permute-start(bf16[256,768]{1,0:T(8,128)(2,1)} %get-tuple-element.136), channel_id=1, source_target_pairs={{0,0},{1,2},{2,16},{3,18},{4,4},{5,6},{6,20},{7,22},{8,8},{9,10},{... | collective-permute-start | bytes 1179656 | tf_op jit(solution)/shard_map/ppermute | solution.py:40
  91.5 10.5 %collective-permute-done.32 = bf16[2,192,768]{2,1,0:T(8,128)(2,1)S(1)} collective-permute-done((bf16[2,192,768]{2,1,0:T(8,128)(2,1)S(1)}, bf16[2,192,768]{2,1,0:T(8,128)(2,1)S(1)}, u32[]{:S(2)}, u32[]{:S(2)}) %collective-permute-start.32) | collective-permute-done | bytes 589856 | tf_op jit(solution)/shard_map/ppermute | solution.py:40
  142.4 10.6 %fusion.139 = (f32[6,1024]{1,0:T(8,128)S(1)}, f32[6,1024,1024]{1,2,0:T(8,128)}) fusion(bf16[1024,6,64]{0,2,1:T(8,128)(2,1)S(1)} %bitcast.235, bf16[1024,6,64]{0,2,1:T(8,128)(2,1)S(1)} %bitcast.233, pred[1024,1024]{0,1:T(8,128)(4,1)S(1)} %fusion.27), kind=kOutput, calls=%fused_computation.373 | convolution fusion | flops 824174592 | bytes 27811840 | tf_op jit(solution)/shard_map/qhd,khd->hqk/dot_general | solution.py:96
  153.0 10.2 %fusion = f32[6,1024]{1,0:T(8,128)S(1)} fusion(f32[6,1024,1024]{1,2,0:T(8,128)} %get-tuple-element.224, f32[6,1024]{1,0:T(8,128)S(1)} %get-tuple-element.223), kind=kLoop, calls=%fused_computation.12 | loop fusion | flops 12576768 | bytes 25214976 | tf_op jit(solution)/shard_map/reduce_sum | solution.py:100
  164.3 10.8 %fusion.56 = bf16[6,64,1024]{2,1,0:T(8,128)(2,1)S(1)} fusion(bf16[1024,6,64]{0,2,1:T(8,128)(2,1)S(1)} %bitcast.273, f32[6,1024,1024]{1,2,0:T(8,128)} %get-tuple-element.224, f32[6,1024]{1,0:T(8,128)S(1)} %fusion, f32[6,1024]{1,0:T(8,128)S(1)} %get-tuple-element.223), kind=kOutput, calls=%fused_computation.155 | convolution fusion | flops 824573952 | bytes 26787840 | tf_op jit(solution)/shard_map/hqk,khd->qhd/dot_general | solution.py:102
  184.8 10.2 %collective-permute-done.21 = bf16[2,192,1536]{2,1,0:T(8,128)(2,1)S(1)} collective-permute-done((bf16[2,192,1536]{2,1,0:T(8,128)(2,1)S(1)}, bf16[2,192,1536]{2,1,0:T(8,128)(2,1)S(1)}, u32[]{:S(2)}, u32[]{:S(2)}) %collective-permute-start.21) | collective-permute-done | bytes 1179680 | tf_op jit(solution)/shard_map/ppermute | solution.py:40
  226.6 10.9 %collective-permute-done.40 = bf16[256,768]{1,0:T(8,128)(2,1)S(1)} collective-permute-done((bf16[256,768]{1,0:T(8,128)(2,1)S(1)}, bf16[256,768]{1,0:T(8,128)(2,1)S(1)}, u32[]{:S(2)}, u32[]{:S(2)}) %collective-permute-start.40) | collective-permute-done | bytes 393248 | tf_op jit(solution)/shard_map/ppermute | solution.py:40
  248.8 33.5 %collective-permute-done.24 = bf16[1024,768]{1,0:T(8,128)(2,1)S(1)} collective-permute-done((bf16[1024,768]{1,0:T(8,128)(2,1)S(1)}, bf16[1024,768]{1,0:T(8,128)(2,1)S(1)}, u32[]{:S(2)}, u32[]{:S(2)}) %collective-permute-start.24) | collective-permute-done | bytes 1572896 | tf_op jit(solution)/shard_map/ppermute | solution.py:40
  283.3 10.7 %fusion.140 = (f32[6,1024]{1,0:T(8,128)S(1)}, f32[6,1024,1024]{1,2,0:T(8,128)}) fusion(bf16[1024,6,64]{0,2,1:T(8,128)(2,1)S(1)} %bitcast.237, bf16[1024,6,64]{0,2,1:T(8,128)(2,1)S(1)} %bitcast.239, pred[1024]{0:T(1024)(128)(4,1)S(1)} %fusion.67), kind=kOutput, calls=%fused_computation.374 | convolution fusion | flops 824174592 | bytes 26764288 | tf_op jit(solution)/shard_map/qhd,khd->hqk/dot_general | solution.py:96
  294.0 10.2 %fusion.1 = f32[6,1024]{1,0:T(8,128)S(1)} fusion(f32[6,1024,1024]{1,2,0:T(8,128)} %get-tuple-element.226, f32[6,1024]{1,0:T(8,128)S(1)} %get-tuple-element.225), kind=kLoop, calls=%fused_computation.13 | loop fusion | flops 12576768 | bytes 25214976 | tf_op jit(solution)/shard_map/reduce_sum | solution.py:100
  305.2 10.8 %fusion.55 = bf16[6,64,1024]{2,1,0:T(8,128)(2,1)S(1)} fusion(bf16[1024,6,64]{0,2,1:T(8,128)(2,1)S(1)} %bitcast.275, f32[6,1024,1024]{1,2,0:T(8,128)} %get-tuple-element.226, f32[6,1024]{1,0:T(8,128)S(1)} %fusion.1, f32[6,1024]{1,0:T(8,128)S(1)} %get-tuple-element.225), kind=kOutput, calls=%fused_computation.154 | convolution fusion | flops 824573952 | bytes 26787840 | tf_op jit(solution)/shard_map/hqk,khd->qhd/dot_general | solution.py:102
  361.7 10.3 %fusion.49 = bf16[6,64,1024]{2,1,0:T(8,128)(2,1)S(1)} fusion(bf16[1024,6,64]{0,2,1:T(8,128)(2,1)S(1)} %bitcast.229, f32[6,1024,1024]{1,2,0:T(8,128)} %get-tuple-element.226, f32[6,1024]{1,0:T(8,128)S(1)} %log_add_fusion.1), kind=kOutput, calls=%fused_computation.152 | convolution fusion | flops 818282496 | bytes 26763264 | tf_op jit(solution)/shard_map/hqk,qhd->khd/dot_general | solution.py:113
  376.5 15.8 %multiply_reduce_fusion.1 = (f32[6,1024]{1,0:T(8,128)S(1)}, f32[6,1024,1024]{1,2,0:T(8,128)}) fusion(f32[6,1024,1024]{1,2,0:T(8,128)} %get-tuple-element.226, f32[6,1024]{1,0:T(8,128)S(1)} %log_add_fusion.1, bf16[1024,6,64]{0,2,1:T(8,128)(2,1)S(1)} %bitcast.230, bf16[1024,6,64]{0,2,1:T(8,128)(2,1)S(1)} %bitcast.276), kind=kOutput, calls=%fused_computation.4 | convolution fusion | flops 824174592 | bytes 51953664 | tf_op jit(solution)/shard_map/qhd,khd->hqk/dot_general | solution.py:110
  392.2 16.9 %multiply_convert_fusion.1 = bf16[6,1024,1024]{1,2,0:T(8,128)(2,1)S(1)} fusion(f32[6,1024,1024]{1,2,0:T(8,128)} %get-tuple-element.228, f32[6,1024,1024]{1,2,0:T(8,128)} %get-tuple-element.226, f32[6,1024]{1,0:T(8,128)S(1)} %get-tuple-element.227, f32[6,1024]{1,0:T(8,128)S(1)} %log_add_fusion.1), kind=kLoop, calls=%fused_computation.3 | loop fusion | flops 25165824 | bytes 62963712 | tf_op jit(solution)/shard_map/convert_element_type | solution.py:112
  447.8 17.0 %collective-permute-done.63 = bf16[2,768,768]{2,1,0:T(8,128)(2,1)S(1)} collective-permute-done((bf16[2,768,768]{2,1,0:T(8,128)(2,1)S(1)}, bf16[2,768,768]{2,1,0:T(8,128)(2,1)S(1)}, u32[]{:S(2)}, u32[]{:S(2)}) %collective-permute-start.63) | collective-permute-done | bytes 2359328 | tf_op jit(solution)/shard_map/ppermute | solution.py:40
  471.9 9.2 %collective-permute-done.38 = bf16[256,768]{1,0:T(8,128)(2,1)S(1)} collective-permute-done((bf16[256,768]{1,0:T(8,128)(2,1)S(1)}, bf16[256,768]{1,0:T(8,128)(2,1)S(1)}, u32[]{:S(2)}, u32[]{:S(2)}) %collective-permute-start.38) | collective-permute-done | bytes 393248 | tf_op jit(solution)/shard_map/ppermute | solution.py:40
  481.1 38.3 %collective-permute-start.44 = (bf16[1024,768]{1,0:T(8,128)(2,1)}, bf16[1024,768]{1,0:T(8,128)(2,1)}, u32[]{:S(2)}, u32[]{:S(2)}) collective-permute-start(bf16[1024,768]{1,0:T(8,128)(2,1)} %convolution_convert_fusion.4), channel_id=1, source_target_pairs={{0,16},{1,17},{2,18},{3,19},{4,20},{5,21},{6,22},{7,23},{8,24},{9,... | collective-permute-start | bytes 4718600 | tf_op jit(solution)/shard_map/ppermute | solution.py:40
  602.1 10.4 %fusion.52 = bf16[6,64,1024]{2,1,0:T(8,128)(2,1)S(1)} fusion(bf16[1024,6,64]{0,2,1:T(8,128)(2,1)S(1)} %bitcast.231, f32[6,1024,1024]{1,2,0:T(8,128)} %get-tuple-element.224, f32[6,1024]{1,0:T(8,128)} %log_add_fusion), kind=kOutput, calls=%fused_computation.153 | convolution fusion | flops 818282496 | bytes 26763264 | tf_op jit(solution)/shard_map/hqk,qhd->khd/dot_general | solution.py:113
  615.2 18.6 %multiply_reduce_fusion = (f32[6,1024]{1,0:T(8,128)S(1)}, f32[6,1024,1024]{1,2,0:T(8,128)}) fusion(f32[6,1024,1024]{1,2,0:T(8,128)} %get-tuple-element.224, f32[6,1024]{1,0:T(8,128)} %log_add_fusion, bf16[1024,6,64]{0,2,1:T(8,128)(2,1)S(1)} %bitcast.232, bf16[1024,6,64]{0,2,1:T(8,128)(2,1)} %bitcast.274), kind=kOutput, calls=%fused_computation.1 | convolution fusion | flops 824174592 | bytes 51953664 | tf_op jit(solution)/shard_map/qhd,khd->hqk/dot_general | solution.py:110
  633.9 17.4 %multiply_convert_fusion = bf16[6,1024,1024]{1,2,0:T(8,128)(2,1)S(1)} fusion(f32[6,1024,1024]{1,2,0:T(8,128)} %get-tuple-element.230, f32[6,1024,1024]{1,2,0:T(8,128)} %get-tuple-element.224, f32[6,1024]{1,0:T(8,128)S(1)} %get-tuple-element.229, f32[6,1024]{1,0:T(8,128)S(1)} %copy-done.156), kind=kLoop, calls=%fused_computation | loop fusion | flops 25165824 | bytes 62963712 | tf_op jit(solution)/shard_map/convert_element_type | solution.py:112
  699.3 16.9 %collective-permute-done.57 = bf16[2,768,768]{2,1,0:T(8,128)(2,1)} collective-permute-done((bf16[2,768,768]{2,1,0:T(8,128)(2,1)}, bf16[2,768,768]{2,1,0:T(8,128)(2,1)}, u32[]{:S(2)}, u32[]{:S(2)}) %collective-permute-start.57) | collective-permute-done | bytes 2359328 | tf_op jit(solution)/shard_map/ppermute | solution.py:40
  741.9 41.3 %psum.7 = f32[2,3,768]{2,1,0:T(4,128)S(1)} all-reduce(f32[2,3,768]{2,1,0:T(4,128)S(1)} %pad_maximum_fusion.25), channel_id=1, replica_groups=mesh['section'=2,'dp'=4,'tensor'=4] {'section','dp','tensor'}, use_global_device_ids=true, to_apply=%region_29.30 | all-reduce | flops 4608 | bytes 36864 | tf_op jit(solution)/shard_map/psum | solution.py:361
  814.2 10.4 %collective-permute-done.56 = bf16[192,768]{1,0:T(8,128)(2,1)S(1)} collective-permute-done((bf16[192,768]{1,0:T(8,128)(2,1)S(1)}, bf16[192,768]{1,0:T(8,128)(2,1)S(1)}, u32[]{:S(2)}, u32[]{:S(2)}) %collective-permute-start.56) | collective-permute-done | bytes 294944 | tf_op jit(solution)/shard_map/ppermute | solution.py:40
  830.2 22.3 %collective-permute-done.76 = bf16[192,1536]{1,0:T(8,128)(2,1)} collective-permute-done((bf16[192,1536]{1,0:T(8,128)(2,1)}, bf16[192,1536]{1,0:T(8,128)(2,1)}, u32[]{:S(2)}, u32[]{:S(2)}) %collective-permute-start.76) | collective-permute-done | bytes 589856 | tf_op jit(solution)/shard_map/ppermute | solution.py:40
  (801 shorter events, 464.7 us)
Async XLA Ops:
  29.2 43.5 %collective-permute-start.15 = (bf16[192,1536]{1,0:T(8,128)(2,1)}, bf16[192,1536]{1,0:T(8,128)(2,1)S(1)}, u32[]{:S(2)}, u32[]{:S(2)}) collective-permute-start(bf16[192,1536]{1,0:T(8,128)(2,1)} %pad_maximum_fusion.15), channel_id=1, source_target_pairs={{1,0},{3,18},{5,4},{7,22},{9,8},{11,26},{13,12},{15,30},{16,1},{18... | collective-permute-start | bytes 1769480 | tf_op jit(solution)/shard_map/ppermute | solution.py:40
  75.8 47.6 %collective-permute-start.17 = (bf16[2,192,1536]{2,1,0:T(8,128)(2,1)S(1)}, bf16[2,192,1536]{2,1,0:T(8,128)(2,1)S(1)}, u32[]{:S(2)}, u32[]{:S(2)}) collective-permute-start(bf16[2,192,1536]{2,1,0:T(8,128)(2,1)S(1)} %pad_maximum_fusion.8), channel_id=1, source_target_pairs={{0,4},{1,5},{4,8},{5,9},{8,12},{9,13},{12,0},{13,1},{18,22},{19,23... | collective-permute-start | bytes 3538952 | tf_op jit(solution)/shard_map/ppermute | solution.py:40
  123.4 58.2 %collective-permute-start.16 = (bf16[2,192,1536]{2,1,0:T(8,128)(2,1)S(1)}, bf16[2,192,1536]{2,1,0:T(8,128)(2,1)S(1)}, u32[]{:S(2)}, u32[]{:S(2)}) collective-permute-start(bf16[2,192,1536]{2,1,0:T(8,128)(2,1)S(1)} %pad_maximum_fusion.8), channel_id=1, source_target_pairs={{0,2},{1,3},{4,6},{5,7},{8,10},{9,11},{12,14},{13,15},{18,16},{19,... | collective-permute-start | bytes 3538952 | tf_op jit(solution)/shard_map/ppermute | solution.py:40
  124.8 50.3 %collective-permute-start.19 = (bf16[2,192,1536]{2,1,0:T(8,128)(2,1)S(1)}, bf16[2,192,1536]{2,1,0:T(8,128)(2,1)S(1)}, u32[]{:S(2)}, u32[]{:S(2)}) collective-permute-start(bf16[2,192,1536]{2,1,0:T(8,128)(2,1)S(1)} %collective-permute-done.17), channel_id=1, source_target_pairs={{0,4},{1,5},{4,8},{5,9},{8,12},{9,13},{12,0},{13,1},{18,22},{19,23... | collective-permute-start | bytes 3538952 | tf_op jit(solution)/shard_map/ppermute | solution.py:40
  126.9 57.5 %collective-permute-start.18 = (bf16[2,192,1536]{2,1,0:T(8,128)(2,1)S(1)}, bf16[2,192,1536]{2,1,0:T(8,128)(2,1)S(1)}, u32[]{:S(2)}, u32[]{:S(2)}) collective-permute-start(bf16[2,192,1536]{2,1,0:T(8,128)(2,1)S(1)} %collective-permute-done.17), channel_id=1, source_target_pairs={{0,2},{1,3},{4,6},{5,7},{8,10},{9,11},{12,14},{13,15},{18,16},{19,... | collective-permute-start | bytes 3538952 | tf_op jit(solution)/shard_map/ppermute | solution.py:40
  238.5 80.5 %collective-permute-start.42 = (bf16[2,256,768]{2,1,0:T(8,128)(2,1)}, bf16[2,256,768]{2,1,0:T(8,128)(2,1)}, u32[]{:S(2)}, u32[]{:S(2)}) collective-permute-start(bf16[2,256,768]{2,1,0:T(8,128)(2,1)} %pad_maximum_fusion.9), channel_id=1, source_target_pairs={{0,16},{1,17},{2,18},{3,19},{4,20},{5,21},{6,22},{7,23},{8,24},{9,... | collective-permute-start | bytes 2359304 | tf_op jit(solution)/shard_map/ppermute | solution.py:40
  244.0 38.3 %collective-permute-start.24 = (bf16[1024,768]{1,0:T(8,128)(2,1)S(1)}, bf16[1024,768]{1,0:T(8,128)(2,1)S(1)}, u32[]{:S(2)}, u32[]{:S(2)}) collective-permute-start(bf16[1024,768]{1,0:T(8,128)(2,1)S(1)} %multiply_convert_fusion.5), channel_id=1, source_target_pairs={{0,1},{2,3},{4,5},{6,7},{8,9},{10,11},{12,13},{14,15},{16,17},{18,... | collective-permute-start | bytes 4718600 | tf_op jit(solution)/shard_map/ppermute | solution.py:40
  335.7 104.9 %collective-permute-start.37 = (bf16[1024,768]{1,0:T(8,128)(2,1)}, bf16[1024,768]{1,0:T(8,128)(2,1)}, u32[]{:S(2)}, u32[]{:S(2)}) collective-permute-start(bf16[1024,768]{1,0:T(8,128)(2,1)} %convolution_convert_fusion.9), channel_id=1, source_target_pairs={{0,16},{1,17},{2,18},{3,19},{4,20},{5,21},{6,22},{7,23},{8,24},{9,... | collective-permute-start | bytes 4718600 | tf_op jit(solution)/shard_map/ppermute | solution.py:40
  436.2 105.8 %collective-permute-start.77 = (bf16[2,768,1536]{2,1,0:T(8,128)(2,1)S(1)}, bf16[2,768,1536]{2,1,0:T(8,128)(2,1)}, u32[]{:S(2)}, u32[]{:S(2)}) collective-permute-start(bf16[2,768,1536]{2,1,0:T(8,128)(2,1)S(1)} %pad_maximum_fusion.1), channel_id=1, source_target_pairs={{3,1},{7,5},{11,9},{15,13},{17,19},{21,23},{25,27},{29,31}} | collective-permute-start | bytes 14155784 | tf_op jit(solution)/shard_map/ppermute | solution.py:40
  438.5 85.6 %collective-permute-start.46 = (bf16[1024,768]{1,0:T(8,128)(2,1)S(1)}, bf16[1024,768]{1,0:T(8,128)(2,1)S(1)}, u32[]{:S(2)}, u32[]{:S(2)}) collective-permute-start(bf16[1024,768]{1,0:T(8,128)(2,1)S(1)} %add_convert_fusion.1), channel_id=1, source_target_pairs={{1,0},{3,2},{5,4},{7,6},{9,8},{11,10},{13,12},{15,14},{17,16},{19,... | collective-permute-start | bytes 4718600 | tf_op jit(solution)/shard_map/ppermute | solution.py:40
  442.5 38.6 %collective-permute-start.38 = (bf16[256,768]{1,0:T(8,128)(2,1)S(1)}, bf16[256,768]{1,0:T(8,128)(2,1)S(1)}, u32[]{:S(2)}, u32[]{:S(2)}) collective-permute-start(bf16[256,768]{1,0:T(8,128)(2,1)S(1)} %get-tuple-element.130), channel_id=1, source_target_pairs={{0,0},{1,16},{2,1},{3,17},{4,4},{5,20},{6,5},{7,21},{8,8},{9,24},{... | collective-permute-start | bytes 1179656 | tf_op jit(solution)/shard_map/ppermute | solution.py:40
  444.5 74.9 %collective-permute-start.39 = (bf16[256,768]{1,0:T(8,128)(2,1)S(1)}, bf16[256,768]{1,0:T(8,128)(2,1)S(1)}, u32[]{:S(2)}, u32[]{:S(2)}) collective-permute-start(bf16[256,768]{1,0:T(8,128)(2,1)S(1)} %get-tuple-element.131), channel_id=1, source_target_pairs={{0,1},{1,17},{2,0},{3,16},{4,5},{5,21},{6,4},{7,20},{8,9},{9,25},{... | collective-permute-start | bytes 1179656 | tf_op jit(solution)/shard_map/ppermute | solution.py:40
  465.5 54.9 %collective-permute-start.64 = (bf16[2,192,768]{2,1,0:T(8,128)(2,1)S(1)}, bf16[2,192,768]{2,1,0:T(8,128)(2,1)S(1)}, u32[]{:S(2)}, u32[]{:S(2)}) collective-permute-start(bf16[2,192,768]{2,1,0:T(8,128)(2,1)S(1)} %dynamic-slice_convert_fusion.2), channel_id=1, source_target_pairs={{1,5},{5,9},{9,13},{13,1},{19,23},{23,27},{27,31},{31,19}} | collective-permute-start | bytes 1769480 | tf_op jit(solution)/shard_map/ppermute | solution.py:40
  481.1 105.2 %collective-permute-start.44 = (bf16[1024,768]{1,0:T(8,128)(2,1)}, bf16[1024,768]{1,0:T(8,128)(2,1)}, u32[]{:S(2)}, u32[]{:S(2)}) collective-permute-start(bf16[1024,768]{1,0:T(8,128)(2,1)} %convolution_convert_fusion.4), channel_id=1, source_target_pairs={{0,16},{1,17},{2,18},{3,19},{4,20},{5,21},{6,22},{7,23},{8,24},{9,... | collective-permute-start | bytes 4718600 | tf_op jit(solution)/shard_map/ppermute | solution.py:40
  520.6 39.6 %collective-permute-start.65 = (bf16[2,192,768]{2,1,0:T(8,128)(2,1)S(1)}, bf16[2,192,768]{2,1,0:T(8,128)(2,1)}, u32[]{:S(2)}, u32[]{:S(2)}) collective-permute-start(bf16[2,192,768]{2,1,0:T(8,128)(2,1)S(1)} %add_convert_fusion.11), channel_id=1, source_target_pairs={{1,5},{5,9},{9,13},{13,1},{19,23},{23,27},{27,31},{31,19}} | collective-permute-start | bytes 1769480 | tf_op jit(solution)/shard_map/ppermute | solution.py:40
  568.5 155.2 %collective-permute-start.71 = (bf16[2,768,1536]{2,1,0:T(8,128)(2,1)}, bf16[2,768,1536]{2,1,0:T(8,128)(2,1)}, u32[]{:S(2)}, u32[]{:S(2)}) collective-permute-start(bf16[2,768,1536]{2,1,0:T(8,128)(2,1)} %pad_maximum_fusion), channel_id=1, source_target_pairs={{2,0},{6,4},{10,8},{14,12},{16,18},{20,22},{24,26},{28,30}} | collective-permute-start | bytes 14155784 | tf_op jit(solution)/shard_map/ppermute | solution.py:40
  577.7 95.4 %collective-permute-start.69 = (bf16[192,384]{1,0:T(8,128)(2,1)}, bf16[192,384]{1,0:T(8,128)(2,1)}, u32[]{:S(2)}, u32[]{:S(2)}) collective-permute-start(bf16[192,384]{1,0:T(8,128)(2,1)} %pad_maximum_fusion.23), channel_id=1, source_target_pairs={{1,17},{5,21},{9,25},{13,29},{19,19},{23,23},{27,27},{31,31}} | collective-permute-start | bytes 442376 | tf_op jit(solution)/shard_map/ppermute | solution.py:40
  582.0 92.3 %collective-permute-start.67 = (bf16[192,384]{1,0:T(8,128)(2,1)}, bf16[192,384]{1,0:T(8,128)(2,1)}, u32[]{:S(2)}, u32[]{:S(2)}) collective-permute-start(bf16[192,384]{1,0:T(8,128)(2,1)} %pad_maximum_fusion.21), channel_id=1, source_target_pairs={{1,1},{5,5},{9,9},{13,13},{19,3},{23,7},{27,11},{31,15}} | collective-permute-start | bytes 442376 | tf_op jit(solution)/shard_map/ppermute | solution.py:40
  586.3 98.2 %collective-permute-start.79 = (bf16[2,192,1536]{2,1,0:T(8,128)(2,1)}, bf16[2,192,1536]{2,1,0:T(8,128)(2,1)}, u32[]{:S(2)}, u32[]{:S(2)}) collective-permute-start(bf16[2,192,1536]{2,1,0:T(8,128)(2,1)} %add_convert_fusion.5), channel_id=1, source_target_pairs={{1,5},{5,9},{9,13},{13,1},{19,23},{23,27},{27,31},{31,19}} | collective-permute-start | bytes 3538952 | tf_op jit(solution)/shard_map/ppermute | solution.py:40
  687.9 105.9 %collective-permute-start.80 = (bf16[2,192,1536]{2,1,0:T(8,128)(2,1)}, bf16[2,192,1536]{2,1,0:T(8,128)(2,1)}, u32[]{:S(2)}, u32[]{:S(2)}) collective-permute-start(bf16[2,192,1536]{2,1,0:T(8,128)(2,1)} %add_convert_fusion.4), channel_id=1, source_target_pairs={{1,5},{5,9},{9,13},{13,1},{19,23},{23,27},{27,31},{31,19}} | collective-permute-start | bytes 3538952 | tf_op jit(solution)/shard_map/ppermute | solution.py:40
  697.1 110.0 %collective-permute-start.49 = (bf16[256,768]{1,0:T(8,128)(2,1)}, bf16[256,768]{1,0:T(8,128)(2,1)S(1)}, u32[]{:S(2)}, u32[]{:S(2)}) collective-permute-start(bf16[256,768]{1,0:T(8,128)(2,1)} %get-tuple-element.124), channel_id=1, source_target_pairs={{0,0},{1,16},{2,1},{3,17},{4,4},{5,20},{6,5},{7,21},{8,8},{9,24},{... | collective-permute-start | bytes 1179656 | tf_op jit(solution)/shard_map/ppermute | solution.py:40
  732.4 58.1 %collective-permute-start.72 = (bf16[2,192,1536]{2,1,0:T(8,128)(2,1)}, bf16[2,192,1536]{2,1,0:T(8,128)(2,1)S(1)}, u32[]{:S(2)}, u32[]{:S(2)}) collective-permute-start(bf16[2,192,1536]{2,1,0:T(8,128)(2,1)} %dynamic-slice_convert_fusion.1), channel_id=1, source_target_pairs={{0,4},{4,8},{8,12},{12,0},{18,22},{22,26},{26,30},{30,18}} | collective-permute-start | bytes 3538952 | tf_op jit(solution)/shard_map/ppermute | solution.py:40
  736.0 48.5 %collective-permute-start.59 = (bf16[2,192,768]{2,1,0:T(8,128)(2,1)}, bf16[2,192,768]{2,1,0:T(8,128)(2,1)S(1)}, u32[]{:S(2)}, u32[]{:S(2)}) collective-permute-start(bf16[2,192,768]{2,1,0:T(8,128)(2,1)} %add_convert_fusion.14), channel_id=1, source_target_pairs={{1,5},{5,9},{9,13},{13,1},{19,23},{23,27},{27,31},{31,19}} | collective-permute-start | bytes 1769480 | tf_op jit(solution)/shard_map/ppermute | solution.py:40
  740.4 46.4 %collective-permute-start.53 = (bf16[2,192,768]{2,1,0:T(8,128)(2,1)}, bf16[2,192,768]{2,1,0:T(8,128)(2,1)}, u32[]{:S(2)}, u32[]{:S(2)}) collective-permute-start(bf16[2,192,768]{2,1,0:T(8,128)(2,1)} %add_convert_fusion.17), channel_id=1, source_target_pairs={{0,4},{4,8},{8,12},{12,0},{18,22},{22,26},{26,30},{30,18}} | collective-permute-start | bytes 1769480 | tf_op jit(solution)/shard_map/ppermute | solution.py:40
  (259 other events, 4674.1 us)

commit v2 on v1

--- a/solution.py
+++ b/solution.py
@@ -1,6 +1,10 @@
+import functools
+
 import jax
 import jax.numpy as jnp
 from jax import lax
+from jax.experimental import pallas as pl
+from jax.experimental.pallas import tpu as pltpu
 from jax.sharding import PartitionSpec as P
 
 HEAD = 64
@@ -62,7 +66,7 @@
     return (scaled - first - normal * second) * scale, jnp.sum(grad * normal, axis=0)
 
 
-ORDER = (("q", 0), ("q", 1), ("k", 0), ("k", 1), ("v", 0), ("v", 1), ("q", 2), ("v", 2), ("k", 2), ("o", 2), ("o", 0), ("o", 1))
+ORDER = (("q", 0), ("q", 1), ("q", 2), ("o", 2), ("o", 0), ("o", 1), ("k", 0), ("k", 1), ("v", 0), ("v", 1), ("k", 2), ("v", 2))
 
 
 def pack_heads(parts):
@@ -125,9 +129,557 @@
     return 0.5 * value * (1.0 + soft), slope
 
 
+MESH = pl.DeviceIdType.MESH
+GROUPS = ("att", "crs", "up", "dn")
+BLOCK = 256
+VMEM_BYTES = 62 * 2**20
+
+
+def lanes(shape):
+    return lax.broadcasted_iota(jnp.int32, shape, len(shape) - 1)
+
+
+def subs(shape):
+    return lax.broadcasted_iota(jnp.int32, shape, 0)
+
+
+def strip(i, size):
+    return pl.ds(pl.multiple_of(i * size, size), size)
+
+
+def head_place(h):
+    two = (h == 2).astype(jnp.int32)
+    one = (h >= 1).astype(jnp.int32)
+    return two, 2 + 2 * two, 3 + two, 1 - two, HEAD * (one - two), HEAD * one
+
+
+def each(count, step):
+    def run(i, carry):
+        step(i)
+        return carry
+
+    lax.fori_loop(0, count, run, 0)
+
+
+class Place:
+    def __init__(self, planes):
+        self.planes = planes
+        self.c = lax.axis_index("section")
+        self.z = lax.axis_index("dp")
+        self.t = lax.axis_index("tensor")
+        self.y = lax.div(self.t, 2)
+        self.r = lax.rem(self.t, 2)
+        self.twin = (1 - self.c, self.z, self.t)
+        self.above = (self.c, lax.rem(self.z + 1, planes), self.t)
+        self.below = (self.c, lax.rem(self.z + planes - 1, planes), self.t)
+        self.across = (self.c, self.z, lax.rem(self.t + 2, 4))
+        self.beside = (self.c, self.z, self.t + 1 - 2 * self.r)
+        self.relays = self.c == self.y
+        self.encodes = self.r == 0
+        self.decodes = self.r == 1
+
+    def meet(self):
+        barrier = pltpu.get_barrier_semaphore()
+        peers = [self.above, self.below]
+        for dc in range(2):
+            for dt in range(4):
+                if dc or dt:
+                    peers.append((lax.rem(self.c + dc, 2), self.z, lax.rem(self.t + dt, 4)))
+        for peer in peers:
+            pl.semaphore_signal(barrier, inc=1, device_id=peer, device_id_type=MESH)
+        pl.semaphore_wait(barrier, len(peers))
+
+
+def push(source, goal, sent, got, device):
+    return pltpu.make_async_remote_copy(
+        src_ref=source, dst_ref=goal, send_sem=sent, recv_sem=got, device_id=device, device_id_type=MESH
+    )
+
+
+def both(first, second):
+    return jnp.logical_and(first, second)
+
+
+def center(values):
+    middle = values - jnp.mean(values, axis=-1, keepdims=True)
+    scale = lax.rsqrt(jnp.mean(middle * middle, axis=-1, keepdims=True) + EPSILON)
+    return middle * scale, scale
+
+
+def attend_block(h, p, o, lse, lse_row, bias, kx, qx, vt, causal):
+    count = p.shape[0]
+    qt, kt, vtile, ot, qlo, vlo = head_place(h)
+    lane = lanes((count, TILE))
+    in_q = both(lane >= qlo, lane < qlo + HEAD)
+    in_v = both(lane >= vlo, lane < vlo + HEAD)
+    spare = HEAD - qlo
+    kx[...] = jnp.where(lane == spare, bias[...], jnp.where(in_q, p[:, strip(kt, TILE)], jnp.zeros((), LOW)))
+    vt[...] = jnp.where(in_v, p[:, strip(vtile, TILE)].astype(WIDE), 1.0).T.astype(LOW)
+    qx[...] = jnp.where(
+        in_q, p[:, strip(qt, TILE)].astype(WIDE) * SCORE_SCALE, jnp.where(lane == spare, 1.0, 0.0)
+    ).astype(LOW)
+    scores = mm_nt(kx[...], qx[...])
+    if causal:
+        scores = jnp.where(subs(scores.shape) <= lanes(scores.shape), scores, NEG_FILL)
+    top = jnp.max(scores, axis=0, keepdims=True)
+    power = jnp.exp(scores - top).astype(LOW)
+    out = mm(vt[...], power)
+    total = jnp.where(vlo == 0, out[HEAD : HEAD + 1, :], out[0:1, :])
+    result = (out / total).T
+    o[:, strip(ot, TILE)] = jnp.where(in_v, result, o[:, strip(ot, TILE)].astype(WIDE)).astype(LOW)
+    row = subs((8, count))
+    lse[...] = jnp.where(row == lse_row, top + jnp.log(total), lse[...])
+
+
+def forward_kernel(
+    planes, self_in, crs_in, up_in, dn_in, x_in, cot_in, gain_in, bias_self, bias_cross,
+    w_att, w_crs, w_up, w_dn, cot, first, p_self, o_self, lse_self, mid, second, act, slope, late, third,
+    memory, p_cross, o_cross, lse_cross, gains_out,
+    x_v, att_v, crs_v, up_v, dn_v, first_v, p_v, o_v, lse_v, mid_v, second_v, act_v, slope_v, late_v, memory_v,
+    send_v, recv_v, gain_v, kx, qx, vt,
+    x_sem, x_sent, z_got, z_sent, y_got, y_sent, c_sem,
+    row_got, row_sent, fwd_sem, cot_got, ex_got, ex_sent, mem_got, mem_sent, mf_got, mf_sent, gain_sem, put_sem,
+):
+    at = Place(planes)
+    c, z, t, y, r = at.c, at.z, at.t, at.y, at.r
+    rows = x_in.shape[1]
+    slot = x_v.shape[0]
+    tiles = slot // BLOCK
+    depth = up_in.shape[0]
+    vmem = {"att": att_v, "crs": crs_v, "up": up_v, "dn": dn_v}
+    shard = {"att": self_in, "up": up_in, "dn": dn_in}
+    here = pl.ds(pl.multiple_of(z * depth, depth), depth)
+    at.meet()
+
+    relay_dev = (y, z, 2 * y + c)
+    stays = both(c == y, r == c)
+
+    def launch(g):
+        i = GROUPS.index(g)
+        goal = vmem[g].at[r, here, :]
+
+        @pl.when(stays)
+        def _():
+            pltpu.make_async_copy(shard[g], goal, x_sem.at[i, r]).start()
+
+        @pl.when(jnp.logical_not(stays))
+        def _():
+            push(shard[g], goal, x_sent.at[i], x_sem.at[i, r], relay_dev).start()
+
+    crs_dev = (y, z, 2 * y + 1)
+    crs_stays = both(c == y, r == 1)
+    side = crs_in.shape[1]
+
+    def crs_goal(block, section):
+        return crs_v.at[block, here, pl.ds(pl.multiple_of((1 - section) * side, side), side)]
+
+    def launch_crs():
+        @pl.when(crs_stays)
+        def _():
+            pltpu.make_async_copy(crs_in, crs_goal(r, c), c_sem.at[r, c]).start()
+
+        @pl.when(jnp.logical_not(crs_stays))
+        def _():
+            push(crs_in, crs_goal(r, c), x_sent.at[1], c_sem.at[r, c], crs_dev).start()
+
+    row_goal = x_v.at[strip(t, rows), :]
+    cot_goal = cot.at[strip(t, rows), :]
+
+    def launch_rows(s):
+        dev = (y, z, 2 * s + c)
+        own = both(both(c == y, r == c), y == s)
+
+        @pl.when(own)
+        def _():
+            pltpu.make_async_copy(x_in.at[s], row_goal, row_got.at[r]).start()
+
+        @pl.when(jnp.logical_not(own))
+        def _():
+            push(x_in.at[s], row_goal, row_sent.at[s], row_got.at[r], dev).start()
+
+    cot_stays = both(c == y, r == 1)
+
+    def launch_cot():
+        dev = (y, z, 2 * c + 1)
+
+        @pl.when(cot_stays)
+        def _():
+            pltpu.make_async_copy(cot_in.at[c], cot_goal, cot_got.at[r]).start()
+
+        @pl.when(jnp.logical_not(cot_stays))
+        def _():
+            push(cot_in.at[c], cot_goal, row_sent.at[2], cot_got.at[r], dev).start()
+
+    gain_copy = push(gain_in, gain_v.at[c], gain_sem.at[0], gain_sem.at[1], at.twin)
+    gain_copy.start()
+    launch("att")
+    launch_rows(0)
+    launch_rows(1)
+    launch_crs()
+    launch("up")
+    launch("dn")
+    launch_cot()
+
+    def piece(g, k):
+        j = lax.rem(z - k + planes, planes)
+        return vmem[g].at[:, pl.ds(pl.multiple_of(j * depth, depth), depth), :]
+
+    def ring(g, k):
+        i = GROUPS.index(g)
+        return push(piece(g, k - 1), piece(g, k - 1), z_sent.at[i, k - 1], z_got.at[i, k - 1], at.above)
+
+    def ring_in(g, k):
+        i = GROUPS.index(g)
+        return push(piece(g, k), piece(g, k), z_sent.at[i, k - 1], z_got.at[i, k - 1], at.above)
+
+    def cross_over(g, k):
+        i = GROUPS.index(g)
+        return push(piece(g, k), piece(g, k), y_sent.at[i, k], y_got.at[i, k], at.across)
+
+    def member(g):
+        return both(at.relays, at.decodes) if g == "crs" else at.relays
+
+    def listens(g):
+        other = jnp.logical_not(at.relays)
+        return both(other, at.decodes) if g == "crs" else other
+
+    def arrive(g, k):
+        i = GROUPS.index(g)
+        if k:
+            ring_in(g, k).wait_recv()
+        elif g == "crs":
+            for block in range(2):
+                for section in range(2):
+                    goal = crs_goal(block, section)
+                    push(goal, goal, x_sent.at[1], c_sem.at[block, section], at.twin).wait_recv()
+        else:
+            for block in range(2):
+                goal = vmem[g].at[block, here, :]
+                push(goal, goal, x_sent.at[i], x_sem.at[i, block], at.twin).wait_recv()
+
+    def relay_up(g, k):
+        @pl.when(member(g))
+        def _():
+            arrive(g, k)
+            if k + 1 < planes:
+                ring(g, k + 1).start()
+
+    def relay_over(g, k):
+        @pl.when(member(g))
+        def _():
+            cross_over(g, k).start()
+
+    def relay(g, k):
+        relay_up(g, k)
+        relay_over(g, k)
+
+    def settle(g):
+        @pl.when(listens(g))
+        def _():
+            for k in range(planes):
+                cross_over(g, k).wait_recv()
+
+    puts = []
+
+    def put(source, goal):
+        copy = pltpu.make_async_copy(source, goal, put_sem.at[len(puts)])
+        copy.start()
+        puts.append(copy)
+        return copy
+
+    relay("att", 0)
+    half = pl.ds(pl.multiple_of(c * 2 * rows, 2 * rows), 2 * rows)
+    far_half = pl.ds(pl.multiple_of((1 - c) * 2 * rows, 2 * rows), 2 * rows)
+    for k in range(2):
+        goal = x_v.at[strip(2 * c + k, rows), :]
+        push(goal, goal, row_sent.at[0], row_got.at[k], at.twin).wait_recv()
+    rows_on = push(x_v.at[half, :], x_v.at[half, :], fwd_sem.at[0], fwd_sem.at[1], at.twin)
+    rows_on.start()
+    relay("att", 1)
+    push(gain_in, gain_v.at[1 - c], gain_sem.at[0], gain_sem.at[1], at.twin).wait_recv()
+    gain_here = pltpu.make_async_copy(gain_in, gain_v.at[c], gain_sem.at[2])
+    gain_here.start()
+    gain_here.wait()
+    gains = gain_v.at[r]
+    push(x_v.at[far_half, :], x_v.at[far_half, :], fwd_sem.at[0], fwd_sem.at[1], at.twin).wait_recv()
+
+    def enter(i):
+        q = strip(i, BLOCK)
+        first_v[q, :] = (center(x_v[q, :].astype(WIDE))[0] * gains[0:1, :]).astype(LOW)
+
+    each(tiles, enter)
+    put(first_v, first)
+    relay("att", 2)
+    relay("att", 3)
+
+    @pl.when(at.decodes)
+    def _():
+        for k in range(2):
+            goal = cot.at[strip(2 * c + k, rows), :]
+            push(goal, goal, row_sent.at[2], cot_got.at[k], at.twin).wait_recv()
+        push(cot.at[half, :], cot.at[half, :], fwd_sem.at[2], fwd_sem.at[3], at.twin).start()
+
+    for k in range(4):
+        relay("crs", k)
+    relay("up", 0)
+    settle("att")
+
+    def project(source, weights, part):
+        def run(i):
+            q = strip(i, BLOCK)
+            for b in range(2):
+                if part != "kv":
+                    p_v[b, q, 0:256] = mm(source[q, :], weights[b, :, 0:256]).astype(LOW)
+                if part != "q":
+                    p_v[b, q, 256:640] = mm(source[q, :], weights[b, :, 384:768]).astype(LOW)
+
+        each(tiles, run)
+
+    project(first_v, att_v, "all")
+    p_put = put(p_v, p_self)
+    o_v[...] = jnp.zeros_like(o_v)
+    lse_v[...] = jnp.zeros_like(lse_v)
+    relay("up", 1)
+
+    def attend_half(b, bias, causal):
+        def run(h):
+            attend_block(h, p_v.at[b], o_v.at[b], lse_v, 3 * b + h, bias, kx, qx, vt, causal)
+
+        each(3, run)
+
+    for b in range(2):
+        pl.when(at.encodes)(functools.partial(attend_half, b, bias_self, False))
+        pl.when(at.decodes)(functools.partial(attend_half, b, bias_self, True))
+        relay("up", 2 + b)
+    relay("dn", 0)
+    o_put = put(o_v, o_self)
+    lse_put = put(lse_v, lse_self)
+
+    def exchange(k, i):
+        q = strip(i, BLOCK)
+        return push(send_v.at[k, q, :], recv_v.at[k, q, :], ex_sent.at[k, i], ex_got.at[k, i], at.twin)
+
+    def out_project(k, weights):
+        def run(i):
+            q = strip(i, BLOCK)
+            part = mm_nt(o_v[0, q, :], weights[0, :, 128:384]) + mm_nt(o_v[1, q, :], weights[1, :, 128:384])
+            send_v[k, q, :] = part.astype(LOW)
+            exchange(k, i).start()
+
+        each(tiles, run)
+
+    def joined(k, i):
+        q = strip(i, BLOCK)
+        exchange(k, i).wait_recv()
+        return send_v[k, q, :].astype(WIDE) + recv_v[k, q, :].astype(WIDE)
+
+    out_project(0, att_v)
+    relay("dn", 1)
+
+    def middle(i):
+        q = strip(i, BLOCK)
+        value = x_v[q, :].astype(WIDE) + joined(0, i)
+        mid_v[q, :] = value
+        second_v[q, :] = (center(value)[0] * gains[1:2, :]).astype(LOW)
+
+    each(tiles, middle)
+    put(mid_v, mid)
+    put(second_v, second)
+    put(att_v, w_att)
+
+    def mem_send(i):
+        q = pl.ds(pl.multiple_of(c * 2 * BLOCK + i * BLOCK, BLOCK), BLOCK)
+        return push(memory_v.at[q, :], memory_v.at[q, :], mem_sent.at[i], mem_got.at[i], at.beside)
+
+    def mem_forward(i, core):
+        q = pl.ds(pl.multiple_of(core * 2 * BLOCK + i * BLOCK, BLOCK), BLOCK)
+        return push(memory_v.at[q, :], memory_v.at[q, :], mf_sent.at[i], mf_got.at[i], at.twin)
+
+    settle("up")
+    put(up_v, w_up)
+
+    @pl.when(at.encodes)
+    def _():
+        def run(i):
+            q = strip(i, BLOCK)
+            for b in range(2):
+                value, grade = gelu_parts(mm(second_v[q, :], up_v[b]))
+                act_v[b, q, :] = value.astype(LOW)
+                slope_v[b, q, :] = grade.astype(LOW)
+
+        each(tiles, run)
+
+    relay("dn", 2)
+    relay("dn", 3)
+    settle("dn")
+    put(dn_v, w_dn)
+    put(act_v, act)
+    put(slope_v, slope)
+
+    @pl.when(at.encodes)
+    def _():
+        def run(i):
+            q = strip(i, BLOCK)
+            part = mm_nt(act_v[0, q, :], dn_v[0]) + mm_nt(act_v[1, q, :], dn_v[1])
+            send_v[1, q, :] = part.astype(LOW)
+            exchange(1, i).start()
+
+        each(tiles, run)
+
+        def finish(n):
+            i = lax.rem(n + 2 * c, 4)
+            q = strip(i, BLOCK)
+            value = mid_v[q, :] + joined(1, i)
+            late_v[q, :] = value
+            memory_v[q, :] = (center(value)[0] * gains[2:3, :]).astype(LOW)
+
+            @pl.when(n < 2)
+            def _():
+                mem_send(n).start()
+
+        each(tiles, finish)
+
+    p_put.wait()
+    o_put.wait()
+    lse_put.wait()
+    puts[0].wait()
+    settle("crs")
+
+    @pl.when(at.decodes)
+    def _():
+        project(second_v, crs_v, "q")
+        for i in range(2):
+            mem_send(i).wait_recv()
+            mem_forward(i, c).start()
+        for i in range(2):
+            mem_forward(i, 1 - c).wait_recv()
+        project(memory_v, crs_v, "kv")
+        o_v[...] = jnp.zeros_like(o_v)
+        lse_v[...] = jnp.zeros_like(lse_v)
+        attend_half(0, bias_cross, False)
+        attend_half(1, bias_cross, False)
+        out_project(1, crs_v)
+
+        def finish(i):
+            q = strip(i, BLOCK)
+            value = mid_v[q, :] + joined(1, i)
+            late_v[q, :] = value
+            first_v[q, :] = (center(value)[0] * gains[2:3, :]).astype(LOW)
+
+        each(tiles, finish)
+
+    put(crs_v, w_crs)
+    put(p_v, p_cross)
+    put(o_v, o_cross)
+    put(lse_v, lse_cross)
+    put(late_v, late)
+    put(first_v, third)
+    put(memory_v, memory)
+    put(gains, gains_out)
+
+    skip = (id(puts[0]), id(p_put), id(o_put), id(lse_put))
+    for copy in puts:
+        if id(copy) not in skip:
+            copy.wait()
+    gain_copy.wait_send()
+    rows_on.wait_send()
+
+    @pl.when(jnp.logical_not(stays))
+    def _():
+        for g in ("att", "up", "dn"):
+            push(shard[g], vmem[g].at[r, here, :], x_sent.at[GROUPS.index(g)], x_sem.at[0, 0], relay_dev).wait_send()
+
+    @pl.when(jnp.logical_not(crs_stays))
+    def _():
+        push(crs_in, crs_goal(r, c), x_sent.at[1], c_sem.at[0, 0], crs_dev).wait_send()
+
+    for s in range(2):
+
+        @pl.when(jnp.logical_not(both(both(c == y, r == c), y == s)))
+        def _():
+            push(x_in.at[s], row_goal, row_sent.at[s], row_got.at[r], at.twin).wait_send()
+
+    @pl.when(jnp.logical_not(cot_stays))
+    def _():
+        push(cot_in.at[c], cot_goal, row_sent.at[2], cot_got.at[r], at.twin).wait_send()
+
+    for g in GROUPS:
+
+        @pl.when(member(g))
+        def _():
+            for k in range(1, planes):
+                ring(g, k).wait_send()
+            for k in range(planes):
+                cross_over(g, k).wait_send()
+
+    def drain(i):
+        exchange(0, i).wait_send()
+        exchange(1, i).wait_send()
+
+    each(tiles, drain)
+
+    @pl.when(at.encodes)
+    def _():
+        for i in range(2):
+            mem_send(i).wait_send()
+
+    @pl.when(at.decodes)
+    def _():
+        for i in range(2):
+            mem_forward(i, c).wait_send()
+        cot_on = push(cot.at[half, :], cot.at[half, :], fwd_sem.at[2], fwd_sem.at[3], at.twin)
+        cot_on.wait_send()
+        push(cot.at[far_half, :], cot.at[far_half, :], fwd_sem.at[2], fwd_sem.at[3], at.twin).wait_recv()
+
+
+def forward_call(planes, slot, width, hidden, args):
+    shape = jax.ShapeDtypeStruct
+    weights = [(2, width, width), (2, width, width), (2, width, hidden), (2, width, hidden)]
+    packed, outs, square = (2, slot, 640), (2, slot, 256), (slot, width)
+    out_shape = (
+        [shape(s, LOW) for s in weights]
+        + [shape(square, LOW), shape(square, LOW), shape(packed, LOW), shape(outs, LOW), shape((8, slot), WIDE)]
+        + [shape(square, WIDE), shape(square, LOW), shape((2, slot, hidden), LOW), shape((2, slot, hidden), LOW)]
+        + [shape(square, WIDE), shape(square, LOW), shape(square, LOW)]
+        + [shape(packed, LOW), shape(outs, LOW), shape((8, slot), WIDE), shape((8, width), WIDE)]
+    )
+    groups = len(GROUPS)
+    dma = pltpu.SemaphoreType.DMA
+    scratch = (
+        [pltpu.VMEM(square, LOW)]
+        + [pltpu.VMEM(s, LOW) for s in weights]
+        + [pltpu.VMEM(square, LOW), pltpu.VMEM(packed, LOW), pltpu.VMEM(outs, LOW), pltpu.VMEM((8, slot), WIDE)]
+        + [pltpu.VMEM(square, WIDE), pltpu.VMEM(square, LOW)]
+        + [pltpu.VMEM((2, slot, hidden), LOW)] * 2
+        + [pltpu.VMEM(square, WIDE), pltpu.VMEM(square, LOW)]
+        + [pltpu.VMEM((2,) + square, LOW)] * 2
+        + [pltpu.VMEM((2, 8, width), WIDE)]
+        + [pltpu.VMEM((slot, TILE), LOW)] * 2
+        + [pltpu.VMEM((TILE, slot), LOW)]
+        + [dma((groups, 2)), dma((groups,)), dma((groups, planes)), dma((groups, planes))]
+        + [dma((groups, planes)), dma((groups, planes)), dma((2, 2))]
+        + [dma((2,)), dma((3,)), dma((4,)), dma((2,)), dma((2, 4)), dma((2, 4))]
+        + [dma((2,)), dma((2,)), dma((2,)), dma((2,)), dma((3,)), dma((24,))]
+    )
+    any_spec = pl.BlockSpec(memory_space=pl.ANY)
+    vmem_spec = pl.BlockSpec(memory_space=pltpu.VMEM)
+    return pl.pallas_call(
+        functools.partial(forward_kernel, planes),
+        out_shape=out_shape,
+        in_specs=[any_spec] * 6 + [vmem_spec] * 3,
+        out_specs=[any_spec] * len(out_shape),
+        scratch_shapes=scratch,
+        compiler_params=pltpu.CompilerParams(collective_id=0, has_side_effects=True, vmem_limit_bytes=VMEM_BYTES),
+    )(*args)
+
+
 def ring_gather(lay, shard):
     planes = lay.planes
     rows = shard.shape[1]
+    if planes > 4:
+        piece = lax.all_gather(shard, "dp", axis=1, tiled=True)
+        across = lay.route(piece, lambda c, z, t: (c, z, (t + 2) % 4) if c == t // 2 else None)
+        return jnp.where(lay.relays, piece, across)
     relay = lambda c, z, t: (c, (z + 1) % planes, t) if c == t // 2 else None
     whole = jnp.zeros((shard.shape[0], planes * rows, shard.shape[2]), shard.dtype)
     piece = shard
@@ -148,6 +700,8 @@
         low, lambda c, z, t: (c, z, (t + 2) % 4) if (c != t // 2 and t % 2 == holder) else None
     )
     summed = low.astype(WIDE) + across.astype(WIDE)
+    if planes > 4:
+        return lax.psum_scatter(summed.astype(LOW), "dp", scatter_dimension=1, tiled=True)
     relay = lambda c, z, t: (c, (z + 1) % planes, t) if (c == t // 2 and t % 2 == holder) else None
     take = lambda j: lax.dynamic_slice_in_dim(summed, (j % planes) * rows, rows, 1)
     running = take(lay.plane - 1)
@@ -166,7 +720,7 @@
     return same.astype(WIDE) + beside.astype(WIDE)
 
 
-def body(block_input, w_self, w_self_out, w_cross, w_up, w_down, norm_gains, lengths, task_mask, out_grad):
+def general_body(block_input, w_self, w_self_out, w_cross, w_up, w_down, norm_gains, lengths, task_mask, out_grad):
     lay = Layout()
     seqs, rows, width = block_input.shape[1:]
     slot = rows * lay.chips
@@ -382,6 +936,215 @@
     )
 
 
+def body(block_input, w_self, w_self_out, w_cross, w_up, w_down, norm_gains, lengths, task_mask, out_grad):
+    lay = Layout()
+    seqs, rows, width = block_input.shape[1:]
+    slot = rows * lay.chips
+    sec = lay.core
+    item = lay.item
+
+    if lay.planes != 4:
+        return general_body(
+            block_input, w_self, w_self_out, w_cross, w_up, w_down, norm_gains, lengths, task_mask, out_grad
+        )
+
+    depth = w_self.shape[1]
+    wide = w_self.shape[3]
+    hidden = w_up.shape[2]
+    self_block = pack_heads(
+        {"q": w_self[0, :, 0], "k": w_self[0, :, 1], "v": w_self[0, :, 2], "o": w_self_out[0].T}
+    )
+    pair = {"q": w_cross[0, :, 0], "o": w_cross[0, :, 1], "k": w_cross[0, :, 0], "v": w_cross[0, :, 1]}
+    pieces = [pair[n][:, HEAD * h : HEAD * (h + 1)] for n, h in ORDER]
+    cross_block = jnp.where(
+        sec == 1, jnp.concatenate(pieces[:6], axis=1), jnp.concatenate(pieces[6:], axis=1)
+    )
+    gain_block = jnp.concatenate([norm_gains[0].astype(WIDE), jnp.zeros((5, width), WIDE)], axis=0)
+
+    positions = jnp.arange(slot)
+    own_length = jnp.where(lay.is_decoder, lengths[1, item], lengths[0, item])
+    self_allowed = (positions[None, :] < own_length) & (
+        (positions[None, :] <= positions[:, None]) | jnp.logical_not(lay.is_decoder)
+    )
+    cross_allowed = jnp.broadcast_to(
+        ((positions < lengths[0, item]) & (task_mask[item] == 1))[None], (slot, slot)
+    )
+
+    def key_bias(allowed):
+        return jnp.broadcast_to(jnp.where(allowed, 0.0, NEG_FILL)[:, None], (slot, TILE)).astype(LOW)
+
+    (
+        w_att, w_crs, w_up_all, w_dn_all, cotangent, normed0, p_self, o_self, lse_self, x_mid, normed1, act, slope,
+        x_late, normed2, memory, p_cross, o_cross, lse_cross, gains,
+    ) = forward_call(
+        lay.planes,
+        slot,
+        width,
+        hidden,
+        (
+            self_block,
+            cross_block,
+            w_up[0],
+            w_down[0].T,
+            block_input[0],
+            out_grad,
+            gain_block,
+            key_bias(positions < own_length),
+            key_bias((positions < lengths[0, item]) & (task_mask[item] == 1)),
+        ),
+    )
+
+    def joined(partial):
+        low = partial.astype(LOW)
+        return low.astype(WIDE) + lay.other_core(low).astype(WIDE)
+
+    part = lambda w, name: jnp.concatenate([unpack_heads(w[0], name), unpack_heads(w[1], name)], axis=1)
+    att = {n: part(w_att, n) for n in "qkvo"}
+    crs = {n: part(w_crs, n) for n in "qkvo"}
+    up = jnp.concatenate([w_up_all[0], w_up_all[1]], axis=1)
+    down_t = jnp.concatenate([w_dn_all[0], w_dn_all[1]], axis=1)
+    pick = lambda p, cuts: jnp.concatenate([p[b][:, i : i + HEAD] for b in range(2) for i in cuts], axis=1)
+    q, k, v = pick(p_self, (0, 64, 128)), pick(p_self, (256, 320, 512)), pick(p_self, (384, 448, 576))
+    cq, ck, cv = pick(p_cross, (0, 64, 128)), pick(p_cross, (256, 320, 512)), pick(p_cross, (384, 448, 576))
+    out_self, out_cross = pick(o_self, (128, 192, 64)), pick(o_cross, (128, 192, 64))
+    lse_self, lse_cross = lse_self[:6, :, None], lse_cross[:6, :, None]
+    act_enc, slope_enc = (jnp.concatenate([v_[0], v_[1]], axis=1) for v_ in (act, slope))
+    x_late_enc = x_late
+    memory_enc = memory
+    def spread(value, first):
+        pick = value[jnp.where(first, lay.chip % 2, 1 - lay.chip % 2)]
+        flip = 0 if first else 1
+        return lay.route(pick, lambda c, z, t: (t // 2, z, 2 * ((t % 2) ^ flip) + c))
+
+    def merge_rows(mine, theirs):
+        low_half = jnp.where(lay.core == 0, mine, theirs)
+        high_half = jnp.where(lay.core == 0, theirs, mine)
+        return jnp.concatenate([low_half[0], low_half[1], high_half[0], high_half[1]], axis=0)
+
+    first = spread(block_input[0], True)
+    second = spread(block_input[0], False)
+    mine = jnp.where(item == 0, jnp.stack([first, second]), jnp.stack([second, first]))
+    x_rows = merge_rows(mine, lay.other_core(mine)).astype(WIDE)
+
+    pre_dec = mm(normed2, up)
+    act_dec, slope_dec = gelu_parts(pre_dec)
+    act_dec = act_dec.astype(LOW)
+    result_dec = (x_late + joined(mm_nt(act_dec, down_t))).astype(LOW)
+
+    d_out = cotangent.astype(WIDE)
+    d_pre = (slope_dec * mm(cotangent, down_t)).astype(LOW)
+    d_ffn_dec = jnp.concatenate([mm_tn(normed2, d_pre), mm_tn(cotangent, act_dec)], axis=1)
+    d_late_norm, d_gain2_dec = norm_back(x_late, gains[2], joined(mm_nt(d_pre, up)))
+    d_late = d_out + d_late_norm
+    grad_late = d_late.astype(LOW)
+    d_att = mm(grad_late, crs["o"]).astype(LOW)
+    d_cq, d_ck, d_cv = attend_back(cq, ck, cv, lse_cross, d_att, cross_allowed)
+    d_memory = joined(mm_nt(d_ck, crs["k"]) + mm_nt(d_cv, crs["v"]))
+    d_crs = {
+        "q": mm_tn(normed1, d_cq),
+        "k": mm_tn(memory, d_ck),
+        "v": mm_tn(memory, d_cv),
+        "o": mm_tn(grad_late, out_cross),
+    }
+    d_mid_norm, d_gain1_dec = norm_back(x_mid, gains[1], joined(mm_nt(d_cq, crs["q"])))
+    d_mid_dec = d_late + d_mid_norm
+
+    d_memory = lay.route(d_memory.astype(LOW), lambda c, z, t: (c, z, t ^ 1) if t % 2 == 1 else None).astype(WIDE)
+    d_late_enc, d_gain2_enc = norm_back(x_late_enc, gains[2], d_memory)
+    grad_late_enc = d_late_enc.astype(LOW)
+    d_pre = (slope_enc * mm(grad_late_enc, down_t)).astype(LOW)
+    d_ffn_enc = jnp.concatenate([mm_tn(normed1, d_pre), mm_tn(grad_late_enc, act_enc)], axis=1)
+    d_mid_norm, d_gain1_enc = norm_back(x_mid, gains[1], joined(mm_nt(d_pre, up)))
+    d_mid_enc = d_late_enc + d_mid_norm
+
+    d_mid = jnp.where(lay.is_decoder, d_mid_dec, d_mid_enc)
+    grad_mid = d_mid.astype(LOW)
+    d_att = mm(grad_mid, att["o"]).astype(LOW)
+    d_q, d_k, d_v = attend_back(q, k, v, lse_self, d_att, self_allowed)
+    d_norm = joined(mm_nt(d_q, att["q"]) + mm_nt(d_k, att["k"]) + mm_nt(d_v, att["v"]))
+    d_att_w = {
+        "q": mm_tn(normed0, d_q),
+        "k": mm_tn(normed0, d_k),
+        "v": mm_tn(normed0, d_v),
+        "o": mm_tn(grad_mid, out_self),
+    }
+    d_first, d_gain0 = norm_back(x_rows, gains[0], d_norm)
+    d_rows = d_mid + d_first
+
+    half = 3 * HEAD
+
+    def flip(v):
+        return jnp.where(lay.role == 0, v, v[::-1])
+
+    def blocks(parts):
+        return flip(jnp.stack(
+            [pack_heads({n: parts[n][:, half * b : half * (b + 1)] for n in parts}) for b in range(2)]
+        ))
+
+    def feed_blocks(both):
+        total = both.shape[1] // 2
+        return flip(jnp.stack(
+            [
+                jnp.concatenate(
+                    [both[:, hidden * b : hidden * (b + 1)], both[:, total + hidden * b : total + hidden * (b + 1)]],
+                    axis=1,
+                )
+                for b in range(2)
+            ]
+        ))
+
+    self_total = blocks(d_att_w)
+    home_self = hand_back(lay, ring_scatter(lay, self_total, 0), 0, 0) + hand_back(
+        lay, ring_scatter(lay, self_total, 1), 1, 1
+    )
+    home_feed = hand_back(lay, ring_scatter(lay, feed_blocks(d_ffn_enc), 0), 0, 0) + hand_back(
+        lay, ring_scatter(lay, feed_blocks(d_ffn_dec), 1), 1, 1
+    )
+    cross_total = ring_scatter(lay, blocks(d_crs), 1)
+    side = lambda names: jnp.stack(
+        [jnp.concatenate([unpack_heads(cross_total[b], n) for n in names], axis=1) for b in range(2)]
+    )
+    home_cross = hand_back(lay, side("kv"), 1, 0) + hand_back(lay, side("qo"), 1, 1)
+
+    g_self = jnp.stack([unpack_heads(home_self, n) for n in "qkv"], axis=1)[None]
+    g_self_out = unpack_heads(home_self, "o").T[None]
+    g_cross = home_cross.reshape(1, depth, 2, wide)
+    g_up = home_feed[:, :hidden][None]
+    g_down = home_feed[:, hidden:].T[None]
+
+    gain2 = jnp.where(lay.is_decoder, d_gain2_dec, d_gain2_enc)
+    gain1 = jnp.where(lay.is_decoder, d_gain1_dec, d_gain1_enc)
+    gain_rows = jnp.stack([d_gain0, gain1, gain2])
+    slots = jnp.stack(
+        [
+            jnp.where((lay.role == r) & (lay.core == 0), gain_rows, 0.0)
+            for r in range(2)
+        ]
+    )
+    gain_total = lax.psum(slots, AXES)[sec][None]
+
+    def rows_home(value):
+        mine = lax.dynamic_slice_in_dim(value, lay.core * 2 * rows, 2 * rows, 0).reshape(2, rows, width)
+        a = lay.route(mine[item], lambda c, z, t: (t % 2, z, 2 * c + t // 2))
+        b = lay.route(mine[1 - item], lambda c, z, t: (t % 2, z, 2 * c + 1 - t // 2))
+        even = lay.chip % 2 == 0
+        return jnp.where(even, jnp.stack([a, b]), jnp.stack([b, a]))[None]
+
+    block_output = rows_home(jnp.where(lay.is_decoder, result_dec, memory_enc))
+    input_grad = rows_home(d_rows.astype(LOW)).astype(WIDE)
+    return (
+        block_output,
+        input_grad,
+        g_self,
+        g_self_out,
+        g_cross,
+        g_up,
+        g_down,
+        gain_total[:, :2],
+        gain_total[:, 2],
+    )
+
+
 def solution(mesh):
     placed = (
         P("section", "dp", "tensor", None),

time: 866 us -> 810 us (0.935)
  Pallas kernels: 0 us -> 152 us
  starting transfers between devices: 203 us -> 78.3 us
  waiting for transfers between devices: 175 us -> 89.9 us
  local copies, waits for them, and re-layouts: 67.4 us -> 125 us
  matrix products: 199 us -> 159 us
  other arithmetic: 163 us -> 148 us
    pallas_call x0 -> x1, Pallas kernels: none -> 152 us  [forward_call(): pl.pallas_call(functools.partial(forward_kernel, planes), out_shape=out_s...]
    ppermute x83 -> x46, starting transfers between devices: 203 us -> 78.3 us  [route(): return lax.ppermute(value, AXES, pairs)]
    ppermute x83 -> x46, waiting for transfers between devices: 175 us -> 89.9 us  [route(): return lax.ppermute(value, AXES, pairs)]
    slice x1 -> x26, local copies, waits for them, and re-layouts: 0.03 us -> 24.3 us  [the longest x20 21.4 us: body(): p[b][:, i:i + HEAD]]
    dot_general x4 -> x2, matrix products: 42.8 us -> 20.9 us  [attend_back(): jnp.einsum('qhd,khd->hqk', split_heads(q), split_heads(k), preferred_elem...]
    reduce_sum x2 -> x0, other arithmetic: 20.4 us -> none  [attend(): total = jnp.sum(power, axis=-1, keepdims=True)]
    squeeze x2 -> x9, local copies, waits for them, and re-layouts: 0.34 us -> 14.6 us  [the longest x2 7.5 us: body(): v_[0]]
    concatenate x0 -> x6, local copies, waits for them, and re-layouts: none -> 13.7 us  [body(): jnp.concatenate([p[b][:, i:i + HEAD] for b in range(2) for i in cuts], ax...]
  transfers between devices with their start and end apart: 83 -> 46, of which waited for: 21 -> 8; matrix products, arithmetic and copies ran while one was open for 46% -> 48% of each run, Pallas kernels for 0% -> 0%
where the time goes in v2:
time: 810 us; the launch traced here: 798 us
  matrix products  159 us (20%)
  Pallas kernels  152 us (19%)
  other arithmetic  148 us (18%)
  local copies, waits for them, and re-layouts  125 us (15%)
  waiting for transfers between devices  89.9 us (11%)
  starting transfers between devices  78.3 us (10%)
  blocking collectives  42 us (5%)
    pallas_call x1, Pallas kernels, forward_call(): pl.pallas_call(functools.partial(forward_kernel, planes), out_shape=out_s...  152 us
    ppermute x46, waiting for transfers between devices, route(): return lax.ppermute(value, AXES, pairs)  89.9 us
    ppermute x46, starting transfers between devices, route(): return lax.ppermute(value, AXES, pairs)  78.3 us
    psum x1, blocking collectives, body(): gain_total = lax.psum(slots, AXES)[sec][None]  42 us
    dot_general x2, matrix products, attend_back(): jnp.einsum('qhd,khd->hqk', split_heads(d_out), split_heads(v), preferred_...  35.2 us
    convert_element_type x2, other arithmetic, attend_back(): d_scores = (probs * (d_probs - inner)).astype(LOW)  35 us
    dot_general x2, matrix products, attend_back(): jnp.einsum('hqk,qhd->khd', probs.astype(LOW), split_heads(d_out), preferr...  25 us
    dot_general x12, matrix products, mm_tn(): lax.dot_general(left, right, (((0,), (0,)), ((), ())), preferred_element_...  23.4 us
  transfers between devices with their start and end apart: 46, of which 8 were waited for; matrix products, arithmetic and copies ran while one was open for 48% of the time, Pallas kernels for 0%

profile of v2, /device:TPU:2, one launch (start us, length us, event | category | flops | bytes accessed | tf_op | source)
XLA Modules:
  0.0 798.0 jit_solution(11669889518874839718)
XLA Ops:
  10.6 151.5 %shard_map.169 = (bf16[2,768,768]{2,1,0:T(8,128)(2,1)}, bf16[2,768,768]{2,1,0:T(8,128)(2,1)}, bf16[2,768,768]{2,1,0:T(8,128)(2,1)}, bf16[2,768,768]{2,1,0:T(8,12...) custom-call(bf16[192,768]{1,0:T(8,128)(2,1)} %concatenate.195.self_i, ...), custom_call_target="tpu_custom_call" | custom-call | tf_op jit(solution)/shard_map/pallas_call | solution.py:666
  169.8 6.8 fusion.16
  184.4 5.2 fusion.209
  199.6 4.9 convolution_convert_fusion.3
  204.5 9.5 %collective-permute-start = (bf16[1024,768]{1,0:T(8,128)(2,1)}, bf16[1024,768]{1,0:T(8,128)(2,1)}, u32[]{:S(2)}, u32[]{:S(2)}) collective-permute-start(bf16[1024,768]{1,0:T(8,128)(2,1)} %convolution_convert_fusion.3), channel_id=1, source_target_pairs={{0,16},{1,17},{2,18},{3,19},{4,20},{5,21},{6,22},{7,23},{8,24},{9,... | collective-permute-start | bytes 4718600 | tf_op jit(solution)/shard_map/ppermute | solution.py:44
  264.5 10.6 %fusion.200 = f32[6,1024,1024]{1,2,0:T(8,128)} fusion(bf16[1024,6,64]{0,2,1:T(8,128)(2,1)S(1)} %bitcast.224, bf16[1024,6,64]{0,2,1:T(8,128)(2,1)S(1)} %bitcast.222), kind=kOutput, calls=%fused_computation.385 | convolution fusion | flops 805306368 | bytes 26738688 | tf_op jit(solution)/shard_map/qhd,khd->hqk/dot_general | solution.py:111
  279.0 10.2 %fusion.201 = f32[6,1024,1024]{1,2,0:T(8,128)} fusion(bf16[1024,6,64]{0,2,1:T(8,128)(2,1)S(1)} %bitcast.220, bf16[1024,6,64]{0,2,1:T(8,128)(2,1)S(1)} %bitcast.218), kind=kOutput, calls=%fused_computation.386 | convolution fusion | flops 805306368 | bytes 26738688 | tf_op jit(solution)/shard_map/qhd,khd->hqk/dot_general | solution.py:111
  327.9 12.5 %fusion.46 = bf16[6,64,1024]{2,1,0:T(8,128)(2,1)} fusion(bf16[1024,6,64]{0,2,1:T(8,128)(2,1)S(1)} %bitcast.239, f32[6,1024,1024]{1,2,0:T(8,128)} %fusion.200, f32[6,1024]{1,0:T(8,128)S(1)} %bitcast.262, pred[1024]{0:T(1024)(128)(4,1)S(1)} %copy-done.140), kind=kOutput, calls=%fused_computation.124 | convolution fusion | flops 830865408 | bytes 26764288 | tf_op jit(solution)/shard_map/hqk,qhd->khd/dot_general | solution.py:117
  340.4 18.1 %multiply_reduce_fusion.1 = (f32[6,1024]{1,0:T(8,128)}, f32[6,1024,1024]{1,2,0:T(8,128)}) fusion(f32[6,1024,1024]{1,2,0:T(8,128)} %fusion.200, f32[6,1024]{1,0:T(8,128)} %bitcast.260, pred[1024]{0:T(1024)(128)(4,1)} %get-tuple-element.107, bf16[1024,6,64]{0,2,1:T(8,128)(2,1)} %bitcast.240, bf16[1024,6,64]{0,2,1:T(8,128)(2,1)} %bitcast.244), kind=kOutput, calls=%fused_computation.4 | convolution fusion | flops 836757504 | bytes 51954688 | tf_op jit(solution)/shard_map/qhd,khd->hqk/dot_general | solution.py:114
  358.6 17.6 %multiply_convert_fusion.1 = bf16[6,1024,1024]{1,2,0:T(8,128)(2,1)S(1)} fusion(f32[6,1024,1024]{1,2,0:T(8,128)} %get-tuple-element.259, f32[6,1024,1024]{1,2,0:T(8,128)} %fusion.200, f32[6,1024]{1,0:T(8,128)} %get-tuple-element.258, f32[6,1024]{1,0:T(8,128)} %bitcast.261, pred[1024]{0:T(1024)(128)(4,1)} %get-tuple-element.107), kind=kLoop, calls=%fused_computation.3 | loop fusion | flops 37748736 | bytes 62964736 | tf_op jit(solution)/shard_map/convert_element_type | solution.py:116
  383.0 8.8 %multiply_convert_fusion.6 = bf16[6,64,1024]{2,1,0:T(8,128)(2,1)S(1)} fusion(bf16[1024,6,64]{0,2,1:T(8,128)(2,1)S(1)} %bitcast.225, bf16[6,1024,1024]{1,2,0:T(8,128)(2,1)} %copy-done.1), kind=kOutput, calls=%fused_computation.122 | convolution fusion | flops 806092800 | bytes 14155776 | tf_op jit(solution)/shard_map/hqk,qhd->khd/dot_general | solution.py:119
  425.6 20.4 %collective-permute-done.26 = bf16[2,768,768]{2,1,0:T(8,128)(2,1)S(1)} collective-permute-done((bf16[2,768,768]{2,1,0:T(8,128)(2,1)S(1)}, bf16[2,768,768]{2,1,0:T(8,128)(2,1)S(1)}, u32[]{:S(2)}, u32[]{:S(2)}) %collective-permute-start.26) | collective-permute-done | bytes 2359328 | tf_op jit(solution)/shard_map/ppermute | solution.py:44
  452.8 13.1 %collective-permute-done.1 = bf16[256,768]{1,0:T(8,128)(2,1)S(1)} collective-permute-done((bf16[256,768]{1,0:T(8,128)(2,1)S(1)}, bf16[256,768]{1,0:T(8,128)(2,1)S(1)}, u32[]{:S(2)}, u32[]{:S(2)}) %collective-permute-start.1) | collective-permute-done | bytes 393248 | tf_op jit(solution)/shard_map/ppermute | solution.py:44
  518.4 5.8 collective-permute-done.41
  529.9 5.7 multiply_reduce_fusion.4
  535.7 5.5 add_select_fusion
  543.3 12.5 %fusion.49 = bf16[6,64,1024]{2,1,0:T(8,128)(2,1)} fusion(bf16[1024,6,64]{0,2,1:T(8,128)(2,1)S(1)} %bitcast.241, f32[6,1024,1024]{1,2,0:T(8,128)} %fusion.201, f32[6,1024]{1,0:T(8,128)S(1)} %bitcast.263, pred[1024,1024]{0,1:T(8,128)(4,1)S(1)} %copy-done.16), kind=kOutput, calls=%fused_computation.125 | convolution fusion | flops 830865408 | bytes 27811840 | tf_op jit(solution)/shard_map/hqk,qhd->khd/dot_general | solution.py:117
  555.7 17.1 %multiply_reduce_fusion = (f32[6,1024]{1,0:T(8,128)S(1)}, f32[6,1024,1024]{1,2,0:T(8,128)}) fusion(f32[6,1024,1024]{1,2,0:T(8,128)} %fusion.201, f32[6,1024]{1,0:T(8,128)S(1)} %bitcast.264, pred[1024,1024]{0,1:T(8,128)(4,1)S(1)} %copy-done.16, bf16[1024,6,64]{0,2,1:T(8,128)(2,1)S(1)} %bitcast.242, bf16[1024,6,64]{0,2,1:T(8,128)(2,1)S(1)} %bitcast.243), kind=kOutput, calls=%fused_computation.1 | convolution fusion | flops 836757504 | bytes 53002240 | tf_op jit(solution)/shard_map/qhd,khd->hqk/dot_general | solution.py:114
  572.9 17.4 %multiply_convert_fusion = bf16[6,1024,1024]{1,2,0:T(8,128)(2,1)S(1)} fusion(f32[6,1024,1024]{1,2,0:T(8,128)} %get-tuple-element.261, f32[6,1024,1024]{1,2,0:T(8,128)} %fusion.201, f32[6,1024]{1,0:T(8,128)S(1)} %get-tuple-element.260, f32[6,1024]{1,0:T(8,128)S(1)} %bitcast.265, pred[1024,1024]{0,1:T(8,128)(4,1)S(1)} %copy-done.16), kind=kLoop, calls=%fused_computation | loop fusion | flops 37748736 | bytes 64012288 | tf_op jit(solution)/shard_map/convert_element_type | solution.py:116
  590.3 4.8 multiply_convert_fusion.4
  632.6 4.7 fusion.156
  641.1 17.4 %collective-permute-done.20 = bf16[2,768,768]{2,1,0:T(8,128)(2,1)} collective-permute-done((bf16[2,768,768]{2,1,0:T(8,128)(2,1)}, bf16[2,768,768]{2,1,0:T(8,128)(2,1)}, u32[]{:S(2)}, u32[]{:S(2)}) %collective-permute-start.20) | collective-permute-done | bytes 2359328 | tf_op jit(solution)/shard_map/ppermute | solution.py:44
  685.4 42.0 %psum.7 = f32[2,3,768]{2,1,0:T(4,128)} all-reduce(f32[2,3,768]{2,1,0:T(4,128)} %pad_maximum_fusion.23), channel_id=1, replica_groups=mesh['section'=2,'dp'=4,'tensor'=4] {'section','dp','tensor'}, use_global_device_ids=true, to_apply=%region_23.24 | all-reduce | flops 4608 | bytes 36864 | tf_op jit(solution)/shard_map/psum | solution.py:1124
  770.3 24.8 %collective-permute-done.39 = bf16[192,1536]{1,0:T(8,128)(2,1)S(1)} collective-permute-done((bf16[192,1536]{1,0:T(8,128)(2,1)S(1)}, bf16[192,1536]{1,0:T(8,128)(2,1)S(1)}, u32[]{:S(2)}, u32[]{:S(2)}) %collective-permute-start.39) | collective-permute-done | bytes 589856 | tf_op jit(solution)/shard_map/ppermute | solution.py:44
  (641 shorter events, 345.7 us)
Async XLA Ops:
  180.4 139.0 %collective-permute-start.3 = (bf16[1024,768]{1,0:T(8,128)(2,1)}, bf16[1024,768]{1,0:T(8,128)(2,1)}, u32[]{:S(2)}, u32[]{:S(2)}) collective-permute-start(bf16[1024,768]{1,0:T(8,128)(2,1)} %convolution_convert_fusion.2), channel_id=1, source_target_pairs={{0,16},{1,17},{2,18},{3,19},{4,20},{5,21},{6,22},{7,23},{8,24},{9,... | collective-permute-start | bytes 4718600 | tf_op jit(solution)/shard_map/ppermute | solution.py:44
  182.4 134.8 %collective-permute-start.9 = (bf16[256,768]{1,0:T(8,128)(2,1)}, bf16[256,768]{1,0:T(8,128)(2,1)S(1)}, u32[]{:S(2)}, u32[]{:S(2)}) collective-permute-start(bf16[256,768]{1,0:T(8,128)(2,1)} %get-tuple-element.193), channel_id=1, source_target_pairs={{0,0},{1,2},{2,16},{3,18},{4,4},{5,6},{6,20},{7,22},{8,8},{9,10},{... | collective-permute-start | bytes 1179656 | tf_op jit(solution)/shard_map/ppermute | solution.py:44
  184.3 132.9 %collective-permute-start.10 = (bf16[256,768]{1,0:T(8,128)(2,1)}, bf16[256,768]{1,0:T(8,128)(2,1)}, u32[]{:S(2)}, u32[]{:S(2)}) collective-permute-start(bf16[256,768]{1,0:T(8,128)(2,1)} %get-tuple-element.194), channel_id=1, source_target_pairs={{0,2},{1,0},{2,18},{3,16},{4,6},{5,4},{6,22},{7,20},{8,10},{9,8},{... | collective-permute-start | bytes 1179656 | tf_op jit(solution)/shard_map/ppermute | solution.py:44
  197.8 302.4 %collective-permute-start.40 = (bf16[2,768,1536]{2,1,0:T(8,128)(2,1)}, bf16[2,768,1536]{2,1,0:T(8,128)(2,1)}, u32[]{:S(2)}, u32[]{:S(2)}) collective-permute-start(bf16[2,768,1536]{2,1,0:T(8,128)(2,1)} %fusion.9), channel_id=1, source_target_pairs={{3,1},{7,5},{11,9},{15,13},{17,19},{21,23},{25,27},{29,31}} | collective-permute-start | bytes 14155784 | tf_op jit(solution)/shard_map/ppermute | solution.py:44
  204.5 214.4 %collective-permute-start = (bf16[1024,768]{1,0:T(8,128)(2,1)}, bf16[1024,768]{1,0:T(8,128)(2,1)}, u32[]{:S(2)}, u32[]{:S(2)}) collective-permute-start(bf16[1024,768]{1,0:T(8,128)(2,1)} %convolution_convert_fusion.3), channel_id=1, source_target_pairs={{0,16},{1,17},{2,18},{3,19},{4,20},{5,21},{6,22},{7,23},{8,24},{9,... | collective-permute-start | bytes 4718600 | tf_op jit(solution)/shard_map/ppermute | solution.py:44
  319.4 96.9 %collective-permute-start.11 = (bf16[2,256,768]{2,1,0:T(8,128)(2,1)}, bf16[2,256,768]{2,1,0:T(8,128)(2,1)}, u32[]{:S(2)}, u32[]{:S(2)}) collective-permute-start(bf16[2,256,768]{2,1,0:T(8,128)(2,1)} %maximum_select_fusion.1), channel_id=1, source_target_pairs={{0,16},{1,17},{2,18},{3,19},{4,20},{5,21},{6,22},{7,23},{8,24},{9,... | collective-permute-start | bytes 2359304 | tf_op jit(solution)/shard_map/ppermute | solution.py:44
  411.1 35.0 %collective-permute-start.26 = (bf16[2,768,768]{2,1,0:T(8,128)(2,1)S(1)}, bf16[2,768,768]{2,1,0:T(8,128)(2,1)S(1)}, u32[]{:S(2)}, u32[]{:S(2)}) collective-permute-start(bf16[2,768,768]{2,1,0:T(8,128)(2,1)S(1)} %fusion.18), channel_id=1, source_target_pairs={{3,1},{7,5},{11,9},{15,13},{17,19},{21,23},{25,27},{29,31}} | collective-permute-start | bytes 7077896 | tf_op jit(solution)/shard_map/ppermute | solution.py:44
  422.1 48.6 %collective-permute-start.6 = (bf16[1024,768]{1,0:T(8,128)(2,1)S(1)}, bf16[1024,768]{1,0:T(8,128)(2,1)S(1)}, u32[]{:S(2)}, u32[]{:S(2)}) collective-permute-start(bf16[1024,768]{1,0:T(8,128)(2,1)S(1)} %add_convert_fusion.1), channel_id=1, source_target_pairs={{1,0},{3,2},{5,4},{7,6},{9,8},{11,10},{13,12},{15,14},{17,16},{19,... | collective-permute-start | bytes 4718600 | tf_op jit(solution)/shard_map/ppermute | solution.py:44
  423.6 42.4 %collective-permute-start.1 = (bf16[256,768]{1,0:T(8,128)(2,1)S(1)}, bf16[256,768]{1,0:T(8,128)(2,1)S(1)}, u32[]{:S(2)}, u32[]{:S(2)}) collective-permute-start(bf16[256,768]{1,0:T(8,128)(2,1)S(1)} %get-tuple-element.195), channel_id=1, source_target_pairs={{0,0},{1,16},{2,1},{3,17},{4,4},{5,20},{6,5},{7,21},{8,8},{9,24},{... | collective-permute-start | bytes 1179656 | tf_op jit(solution)/shard_map/ppermute | solution.py:44
  425.6 40.4 %collective-permute-start.2 = (bf16[256,768]{1,0:T(8,128)(2,1)S(1)}, bf16[256,768]{1,0:T(8,128)(2,1)S(1)}, u32[]{:S(2)}, u32[]{:S(2)}) collective-permute-start(bf16[256,768]{1,0:T(8,128)(2,1)S(1)} %get-tuple-element.196), channel_id=1, source_target_pairs={{0,1},{1,17},{2,0},{3,16},{4,5},{5,21},{6,4},{7,20},{8,9},{9,25},{... | collective-permute-start | bytes 1179656 | tf_op jit(solution)/shard_map/ppermute | solution.py:44
  466.0 61.6 %collective-permute-start.4 = (bf16[1024,768]{1,0:T(8,128)(2,1)}, bf16[1024,768]{1,0:T(8,128)(2,1)}, u32[]{:S(2)}, u32[]{:S(2)}) collective-permute-start(bf16[1024,768]{1,0:T(8,128)(2,1)} %convolution_convert_fusion), channel_id=1, source_target_pairs={{0,16},{1,17},{2,18},{3,19},{4,20},{5,21},{6,22},{7,23},{8,24},{9,... | collective-permute-start | bytes 4718600 | tf_op jit(solution)/shard_map/ppermute | solution.py:44
  467.2 28.6 %collective-permute-start.28 = (bf16[2,192,768]{2,1,0:T(8,128)(2,1)S(1)}, bf16[2,192,768]{2,1,0:T(8,128)(2,1)S(1)}, u32[]{:S(2)}, u32[]{:S(2)}) collective-permute-start(bf16[2,192,768]{2,1,0:T(8,128)(2,1)S(1)} %add_convert_fusion.11), channel_id=1, source_target_pairs={{1,5},{5,9},{9,13},{13,1},{19,23},{23,27},{27,31},{31,19}} | collective-permute-start | bytes 1769480 | tf_op jit(solution)/shard_map/ppermute | solution.py:44
  479.3 50.6 %collective-permute-start.7 = (bf16[1024,768]{1,0:T(8,128)(2,1)}, bf16[1024,768]{1,0:T(8,128)(2,1)}, u32[]{:S(2)}, u32[]{:S(2)}) collective-permute-start(bf16[1024,768]{1,0:T(8,128)(2,1)} %convolution_convert_fusion.1), channel_id=1, source_target_pairs={{0,16},{1,17},{2,18},{3,19},{4,20},{5,21},{6,22},{7,23},{8,24},{9,... | collective-permute-start | bytes 4718600 | tf_op jit(solution)/shard_map/ppermute | solution.py:44
  492.9 174.4 %collective-permute-start.34 = (bf16[2,768,1536]{2,1,0:T(8,128)(2,1)}, bf16[2,768,1536]{2,1,0:T(8,128)(2,1)}, u32[]{:S(2)}, u32[]{:S(2)}) collective-permute-start(bf16[2,768,1536]{2,1,0:T(8,128)(2,1)} %fusion.8), channel_id=1, source_target_pairs={{2,0},{6,4},{10,8},{14,12},{16,18},{20,22},{24,26},{28,30}} | collective-permute-start | bytes 14155784 | tf_op jit(solution)/shard_map/ppermute | solution.py:44
  513.1 102.5 %collective-permute-start.30 = (bf16[192,384]{1,0:T(8,128)(2,1)}, bf16[192,384]{1,0:T(8,128)(2,1)}, u32[]{:S(2)}, u32[]{:S(2)}) collective-permute-start(bf16[192,384]{1,0:T(8,128)(2,1)} %pad_maximum_fusion.19), channel_id=1, source_target_pairs={{1,1},{5,5},{9,9},{13,13},{19,3},{23,7},{27,11},{31,15}} | collective-permute-start | bytes 442376 | tf_op jit(solution)/shard_map/ppermute | solution.py:44
  524.2 93.8 %collective-permute-start.31 = (bf16[192,384]{1,0:T(8,128)(2,1)}, bf16[192,384]{1,0:T(8,128)(2,1)}, u32[]{:S(2)}, u32[]{:S(2)}) collective-permute-start(bf16[192,384]{1,0:T(8,128)(2,1)} %pad_maximum_fusion.20), channel_id=1, source_target_pairs={{1,0},{5,4},{9,8},{13,12},{19,2},{23,6},{27,10},{31,14}} | collective-permute-start | bytes 442376 | tf_op jit(solution)/shard_map/ppermute | solution.py:44
  527.5 99.2 %collective-permute-start.42 = (bf16[2,192,1536]{2,1,0:T(8,128)(2,1)}, bf16[2,192,1536]{2,1,0:T(8,128)(2,1)}, u32[]{:S(2)}, u32[]{:S(2)}) collective-permute-start(bf16[2,192,1536]{2,1,0:T(8,128)(2,1)} %add_convert_fusion.5), channel_id=1, source_target_pairs={{1,5},{5,9},{9,13},{13,1},{19,23},{23,27},{27,31},{31,19}} | collective-permute-start | bytes 3538952 | tf_op jit(solution)/shard_map/ppermute | solution.py:44
  623.3 35.3 %collective-permute-start.20 = (bf16[2,768,768]{2,1,0:T(8,128)(2,1)}, bf16[2,768,768]{2,1,0:T(8,128)(2,1)}, u32[]{:S(2)}, u32[]{:S(2)}) collective-permute-start(bf16[2,768,768]{2,1,0:T(8,128)(2,1)} %fusion.17), channel_id=1, source_target_pairs={{3,1},{7,5},{11,9},{15,13},{17,19},{21,23},{25,27},{29,31}} | collective-permute-start | bytes 7077896 | tf_op jit(solution)/shard_map/ppermute | solution.py:44
  630.2 107.5 %collective-permute-start.43 = (bf16[2,192,1536]{2,1,0:T(8,128)(2,1)}, bf16[2,192,1536]{2,1,0:T(8,128)(2,1)S(1)}, u32[]{:S(2)}, u32[]{:S(2)}) collective-permute-start(bf16[2,192,1536]{2,1,0:T(8,128)(2,1)} %add_convert_fusion.4), channel_id=1, source_target_pairs={{1,5},{5,9},{9,13},{13,1},{19,23},{23,27},{27,31},{31,19}} | collective-permute-start | bytes 3538952 | tf_op jit(solution)/shard_map/ppermute | solution.py:44
  638.8 114.8 %collective-permute-start.12 = (bf16[256,768]{1,0:T(8,128)(2,1)}, bf16[256,768]{1,0:T(8,128)(2,1)}, u32[]{:S(2)}, u32[]{:S(2)}) collective-permute-start(bf16[256,768]{1,0:T(8,128)(2,1)} %get-tuple-element.187), channel_id=1, source_target_pairs={{0,0},{1,16},{2,1},{3,17},{4,4},{5,20},{6,5},{7,21},{8,8},{9,24},{... | collective-permute-start | bytes 1179656 | tf_op jit(solution)/shard_map/ppermute | solution.py:44
  675.0 58.8 %collective-permute-start.35 = (bf16[2,192,1536]{2,1,0:T(8,128)(2,1)S(1)}, bf16[2,192,1536]{2,1,0:T(8,128)(2,1)S(1)}, u32[]{:S(2)}, u32[]{:S(2)}) collective-permute-start(bf16[2,192,1536]{2,1,0:T(8,128)(2,1)S(1)} %dynamic-slice_convert_fusion.1), channel_id=1, source_target_pairs={{0,4},{4,8},{8,12},{12,0},{18,22},{22,26},{26,30},{30,18}} | collective-permute-start | bytes 3538952 | tf_op jit(solution)/shard_map/ppermute | solution.py:44
  678.0 52.0 %collective-permute-start.16 = (bf16[2,192,768]{2,1,0:T(8,128)(2,1)}, bf16[2,192,768]{2,1,0:T(8,128)(2,1)}, u32[]{:S(2)}, u32[]{:S(2)}) collective-permute-start(bf16[2,192,768]{2,1,0:T(8,128)(2,1)} %add_convert_fusion.17), channel_id=1, source_target_pairs={{0,4},{4,8},{8,12},{12,0},{18,22},{22,26},{26,30},{30,18}} | collective-permute-start | bytes 1769480 | tf_op jit(solution)/shard_map/ppermute | solution.py:44
  681.7 49.9 %collective-permute-start.22 = (bf16[2,192,768]{2,1,0:T(8,128)(2,1)}, bf16[2,192,768]{2,1,0:T(8,128)(2,1)}, u32[]{:S(2)}, u32[]{:S(2)}) collective-permute-start(bf16[2,192,768]{2,1,0:T(8,128)(2,1)} %add_convert_fusion.14), channel_id=1, source_target_pairs={{1,5},{5,9},{9,13},{13,1},{19,23},{23,27},{27,31},{31,19}} | collective-permute-start | bytes 1769480 | tf_op jit(solution)/shard_map/ppermute | solution.py:44
  767.3 27.8 %collective-permute-start.39 = (bf16[192,1536]{1,0:T(8,128)(2,1)S(1)}, bf16[192,1536]{1,0:T(8,128)(2,1)S(1)}, u32[]{:S(2)}, u32[]{:S(2)}) collective-permute-start(bf16[192,1536]{1,0:T(8,128)(2,1)S(1)} %get-tuple-element.156), channel_id=1, source_target_pairs={{0,1},{4,5},{8,9},{12,13},{18,3},{22,7},{26,11},{30,15}} | collective-permute-start | bytes 1769480 | tf_op jit(solution)/shard_map/ppermute | solution.py:44
  (179 other events, 1241.1 us)

commit v3 on v2

--- a/solution.py
+++ b/solution.py
@@ -233,7 +233,7 @@
 
 def forward_kernel(
     planes, self_in, crs_in, up_in, dn_in, x_in, cot_in, gain_in, bias_self, bias_cross,
-    w_att, w_crs, w_up, w_dn, cot, first, p_self, o_self, lse_self, mid, second, act, slope, late, third,
+    w_att, w_crs, w_up, w_dn, x_out, cot, first, p_self, o_self, lse_self, mid, second, act, slope, late, third,
     memory, p_cross, o_cross, lse_cross, gains_out,
     x_v, att_v, crs_v, up_v, dn_v, first_v, p_v, o_v, lse_v, mid_v, second_v, act_v, slope_v, late_v, memory_v,
     send_v, recv_v, gain_v, kx, qx, vt,
@@ -409,6 +409,7 @@
 
     each(tiles, enter)
     put(first_v, first)
+    put(x_v, x_out)
     relay("att", 2)
     relay("att", 3)
 
@@ -638,7 +639,8 @@
     packed, outs, square = (2, slot, 640), (2, slot, 256), (slot, width)
     out_shape = (
         [shape(s, LOW) for s in weights]
-        + [shape(square, LOW), shape(square, LOW), shape(packed, LOW), shape(outs, LOW), shape((8, slot), WIDE)]
+        + [shape(square, LOW)] * 3
+        + [shape(packed, LOW), shape(outs, LOW), shape((8, slot), WIDE)]
         + [shape(square, WIDE), shape(square, LOW), shape((2, slot, hidden), LOW), shape((2, slot, hidden), LOW)]
         + [shape(square, WIDE), shape(square, LOW), shape(square, LOW)]
         + [shape(packed, LOW), shape(outs, LOW), shape((8, slot), WIDE), shape((8, width), WIDE)]
@@ -673,6 +675,717 @@
     )(*args)
 
 
+BUFFER = (0, 1, 0, 1, 0)
+SUMS = ("ffn", "crs", "att")
+
+
+def split_three(value):
+    high = value.astype(LOW).astype(WIDE)
+    middle = (value - high).astype(LOW).astype(WIDE)
+    return high, middle, value - high - middle
+
+
+def attend_back_block(h, p, o, d_o, d_p, lse, lse_row, bias, kx, qx, vx, gx, kt_v, causal):
+    count = p.shape[0]
+    qt, kt, vtile, ot, qlo, vlo = head_place(h)
+    lane = lanes((count, TILE))
+    in_q = both(lane >= qlo, lane < qlo + HEAD)
+    in_v = both(lane >= vlo, lane < vlo + HEAD)
+    sq, sv = HEAD - qlo, HEAD - vlo
+    keys = jnp.where(
+        in_q, p[:, strip(kt, TILE)].astype(WIDE), jnp.where(both(lane > sq, lane < sq + 4), 1.0, 0.0)
+    )
+    keys = jnp.where(lane == sq, bias[...].astype(WIDE), keys)
+    kx[...] = keys.astype(LOW)
+    kt_v[...] = keys.T.astype(LOW)
+    vx[...] = jnp.where(
+        in_v, p[:, strip(vtile, TILE)].astype(WIDE), jnp.where(both(lane >= sv, lane < sv + 3), 1.0, 0.0)
+    ).astype(LOW)
+    own = jnp.sum(jnp.where(subs((8, count)) == lse_row, lse[...], 0.0), axis=0, keepdims=True)
+    a, b, c = split_three(-jnp.broadcast_to(own, (TILE, count)).T)
+    extra = jnp.where(
+        lane == sq,
+        1.0,
+        jnp.where(lane == sq + 1, a, jnp.where(lane == sq + 2, b, jnp.where(lane == sq + 3, c, 0.0))),
+    )
+    qx[...] = jnp.where(in_q, p[:, strip(qt, TILE)].astype(WIDE) * SCORE_SCALE, extra).astype(LOW)
+    grad = jnp.where(in_v, d_o[:, strip(ot, TILE)].astype(WIDE), 0.0)
+    inner = jnp.sum(grad * o[:, strip(ot, TILE)].astype(WIDE), axis=-1, keepdims=True)
+    a, b, c = split_three(-inner)
+    gx[...] = (
+        grad + jnp.where(lane == sv, a, jnp.where(lane == sv + 1, b, jnp.where(lane == sv + 2, c, 0.0)))
+    ).astype(LOW)
+    scores = mm_nt(kx[...], qx[...])
+    if causal:
+        scores = jnp.where(subs(scores.shape) <= lanes(scores.shape), scores, NEG_FILL)
+    probs = jnp.exp(scores)
+    d_scores = (probs * mm_nt(vx[...], gx[...])).astype(LOW)
+    d_v = mm(probs.astype(LOW), gx[...])
+    d_k = mm(d_scores, qx[...])
+    d_q = mm(kt_v[...], d_scores).T * SCORE_SCALE
+
+    def place(tile_index, inside, value):
+        cut = strip(tile_index, TILE)
+        d_p[:, cut] = jnp.where(inside, value, d_p[:, cut].astype(WIDE)).astype(LOW)
+
+    place(qt, in_q, d_q)
+    place(kt, in_q, d_k)
+    place(vtile, in_v, d_v)
+
+
+def backward_kernel(
+    planes, w_att, w_crs, w_up, w_dn, x_rows, cot, first, p_self, o_self, lse_self, mid, second, act, slope, late,
+    third, memory, p_cross, o_cross, lse_cross, gains, bias_self, bias_cross,
+    block_out, grad_out, home_ffn, home_crs, home_att, gain_out, act_keep, y3_keep, grad_keep,
+    dw_ffn, dw_crs, dw_att, yb_ffn, yb_crs, yb_att, zb_ffn, zb_crs, zb_att,
+    att_v, crs_v, up_v, dn_v, a_v, b_v, o_v, do_v, base_v, dres_v, cot_v, grad_v, stage_v, ta, tb, tc,
+    send_v, recv_v, kx, qx, vx, gx, kt_v, lse_v, gain_v, gain_buf, out_st, dw_st, sum_st,
+    load_sem, put_sem, ex_got, ex_sent, dm_got, dm_sent, df_got, df_sent, y_got, y_sent, z_got, z_sent,
+    home_got, home_sent, blk_got, blk_sent, gr_got, gr_sent, gain_got, gain_sent, sum_sem, dw_sem,
+):
+    at = Place(planes)
+    c, z, t, y, r = at.c, at.z, at.t, at.y, at.r
+    slot = cot_v.shape[0]
+    rows = slot // 4
+    tiles = slot // BLOCK
+    depth = home_ffn.shape[0]
+    at.meet()
+    relay = at.relays
+    other = jnp.logical_not(relay)
+    dw = {"ffn": dw_ffn, "crs": dw_crs, "att": dw_att}
+    yb = {"ffn": yb_ffn, "crs": yb_crs, "att": yb_att}
+    zb = {"ffn": zb_ffn, "crs": zb_crs, "att": zb_att}
+    home = {"ffn": home_ffn, "crs": home_crs, "att": home_att}
+    loads = {}
+
+    def load(name, source, goal):
+        index = loads.setdefault(name, len(loads))
+        return pltpu.make_async_copy(source, goal, load_sem.at[index])
+
+    def exchange(e, i):
+        q = strip(i, BLOCK)
+        k = BUFFER[e]
+        return push(send_v.at[k, q, :], recv_v.at[k, q, :], ex_sent.at[e, i], ex_got.at[e, i], at.twin)
+
+    def joined(e, i):
+        q = strip(i, BLOCK)
+        exchange(e, i).wait_recv()
+        return send_v[BUFFER[e], q, :].astype(WIDE) + recv_v[BUFFER[e], q, :].astype(WIDE)
+
+    def ours(i):
+        return lax.div(i, 2) == c
+
+    def norm_grad(values, gain, grad, gain_row, counted):
+        normal, scale = center(values)
+        scaled = grad * gain
+        one = jnp.mean(scaled, axis=-1, keepdims=True)
+        two = jnp.mean(scaled * normal, axis=-1, keepdims=True)
+        total = jnp.sum(grad * normal, axis=0, keepdims=True)
+        gain_v[gain_row : gain_row + 1, :] += jnp.where(counted, total, 0.0)
+        return (scaled - one - normal * two) * scale
+
+    def row_home(k, source, goal, sent, got):
+        dev = (r, z, 2 * c + k)
+        stays = both(both(c == r, y == c), r == k)
+        return stays, source, goal.at[y], sent.at[k], got.at[y], dev
+
+    def go_home(k, source, goal, sent, got):
+        stays, source, goal, sent, got, dev = row_home(k, source, goal, sent, got)
+
+        @pl.when(stays)
+        def _():
+            pltpu.make_async_copy(source, goal, got).start()
+
+        @pl.when(jnp.logical_not(stays))
+        def _():
+            push(source, goal, sent, got, dev).start()
+
+    def went_home(k, source, goal, sent, got):
+        stays, source, goal, sent, got, dev = row_home(k, source, goal, sent, got)
+
+        @pl.when(jnp.logical_not(stays))
+        def _():
+            push(source, goal, sent, got, dev).wait_send()
+
+    def home_block(k, held):
+        return held.at[strip(2 * c + k, rows), :]
+
+    def block_of(k):
+        return lax.rem(z - 1 - k + 2 * planes, planes)
+
+    def y_hop(g, k):
+        i = SUMS.index(g)
+        return push(dw[g].at[k], yb[g].at[k], y_sent.at[i, k], y_got.at[i, k], at.across)
+
+    def z_hop(g, k):
+        i = SUMS.index(g)
+        return push(dw[g].at[k], zb[g].at[k], z_sent.at[i, k], z_got.at[i, k], at.above)
+
+    def emit(g, compute):
+        columns = dw[g].shape[3]
+
+        def put(k, s):
+            return pltpu.make_async_copy(dw_st.at[s, :, :, 0:columns], dw[g].at[k], dw_sem.at[s])
+
+        def run(k):
+            s = lax.rem(k, 2)
+            j = block_of(k)
+            compute(s, pl.ds(pl.multiple_of(j * depth, depth), depth))
+            put(k, s).start()
+
+            @pl.when(k >= 1)
+            def _():
+                put(k - 1, 1 - s).wait()
+                pl.when(other)(lambda: y_hop(g, k - 1).start())
+
+        each(planes, run)
+        put(planes - 1, (planes - 1) % 2).wait()
+        pl.when(other)(lambda: y_hop(g, planes - 1).start())
+
+    def homes(g):
+        columns = dw[g].shape[3]
+        source = dw[g].at[planes - 1]
+        result = []
+        for b in range(2):
+            if g == "crs":
+                for section in range(2):
+                    cut = pl.ds((1 - section) * (columns // 2), columns // 2)
+                    result.append(
+                        (both(c == section, r == b), source.at[b, :, cut], (section, z, 2 * y + b), 2 * b + section)
+                    )
+            else:
+                result.append((both(c == r, r == b), source.at[b], (r, z, 2 * y + b), b))
+        return result
+
+    def sum_step(g, k):
+        i = SUMS.index(g)
+        columns = dw[g].shape[3]
+        members = both(relay, at.decodes) if g == "crs" else relay
+
+        @pl.when(members)
+        def _():
+            y_hop(g, k).wait_recv()
+            parts = [dw[g].at[k], yb[g].at[k]]
+            if k:
+                z_hop(g, k - 1).wait_recv()
+                parts.append(zb[g].at[k - 1])
+            copies = [
+                pltpu.make_async_copy(part, sum_st.at[n, :, :, 0:columns], sum_sem.at[n])
+                for n, part in enumerate(parts)
+            ]
+            for copy in copies:
+                copy.start()
+            for copy in copies:
+                copy.wait()
+            for b in range(2):
+                total = sum_st[0, b, :, 0:columns].astype(WIDE) + sum_st[1, b, :, 0:columns].astype(WIDE)
+                if k:
+                    total = total + sum_st[2, b, :, 0:columns].astype(WIDE)
+                sum_st[0, b, :, 0:columns] = total.astype(LOW)
+            back = pltpu.make_async_copy(sum_st.at[0, :, :, 0:columns], dw[g].at[k], sum_sem.at[0])
+            back.start()
+            back.wait()
+            if k + 1 < planes:
+                z_hop(g, k).start()
+            else:
+                for stays, source, dev, n in homes(g):
+
+                    @pl.when(stays)
+                    def _():
+                        pltpu.make_async_copy(source, home[g], home_got.at[i]).start()
+
+                    @pl.when(jnp.logical_not(stays))
+                    def _():
+                        push(source, home[g], home_sent.at[i, n], home_got.at[i], dev).start()
+
+    def turn(source, goal):
+        def run(i):
+            q = strip(i, BLOCK)
+            goal[:, q] = source[q, :].astype(WIDE).T.astype(LOW)
+
+        each(tiles, run)
+
+    gain_v[...] = jnp.zeros_like(gain_v)
+    g1, g2 = gains[1:2, :], gains[2:3, :]
+
+    early = [
+        load("up", w_up, up_v),
+        load("dn", w_dn, dn_v),
+        load("late", late, base_v),
+        load("att", w_att, att_v),
+    ]
+    for copy in early:
+        copy.start()
+
+    @pl.when(at.decodes)
+    def _():
+        copies = [load("third", third, stage_v), load("cot", cot, cot_v), load("crs", w_crs, crs_v)]
+        for copy in copies:
+            copy.start()
+        for copy in copies[:2]:
+            copy.wait()
+
+    @pl.when(at.encodes)
+    def _():
+        for k in range(2):
+            go_home(k, home_block(k, memory), block_out, blk_sent, blk_got)
+        copies = [load("second", second, stage_v), load("act", act, a_v), load("slope", slope, b_v)]
+        for copy in copies:
+            copy.start()
+        for copy in copies:
+            copy.wait()
+
+    for copy in early[:3]:
+        copy.wait()
+
+    @pl.when(at.decodes)
+    def _():
+        def run(i):
+            q = strip(i, BLOCK)
+            part = None
+            for b in range(2):
+                value, grade = gelu_parts(mm(stage_v[q, :], up_v[b]))
+                a_v[b, q, :] = value.astype(LOW)
+                d_pre = (mm(cot_v[q, :], dn_v[b]) * grade).astype(LOW)
+                b_v[b, q, :] = d_pre
+                term = mm_nt(d_pre, up_v[b])
+                part = term if part is None else part + term
+            send_v[0, q, :] = part.astype(LOW)
+            exchange(0, i).start()
+
+        each(tiles, run)
+        keep = load("keep", a_v, act_keep)
+        keep.start()
+
+    def dm_hop(n):
+        q = pl.ds(pl.multiple_of((2 * c + n) * BLOCK, BLOCK), BLOCK)
+        return push(send_v.at[1, q, :], recv_v.at[1, q, :], dm_sent.at[n], dm_got.at[n], at.beside)
+
+    def df_hop(n, core):
+        q = pl.ds(pl.multiple_of((2 * core + n) * BLOCK, BLOCK), BLOCK)
+        return push(recv_v.at[1, q, :], recv_v.at[1, q, :], df_sent.at[n], df_got.at[n], at.twin)
+
+    @pl.when(at.encodes)
+    def _():
+        def run(n):
+            i = lax.rem(n + 2 * c, 4)
+            q = strip(i, BLOCK)
+
+            @pl.when(n < 2)
+            def _():
+                dm_hop(n).wait_recv()
+                df_hop(n, c).start()
+
+            @pl.when(n >= 2)
+            def _():
+                df_hop(n - 2, 1 - c).wait_recv()
+                df_hop(n - 2, c).wait_send()
+
+            grad = norm_grad(base_v[q, :], g2, recv_v[1, q, :].astype(WIDE), 2, ours(i))
+            dres_v[q, :] = grad
+            low = grad.astype(LOW)
+            cot_v[q, :] = low
+            part = None
+            for b in range(2):
+                d_pre = (mm(low, dn_v[b]) * b_v[b, q, :].astype(WIDE)).astype(LOW)
+                b_v[b, q, :] = d_pre
+                term = mm_nt(d_pre, up_v[b])
+                part = term if part is None else part + term
+            send_v[0, q, :] = part.astype(LOW)
+            exchange(0, i).start()
+
+        each(tiles, run)
+
+    turn(stage_v, ta)
+    turn(cot_v, tb)
+
+    def ffn_block(s, j):
+        for b in range(2):
+            dw_st[s, b, :, 0:768] = mm(ta[j, :], b_v[b]).astype(LOW)
+            dw_st[s, b, :, 768:1536] = mm(tb[j, :], a_v[b]).astype(LOW)
+
+    emit("ffn", ffn_block)
+
+    @pl.when(at.decodes)
+    def _():
+        load("keep", a_v, act_keep).wait()
+        packed = load("p", p_cross, a_v.at[:, :, 0:640])
+        small = [load("o", o_cross, o_v), load("lse", lse_cross, lse_v), load("second", second, stage_v)]
+        packed.start()
+        for copy in small:
+            copy.start()
+
+        def run(i):
+            q = strip(i, BLOCK)
+            grad = cot_v[q, :].astype(WIDE) + norm_grad(base_v[q, :], g2, joined(0, i), 2, ours(i))
+            dres_v[q, :] = grad
+            grad_v[q, :] = grad.astype(LOW)
+
+        each(tiles, run)
+        next_base = load("mid", mid, base_v)
+        next_base.start()
+        load("crs", w_crs, crs_v).wait()
+
+        def spread_out(i):
+            q = strip(i, BLOCK)
+            for b in range(2):
+                do_v[b, q, :] = mm(grad_v[q, :], crs_v[b, :, 128:384]).astype(LOW)
+
+        each(tiles, spread_out)
+        for copy in small:
+            copy.wait()
+        packed.wait()
+        b_v[...] = jnp.zeros_like(b_v)
+
+        def head(n):
+            b = lax.div(n, 3)
+            attend_back_block(
+                lax.rem(n, 3), a_v.at[b], o_v.at[b], do_v.at[b], b_v.at[b], lse_v, n, bias_cross,
+                kx, qx, vx, gx, kt_v, False,
+            )
+
+        each(6, head)
+
+        def to_memory(q):
+            return mm_nt(b_v[0, q, 256:640], crs_v[0, :, 384:768]) + mm_nt(b_v[1, q, 256:640], crs_v[1, :, 384:768])
+
+        def far(n):
+            i = 2 * (1 - c) + n
+            q = strip(i, BLOCK)
+            send_v[1, q, :] = to_memory(q).astype(LOW)
+            exchange(1, i).start()
+
+        each(2, far)
+
+        def near(n):
+            i = 2 * c + n
+            q = strip(i, BLOCK)
+            part = to_memory(q)
+            exchange(1, i).wait_recv()
+            send_v[1, q, :] = (part + recv_v[1, q, :].astype(WIDE)).astype(LOW)
+            dm_hop(n).start()
+
+        each(2, near)
+
+        def to_query(i):
+            q = strip(i, BLOCK)
+            part = mm_nt(b_v[0, q, 0:256], crs_v[0, :, 0:256]) + mm_nt(b_v[1, q, 0:256], crs_v[1, :, 0:256])
+            send_v[0, q, :] = part.astype(LOW)
+            exchange(2, i).start()
+
+        def drained(i):
+            exchange(0, i).wait_send()
+
+        each(tiles, drained)
+        each(tiles, to_query)
+        turn(stage_v, ta)
+        stage_in = load("memory", memory, stage_v)
+        stage_in.start()
+        turn(grad_v, tc)
+        stage_in.wait()
+        turn(stage_v, tb)
+        load("first", first, stage_v).start()
+
+        def crs_block(s, j):
+            for b in range(2):
+                left = mm(ta[j, :], b_v[b, :, 0:256])
+                out = mm(tc[j, :], o_v[b])
+                dw_st[s, b, :, 0:128] = left[:, 0:128].astype(LOW)
+                dw_st[s, b, :, 128:256] = (left[:, 128:256] + out[:, 0:128]).astype(LOW)
+                dw_st[s, b, :, 256:384] = out[:, 128:256].astype(LOW)
+                dw_st[s, b, :, 384:768] = mm(tb[j, :], b_v[b, :, 256:640]).astype(LOW)
+
+        emit("crs", crs_block)
+        next_base.wait()
+
+        def below(i):
+            q = strip(i, BLOCK)
+            grad = dres_v[q, :] + norm_grad(base_v[q, :], g1, joined(2, i), 1, ours(i))
+            dres_v[q, :] = grad
+            grad_v[q, :] = grad.astype(LOW)
+
+        each(tiles, below)
+        load("first", first, stage_v).wait()
+
+    @pl.when(at.encodes)
+    def _():
+        next_base = load("mid", mid, base_v)
+        next_base.start()
+        load("first", first, stage_v).start()
+        next_base.wait()
+
+        def run(i):
+            q = strip(i, BLOCK)
+            grad = dres_v[q, :] + norm_grad(base_v[q, :], g1, joined(0, i), 1, ours(i))
+            dres_v[q, :] = grad
+            grad_v[q, :] = grad.astype(LOW)
+
+        each(tiles, run)
+        load("first", first, stage_v).wait()
+
+    packed = load("p", p_self, a_v.at[:, :, 0:640])
+    small = [load("o", o_self, o_v), load("lse", lse_self, lse_v)]
+    packed.start()
+    for copy in small:
+        copy.start()
+    early[3].wait()
+
+    def spread_self(i):
+        q = strip(i, BLOCK)
+        for b in range(2):
+            do_v[b, q, :] = mm(grad_v[q, :], att_v[b, :, 128:384]).astype(LOW)
+
+    each(tiles, spread_self)
+    b_v[...] = jnp.zeros_like(b_v)
+    for copy in small:
+        copy.wait()
+    packed.wait()
+
+    def self_heads(b, causal):
+        def run(h):
+            attend_back_block(
+                h, a_v.at[b], o_v.at[b], do_v.at[b], b_v.at[b], lse_v, 3 * b + h, bias_self,
+                kx, qx, vx, gx, kt_v, causal,
+            )
+
+        each(3, run)
+
+    for b in range(2):
+        pl.when(at.encodes)(functools.partial(self_heads, b, False))
+        pl.when(at.decodes)(functools.partial(self_heads, b, True))
+        sum_step("ffn", b)
+
+    def to_rows(q):
+        part = None
+        for b in range(2):
+            term = mm_nt(b_v[b, q, 0:256], att_v[b, :, 0:256]) + mm_nt(b_v[b, q, 256:640], att_v[b, :, 384:768])
+            part = term if part is None else part + term
+        return part
+
+    @pl.when(at.decodes)
+    def _():
+        def gone(n):
+            exchange(1, 2 * (1 - c) + n).wait_send()
+            dm_hop(n).wait_send()
+
+        each(2, gone)
+
+    def far_rows(n):
+        i = 2 * (1 - c) + n
+        q = strip(i, BLOCK)
+        send_v[1, q, :] = to_rows(q).astype(LOW)
+        exchange(3, i).start()
+
+    each(2, far_rows)
+    turn(stage_v, ta)
+    x_in = load("x", x_rows, stage_v)
+    x_in.start()
+    turn(grad_v, tc)
+
+    def att_block(s, j):
+        for b in range(2):
+            left = mm(ta[j, :], b_v[b, :, 0:256])
+            out = mm(tc[j, :], o_v[b])
+            dw_st[s, b, :, 0:128] = left[:, 0:128].astype(LOW)
+            dw_st[s, b, :, 128:256] = (left[:, 128:256] + out[:, 0:128]).astype(LOW)
+            dw_st[s, b, :, 256:384] = out[:, 128:256].astype(LOW)
+            dw_st[s, b, :, 384:768] = mm(ta[j, :], b_v[b, :, 256:640]).astype(LOW)
+
+    emit("att", att_block)
+    x_in.wait()
+    gain0 = gains[0:1, :]
+
+    def near_rows(n):
+        i = 2 * c + n
+        q = strip(i, BLOCK)
+        part = to_rows(q)
+        exchange(3, i).wait_recv()
+        grad = part + recv_v[1, q, :].astype(WIDE)
+        value = dres_v[q, :] + norm_grad(stage_v[q, :].astype(WIDE), gain0, grad, 0, True)
+        out_st[strip(n, BLOCK), :] = value.astype(LOW)
+
+    each(2, near_rows)
+    out_put = load("out", out_st, grad_keep)
+    out_put.start()
+    out_put.wait()
+    for k in range(2):
+        go_home(k, grad_keep.at[strip(k, rows), :], grad_out, gr_sent, gr_got)
+
+    def gain_hop(n, source, device):
+        return push(source, gain_buf.at[n], gain_sent.at[n], gain_got.at[n], device)
+
+    gain_buf[0] = gain_v[...]
+    hop = gain_hop(1, gain_buf.at[0], at.twin)
+    hop.start()
+    hop.wait()
+    gain_buf[2] = gain_buf[0] + gain_buf[1]
+    hop = gain_hop(3, gain_buf.at[2], at.across)
+    hop.start()
+    hop.wait()
+    gain_buf[4] = gain_buf[2] + gain_buf[3]
+    source = 4
+    for n in range(planes - 1):
+        hop = gain_hop(5 + n, gain_buf.at[source], at.above)
+        hop.start()
+        hop.wait()
+        source = 5 + n
+    total = None
+    for j in range(planes):
+        held = gain_buf[jnp.where(z == j, 4, 5 + lax.rem(z - 1 - j + planes, planes))]
+        total = held if total is None else total + held
+    last = 4 + planes
+    gain_buf[last] = total
+    hop = gain_hop(last + 1, gain_buf.at[last], at.beside)
+    hop.start()
+    hop.wait()
+    gain_v[...] = jnp.where(r == c, gain_buf[last], gain_buf[last + 1])
+    gains_home = load("gains", gain_v, gain_out)
+    gains_home.start()
+
+    @pl.when(at.decodes)
+    def _():
+        copies = [load("act", act_keep, a_v), load("late", late, base_v)]
+        for copy in copies:
+            copy.start()
+        for copy in copies:
+            copy.wait()
+
+        def free(i):
+            exchange(2, i).wait_send()
+
+        each(tiles, free)
+
+        def to_out(q):
+            return mm_nt(a_v[0, q, :], dn_v[0]) + mm_nt(a_v[1, q, :], dn_v[1])
+
+        def far(n):
+            i = 2 * (1 - c) + n
+            q = strip(i, BLOCK)
+            send_v[0, q, :] = to_out(q).astype(LOW)
+            exchange(4, i).start()
+
+        each(2, far)
+
+        def near(n):
+            i = 2 * c + n
+            q = strip(i, BLOCK)
+            part = to_out(q)
+            exchange(4, i).wait_recv()
+            out_st[strip(n, BLOCK), :] = (base_v[q, :] + part + recv_v[0, q, :].astype(WIDE)).astype(LOW)
+
+        each(2, near)
+        y3_put = load("out", out_st, y3_keep)
+        y3_put.start()
+        y3_put.wait()
+        for k in range(2):
+            go_home(k, y3_keep.at[strip(k, rows), :], block_out, blk_sent, blk_got)
+
+    for k in range(2, planes):
+        sum_step("ffn", k)
+    for k in range(planes):
+        sum_step("crs", k)
+    for k in range(planes):
+        sum_step("att", k)
+
+    gains_home.wait()
+    for s in range(2):
+        for goal, got in ((block_out, blk_got), (grad_out, gr_got)):
+            push(goal.at[s], goal.at[s], blk_sent.at[0], got.at[s], at.twin).wait_recv()
+    for i, g in enumerate(SUMS):
+        push(home[g], home[g], home_sent.at[i, 0], home_got.at[i], at.twin).wait_recv()
+    for k in range(2):
+        went_home(k, grad_keep.at[strip(k, rows), :], grad_out, gr_sent, gr_got)
+
+    @pl.when(at.encodes)
+    def _():
+        for k in range(2):
+            went_home(k, home_block(k, memory), block_out, blk_sent, blk_got)
+
+        def done(i):
+            exchange(0, i).wait_send()
+
+        each(tiles, done)
+
+    @pl.when(at.decodes)
+    def _():
+        for k in range(2):
+            went_home(k, y3_keep.at[strip(k, rows), :], block_out, blk_sent, blk_got)
+
+        def done(n):
+            exchange(4, 2 * (1 - c) + n).wait_send()
+
+        each(2, done)
+
+    def done_rows(n):
+        exchange(3, 2 * (1 - c) + n).wait_send()
+
+    each(2, done_rows)
+    for g in SUMS:
+        there = at.decodes if g == "crs" else jnp.logical_or(at.decodes, at.encodes)
+
+        @pl.when(both(other, there))
+        def _():
+            for k in range(planes):
+                y_hop(g, k).wait_send()
+
+        @pl.when(both(relay, there))
+        def _():
+            for k in range(planes - 1):
+                z_hop(g, k).wait_send()
+            for stays, source, dev, n in homes(g):
+
+                @pl.when(jnp.logical_not(stays))
+                def _():
+                    i = SUMS.index(g)
+                    push(source, home[g], home_sent.at[i, n], home_got.at[i], dev).wait_send()
+
+
+def backward_call(planes, slot, width, hidden, depth, args):
+    shape = jax.ShapeDtypeStruct
+    rows = slot // 4
+    square = (slot, width)
+    wides = {"ffn": 2 * hidden, "crs": width, "att": width}
+    out_shape = (
+        [shape((2, rows, width), LOW)] * 2
+        + [shape((depth, 2 * hidden), LOW), shape((depth, width // 2), LOW), shape((depth, width), LOW)]
+        + [shape((8, width), WIDE), shape((2, slot, hidden), LOW)]
+        + [shape((2 * rows, width), LOW)] * 2
+        + [shape((planes, 2, depth, wides[g]), LOW) for g in SUMS] * 3
+    )
+    dma = pltpu.SemaphoreType.DMA
+    v = pltpu.VMEM
+    scratch = (
+        [v((2, width, width), LOW)] * 2
+        + [v((2, width, hidden), LOW)] * 2
+        + [v((2, slot, hidden), LOW)] * 2
+        + [v((2, slot, 256), LOW)] * 2
+        + [v(square, WIDE)] * 2
+        + [v(square, LOW)] * 3
+        + [v((width, slot), LOW)] * 3
+        + [v((2,) + square, LOW)] * 2
+        + [v((slot, TILE), LOW)] * 4
+        + [v((TILE, slot), LOW), v((8, slot), WIDE), v((8, width), WIDE), v((planes + 6, 8, width), WIDE)]
+        + [v((2 * rows, width), LOW), v((2, 2, depth, 2 * hidden), LOW), v((3, 2, depth, 2 * hidden), LOW)]
+        + [dma((24,)), dma((1,)), dma((5, 4)), dma((5, 4))]
+        + [dma((2,))] * 4
+        + [dma((3, planes))] * 4
+        + [dma((3,)), dma((3, 4))]
+        + [dma((2,))] * 4
+        + [dma((planes + 6,))] * 2
+        + [dma((3,)), dma((2,))]
+    )
+    any_spec = pl.BlockSpec(memory_space=pl.ANY)
+    vmem_spec = pl.BlockSpec(memory_space=pltpu.VMEM)
+    return pl.pallas_call(
+        functools.partial(backward_kernel, planes),
+        out_shape=out_shape,
+        in_specs=[any_spec] * 20 + [vmem_spec] * 3,
+        out_specs=[any_spec] * len(out_shape),
+        scratch_shapes=scratch,
+        compiler_params=pltpu.CompilerParams(collective_id=1, has_side_effects=True, vmem_limit_bytes=VMEM_BYTES),
+    )(*args)
+
+
 def ring_gather(lay, shard):
     planes = lay.planes
     rows = shard.shape[1]
@@ -963,178 +1676,42 @@
 
     positions = jnp.arange(slot)
     own_length = jnp.where(lay.is_decoder, lengths[1, item], lengths[0, item])
-    self_allowed = (positions[None, :] < own_length) & (
-        (positions[None, :] <= positions[:, None]) | jnp.logical_not(lay.is_decoder)
-    )
-    cross_allowed = jnp.broadcast_to(
-        ((positions < lengths[0, item]) & (task_mask[item] == 1))[None], (slot, slot)
-    )
 
     def key_bias(allowed):
         return jnp.broadcast_to(jnp.where(allowed, 0.0, NEG_FILL)[:, None], (slot, TILE)).astype(LOW)
 
-    (
-        w_att, w_crs, w_up_all, w_dn_all, cotangent, normed0, p_self, o_self, lse_self, x_mid, normed1, act, slope,
-        x_late, normed2, memory, p_cross, o_cross, lse_cross, gains,
-    ) = forward_call(
+    biases = (
+        key_bias(positions < own_length),
+        key_bias((positions < lengths[0, item]) & (task_mask[item] == 1)),
+    )
+    kept = forward_call(
         lay.planes,
         slot,
         width,
         hidden,
-        (
-            self_block,
-            cross_block,
-            w_up[0],
-            w_down[0].T,
-            block_input[0],
-            out_grad,
-            gain_block,
-            key_bias(positions < own_length),
-            key_bias((positions < lengths[0, item]) & (task_mask[item] == 1)),
-        ),
-    )
-
-    def joined(partial):
-        low = partial.astype(LOW)
-        return low.astype(WIDE) + lay.other_core(low).astype(WIDE)
-
-    part = lambda w, name: jnp.concatenate([unpack_heads(w[0], name), unpack_heads(w[1], name)], axis=1)
-    att = {n: part(w_att, n) for n in "qkvo"}
-    crs = {n: part(w_crs, n) for n in "qkvo"}
-    up = jnp.concatenate([w_up_all[0], w_up_all[1]], axis=1)
-    down_t = jnp.concatenate([w_dn_all[0], w_dn_all[1]], axis=1)
-    pick = lambda p, cuts: jnp.concatenate([p[b][:, i : i + HEAD] for b in range(2) for i in cuts], axis=1)
-    q, k, v = pick(p_self, (0, 64, 128)), pick(p_self, (256, 320, 512)), pick(p_self, (384, 448, 576))
-    cq, ck, cv = pick(p_cross, (0, 64, 128)), pick(p_cross, (256, 320, 512)), pick(p_cross, (384, 448, 576))
-    out_self, out_cross = pick(o_self, (128, 192, 64)), pick(o_cross, (128, 192, 64))
-    lse_self, lse_cross = lse_self[:6, :, None], lse_cross[:6, :, None]
-    act_enc, slope_enc = (jnp.concatenate([v_[0], v_[1]], axis=1) for v_ in (act, slope))
-    x_late_enc = x_late
-    memory_enc = memory
-    def spread(value, first):
-        pick = value[jnp.where(first, lay.chip % 2, 1 - lay.chip % 2)]
-        flip = 0 if first else 1
-        return lay.route(pick, lambda c, z, t: (t // 2, z, 2 * ((t % 2) ^ flip) + c))
-
-    def merge_rows(mine, theirs):
-        low_half = jnp.where(lay.core == 0, mine, theirs)
-        high_half = jnp.where(lay.core == 0, theirs, mine)
-        return jnp.concatenate([low_half[0], low_half[1], high_half[0], high_half[1]], axis=0)
-
-    first = spread(block_input[0], True)
-    second = spread(block_input[0], False)
-    mine = jnp.where(item == 0, jnp.stack([first, second]), jnp.stack([second, first]))
-    x_rows = merge_rows(mine, lay.other_core(mine)).astype(WIDE)
-
-    pre_dec = mm(normed2, up)
-    act_dec, slope_dec = gelu_parts(pre_dec)
-    act_dec = act_dec.astype(LOW)
-    result_dec = (x_late + joined(mm_nt(act_dec, down_t))).astype(LOW)
-
-    d_out = cotangent.astype(WIDE)
-    d_pre = (slope_dec * mm(cotangent, down_t)).astype(LOW)
-    d_ffn_dec = jnp.concatenate([mm_tn(normed2, d_pre), mm_tn(cotangent, act_dec)], axis=1)
-    d_late_norm, d_gain2_dec = norm_back(x_late, gains[2], joined(mm_nt(d_pre, up)))
-    d_late = d_out + d_late_norm
-    grad_late = d_late.astype(LOW)
-    d_att = mm(grad_late, crs["o"]).astype(LOW)
-    d_cq, d_ck, d_cv = attend_back(cq, ck, cv, lse_cross, d_att, cross_allowed)
-    d_memory = joined(mm_nt(d_ck, crs["k"]) + mm_nt(d_cv, crs["v"]))
-    d_crs = {
-        "q": mm_tn(normed1, d_cq),
-        "k": mm_tn(memory, d_ck),
-        "v": mm_tn(memory, d_cv),
-        "o": mm_tn(grad_late, out_cross),
-    }
-    d_mid_norm, d_gain1_dec = norm_back(x_mid, gains[1], joined(mm_nt(d_cq, crs["q"])))
-    d_mid_dec = d_late + d_mid_norm
-
-    d_memory = lay.route(d_memory.astype(LOW), lambda c, z, t: (c, z, t ^ 1) if t % 2 == 1 else None).astype(WIDE)
-    d_late_enc, d_gain2_enc = norm_back(x_late_enc, gains[2], d_memory)
-    grad_late_enc = d_late_enc.astype(LOW)
-    d_pre = (slope_enc * mm(grad_late_enc, down_t)).astype(LOW)
-    d_ffn_enc = jnp.concatenate([mm_tn(normed1, d_pre), mm_tn(grad_late_enc, act_enc)], axis=1)
-    d_mid_norm, d_gain1_enc = norm_back(x_mid, gains[1], joined(mm_nt(d_pre, up)))
-    d_mid_enc = d_late_enc + d_mid_norm
-
-    d_mid = jnp.where(lay.is_decoder, d_mid_dec, d_mid_enc)
-    grad_mid = d_mid.astype(LOW)
-    d_att = mm(grad_mid, att["o"]).astype(LOW)
-    d_q, d_k, d_v = attend_back(q, k, v, lse_self, d_att, self_allowed)
-    d_norm = joined(mm_nt(d_q, att["q"]) + mm_nt(d_k, att["k"]) + mm_nt(d_v, att["v"]))
-    d_att_w = {
-        "q": mm_tn(normed0, d_q),
-        "k": mm_tn(normed0, d_k),
-        "v": mm_tn(normed0, d_v),
-        "o": mm_tn(grad_mid, out_self),
-    }
-    d_first, d_gain0 = norm_back(x_rows, gains[0], d_norm)
-    d_rows = d_mid + d_first
-
-    half = 3 * HEAD
-
-    def flip(v):
-        return jnp.where(lay.role == 0, v, v[::-1])
-
-    def blocks(parts):
-        return flip(jnp.stack(
-            [pack_heads({n: parts[n][:, half * b : half * (b + 1)] for n in parts}) for b in range(2)]
-        ))
-
-    def feed_blocks(both):
-        total = both.shape[1] // 2
-        return flip(jnp.stack(
-            [
-                jnp.concatenate(
-                    [both[:, hidden * b : hidden * (b + 1)], both[:, total + hidden * b : total + hidden * (b + 1)]],
-                    axis=1,
-                )
-                for b in range(2)
-            ]
-        ))
-
-    self_total = blocks(d_att_w)
-    home_self = hand_back(lay, ring_scatter(lay, self_total, 0), 0, 0) + hand_back(
-        lay, ring_scatter(lay, self_total, 1), 1, 1
-    )
-    home_feed = hand_back(lay, ring_scatter(lay, feed_blocks(d_ffn_enc), 0), 0, 0) + hand_back(
-        lay, ring_scatter(lay, feed_blocks(d_ffn_dec), 1), 1, 1
-    )
-    cross_total = ring_scatter(lay, blocks(d_crs), 1)
-    side = lambda names: jnp.stack(
-        [jnp.concatenate([unpack_heads(cross_total[b], n) for n in names], axis=1) for b in range(2)]
-    )
-    home_cross = hand_back(lay, side("kv"), 1, 0) + hand_back(lay, side("qo"), 1, 1)
-
+        (self_block, cross_block, w_up[0], w_down[0].T, block_input[0], out_grad, gain_block) + biases,
+    )
+    block_output, input_grad, home_feed, home_cross, home_self, gain_total = backward_call(
+        lay.planes, slot, width, hidden, depth, tuple(kept) + biases
+    )[:6]
+    home_self, home_feed, home_cross = (v.astype(WIDE) for v in (home_self, home_feed, home_cross))
     g_self = jnp.stack([unpack_heads(home_self, n) for n in "qkv"], axis=1)[None]
     g_self_out = unpack_heads(home_self, "o").T[None]
-    g_cross = home_cross.reshape(1, depth, 2, wide)
+    halves = (ORDER[:6], ORDER[6:])
+    take = lambda order, name: jnp.concatenate(
+        [home_cross[:, HEAD * order.index((name, h)) : HEAD * (order.index((name, h)) + 1)] for h in range(3)], axis=1
+    )
+    g_cross = jnp.where(
+        sec == 1,
+        jnp.stack([take(halves[0], "q"), take(halves[0], "o")], axis=1),
+        jnp.stack([take(halves[1], "k"), take(halves[1], "v")], axis=1),
+    )[None]
     g_up = home_feed[:, :hidden][None]
     g_down = home_feed[:, hidden:].T[None]
-
-    gain2 = jnp.where(lay.is_decoder, d_gain2_dec, d_gain2_enc)
-    gain1 = jnp.where(lay.is_decoder, d_gain1_dec, d_gain1_enc)
-    gain_rows = jnp.stack([d_gain0, gain1, gain2])
-    slots = jnp.stack(
-        [
-            jnp.where((lay.role == r) & (lay.core == 0), gain_rows, 0.0)
-            for r in range(2)
-        ]
-    )
-    gain_total = lax.psum(slots, AXES)[sec][None]
-
-    def rows_home(value):
-        mine = lax.dynamic_slice_in_dim(value, lay.core * 2 * rows, 2 * rows, 0).reshape(2, rows, width)
-        a = lay.route(mine[item], lambda c, z, t: (t % 2, z, 2 * c + t // 2))
-        b = lay.route(mine[1 - item], lambda c, z, t: (t % 2, z, 2 * c + 1 - t // 2))
-        even = lay.chip % 2 == 0
-        return jnp.where(even, jnp.stack([a, b]), jnp.stack([b, a]))[None]
-
-    block_output = rows_home(jnp.where(lay.is_decoder, result_dec, memory_enc))
-    input_grad = rows_home(d_rows.astype(LOW)).astype(WIDE)
+    gain_total = gain_total[None]
     return (
-        block_output,
-        input_grad,
+        block_output[None],
+        input_grad.astype(WIDE)[None],
         g_self,
         g_self_out,
         g_cross,

time: 810 us -> 487 us (0.60)
  the two profiles are of different devices: /device:TPU:2 before, /device:TPU:1 now
where the time goes in v3:
time: 487 us; the launch traced here: 478 us
  Pallas kernels  454 us (93%)
  local copies, waits for them, and re-layouts  14.9 us (3%)
  other arithmetic  6.9 us (1%)
    pallas_call x1, Pallas kernels, backward_call(): pl.pallas_call(functools.partial(backward_kernel, planes), out_shape=out_...  335 us
    pallas_call x1, Pallas kernels, forward_call(): pl.pallas_call(functools.partial(forward_kernel, planes), out_shape=out_s...  118 us

profile of v3, /device:TPU:1, one launch (start us, length us, event | category | flops | bytes accessed | tf_op | source)
XLA Modules:
  0.0 478.1 jit_solution(18263094353328846293)
XLA Ops:
  0.7 0.8 compare_reduce_fusion
  1.5 1.3 constant_dynamic-slice_fusion
  4.1 0.7 select_convert_fusion
  4.8 1.3 pad_convert_fusion.gain_in
  6.1 1.0 copy.19
  7.1 0.9 broadcast_in_dim.50.bias_self
  8.0 0.9 broadcast_in_dim.51.bias_cross
  8.9 1.0 slice_bitcast_fusion.4
  10.0 0.8 concatenate.58.self_in
  10.8 0.3 fusion.3
  11.2 0.8 maximum_select_fusion.1.crs_in
  12.0 118.4 %shard_map.169 = (bf16[2,768,768]{2,1,0:T(8,128)(2,1)}, bf16[2,768,768]{2,1,0:T(8,128)(2,1)}, bf16[2,768,768]{2,1,0:T(8,128)(2,1)}, bf16[2,768,768]{2,1,0:T(8,12...) custom-call(bf16[192,768]{1,0:T(8,128)(2,1)} %concatenate.58.self_in, ...), custom_call_target="tpu_custom_call" | custom-call | tf_op jit(solution)/shard_map/pallas_call | solution.py:668
  130.3 335.3 %shard_map.170 = (bf16[2,256,768]{2,1,0:T(8,128)(2,1)}, bf16[2,256,768]{2,1,0:T(8,128)(2,1)}, bf16[192,1536]{1,0:T(8,128)(2,1)}, bf16[192,384]{1,0:T(8,128)(2,1)...) custom-call(bf16[2,768,768]{2,1,0:T(8,128)(2,1)} %get-tuple-element., ...), custom_call_target="tpu_custom_call" | custom-call | tf_op jit(solution)/shard_map/pallas_call | solution.py:1379
  465.7 1.4 slice_bitcast_fusion.7
  467.0 1.3 slice.200
  468.4 0.9 convert_element_type.24
  469.3 1.0 fusion.2
  470.3 0.9 fusion.1
  471.2 0.8 copy.22
  472.2 0.9 maximum_bitcast_fusion
  473.3 1.1 copy.23
  474.5 1.1 slice_bitcast_fusion
  475.6 1.3 bitcast_convert_fusion
  476.8 0.9 copy.29
  (37 shorter events, 0.6 us)
Async XLA Ops:
  0.6 10.2 %copy-start.3 = (bf16[1,192,2,192]{3,2,1,0:T(2,128)(2,1)S(1)}, bf16[1,192,2,192]{3,2,1,0:T(2,128)(2,1)}, u32[]{:S(2)}) copy-start(bf16[1,192,2,192]{3,2,1,0:T(2,128)(2,1)} %param.13) | copy-start | bytes 442372
  465.6 6.4 %copy-start.1 = (bf16[192,768]{1,0:T(8,128)(2,1)S(1)}, bf16[192,768]{1,0:T(8,128)(2,1)}, u32[]{:S(2)}) copy-start(bf16[192,768]{1,0:T(8,128)(2,1)} %get-tuple-element.59) | copy-start | bytes 884740
  470.3 2.7 copy-start
  473.0 1.3 copy-start.5
  473.3 2.3 copy-start.4
  474.5 2.4 copy-start.2

commit v4 on v1

--- a/solution.py
+++ b/solution.py
@@ -1,6 +1,10 @@
+import functools
+
 import jax
 import jax.numpy as jnp
 from jax import lax
+from jax.experimental import pallas as pl
+from jax.experimental.pallas import tpu as pltpu
 from jax.sharding import PartitionSpec as P
 
 HEAD = 64
@@ -62,7 +66,7 @@
     return (scaled - first - normal * second) * scale, jnp.sum(grad * normal, axis=0)
 
 
-ORDER = (("q", 0), ("q", 1), ("k", 0), ("k", 1), ("v", 0), ("v", 1), ("q", 2), ("v", 2), ("k", 2), ("o", 2), ("o", 0), ("o", 1))
+ORDER = (("q", 0), ("q", 1), ("q", 2), ("o", 2), ("o", 0), ("o", 1), ("k", 0), ("k", 1), ("v", 0), ("v", 1), ("k", 2), ("v", 2))
 
 
 def pack_heads(parts):
@@ -125,9 +129,1242 @@
     return 0.5 * value * (1.0 + soft), slope
 
 
+MESH = pl.DeviceIdType.MESH
+GROUPS = ("att", "crs", "up", "dn")
+BLOCK = 256
+VMEM_BYTES = 62 * 2**20
+
+
+def lanes(shape):
+    return lax.broadcasted_iota(jnp.int32, shape, len(shape) - 1)
+
+
+def subs(shape):
+    return lax.broadcasted_iota(jnp.int32, shape, 0)
+
+
+def strip(i, size):
+    return pl.ds(pl.multiple_of(i * size, size), size)
+
+
+def head_place(h):
+    two = (h == 2).astype(jnp.int32)
+    one = (h >= 1).astype(jnp.int32)
+    return two, 2 + 2 * two, 3 + two, 1 - two, HEAD * (one - two), HEAD * one
+
+
+def each(count, step, name=None):
+    def run(i, carry):
+        step(i)
+        return carry
+
+    with jax.named_scope(name or step.__name__):
+        lax.fori_loop(0, count, run, 0)
+
+
+class Place:
+    def __init__(self, planes):
+        self.planes = planes
+        self.c = lax.axis_index("section")
+        self.z = lax.axis_index("dp")
+        self.t = lax.axis_index("tensor")
+        self.y = lax.div(self.t, 2)
+        self.r = lax.rem(self.t, 2)
+        self.twin = (1 - self.c, self.z, self.t)
+        self.above = (self.c, lax.rem(self.z + 1, planes), self.t)
+        self.below = (self.c, lax.rem(self.z + planes - 1, planes), self.t)
+        self.across = (self.c, self.z, lax.rem(self.t + 2, 4))
+        self.beside = (self.c, self.z, self.t + 1 - 2 * self.r)
+        self.relays = self.c == self.y
+        self.encodes = self.r == 0
+        self.decodes = self.r == 1
+
+    def meet(self):
+        barrier = pltpu.get_barrier_semaphore()
+        peers = [self.above, self.below]
+        for dc in range(2):
+            for dt in range(4):
+                if dc or dt:
+                    peers.append((lax.rem(self.c + dc, 2), self.z, lax.rem(self.t + dt, 4)))
+        for peer in peers:
+            pl.semaphore_signal(barrier, inc=1, device_id=peer, device_id_type=MESH)
+        pl.semaphore_wait(barrier, len(peers))
+
+
+def push(source, goal, sent, got, device):
+    return pltpu.make_async_remote_copy(
+        src_ref=source, dst_ref=goal, send_sem=sent, recv_sem=got, device_id=device, device_id_type=MESH
+    )
+
+
+def both(first, second):
+    return jnp.logical_and(first, second)
+
+
+def center(values):
+    middle = values - jnp.mean(values, axis=-1, keepdims=True)
+    scale = lax.rsqrt(jnp.mean(middle * middle, axis=-1, keepdims=True) + EPSILON)
+    return middle * scale, scale
+
+
+def attend_block(h, p, o, lse, lse_row, bias, kx, qx, vt, causal):
+    count = p.shape[0]
+    qt, kt, vtile, ot, qlo, vlo = head_place(h)
+    lane = lanes((count, TILE))
+    in_q = both(lane >= qlo, lane < qlo + HEAD)
+    in_v = both(lane >= vlo, lane < vlo + HEAD)
+    spare = HEAD - qlo
+    kx[...] = jnp.where(lane == spare, bias[...], jnp.where(in_q, p[:, strip(kt, TILE)], jnp.zeros((), LOW)))
+    vt[...] = jnp.where(in_v, p[:, strip(vtile, TILE)].astype(WIDE), 1.0).T.astype(LOW)
+    qx[...] = jnp.where(
+        in_q, p[:, strip(qt, TILE)].astype(WIDE) * SCORE_SCALE, jnp.where(lane == spare, 1.0, 0.0)
+    ).astype(LOW)
+    scores = mm_nt(kx[...], qx[...])
+    if causal:
+        scores = jnp.where(subs(scores.shape) <= lanes(scores.shape), scores, NEG_FILL)
+    top = jnp.max(scores, axis=0, keepdims=True)
+    power = jnp.exp(scores - top).astype(LOW)
+    out = mm(vt[...], power)
+    total = jnp.where(vlo == 0, out[HEAD : HEAD + 1, :], out[0:1, :])
+    result = (out / total).T
+    o[:, strip(ot, TILE)] = jnp.where(in_v, result, o[:, strip(ot, TILE)].astype(WIDE)).astype(LOW)
+    row = subs((8, count))
+    lse[...] = jnp.where(row == lse_row, top + jnp.log(total), lse[...])
+
+
+SUMS = ("ffn", "crs", "att")
+DIRECT = ("att", "up")
+
+
+def split_three(value):
+    high = value.astype(LOW).astype(WIDE)
+    middle = (value - high).astype(LOW).astype(WIDE)
+    return high, middle, value - high - middle
+
+
+def attend_back_block(h, p, o, d_o, d_p, lse, lse_row, bias, kx, qx, vx, gx, kt_v, causal):
+    count = p.shape[0]
+    qt, kt, vtile, ot, qlo, vlo = head_place(h)
+    lane = lanes((count, TILE))
+    in_q = both(lane >= qlo, lane < qlo + HEAD)
+    in_v = both(lane >= vlo, lane < vlo + HEAD)
+    sq, sv = HEAD - qlo, HEAD - vlo
+    keys = jnp.where(
+        in_q, p[:, strip(kt, TILE)].astype(WIDE), jnp.where(both(lane > sq, lane < sq + 4), 1.0, 0.0)
+    )
+    keys = jnp.where(lane == sq, bias[...].astype(WIDE), keys)
+    kx[...] = keys.astype(LOW)
+    kt_v[...] = keys.T.astype(LOW)
+    vx[...] = jnp.where(
+        in_v, p[:, strip(vtile, TILE)].astype(WIDE), jnp.where(both(lane >= sv, lane < sv + 3), 1.0, 0.0)
+    ).astype(LOW)
+    own = jnp.sum(jnp.where(subs((8, count)) == lse_row, lse[...], 0.0), axis=0, keepdims=True)
+    a, b, c = split_three(-jnp.broadcast_to(own, (TILE, count)).T)
+    extra = jnp.where(
+        lane == sq,
+        1.0,
+        jnp.where(lane == sq + 1, a, jnp.where(lane == sq + 2, b, jnp.where(lane == sq + 3, c, 0.0))),
+    )
+    qx[...] = jnp.where(in_q, p[:, strip(qt, TILE)].astype(WIDE) * SCORE_SCALE, extra).astype(LOW)
+    grad = jnp.where(in_v, d_o[:, strip(ot, TILE)].astype(WIDE), 0.0)
+    inner = jnp.sum(grad * o[:, strip(ot, TILE)].astype(WIDE), axis=-1, keepdims=True)
+    a, b, c = split_three(-inner)
+    gx[...] = (
+        grad + jnp.where(lane == sv, a, jnp.where(lane == sv + 1, b, jnp.where(lane == sv + 2, c, 0.0)))
+    ).astype(LOW)
+    scores = mm_nt(kx[...], qx[...])
+    if causal:
+        scores = jnp.where(subs(scores.shape) <= lanes(scores.shape), scores, NEG_FILL)
+    probs = jnp.exp(scores)
+    d_scores = (probs * mm_nt(vx[...], gx[...])).astype(LOW)
+    d_v = mm(probs.astype(LOW), gx[...])
+    d_k = mm(d_scores, qx[...])
+    d_q = mm(kt_v[...], d_scores).T * SCORE_SCALE
+
+    def place(tile_index, inside, value):
+        cut = strip(tile_index, TILE)
+        d_p[:, cut] = jnp.where(inside, value, d_p[:, cut].astype(WIDE)).astype(LOW)
+
+    place(qt, in_q, d_q)
+    place(kt, in_q, d_k)
+    place(vtile, in_v, d_v)
+
+
+def block_kernel(
+    planes, self_in, crs_in, up_in, dn_in, x_in, cot_in, gain_in, bias_self, bias_cross,
+    block_out, grad_out, home_ffn, home_crs, home_att, gain_out,
+    cot, first_k, x_k, second_k, late_k, memory_k, p_k, o_k, lse_k, pc_k, oc_k, lsec_k, act_k, grad_k, y3_k,
+    dw_ffn, dw_crs, dw_att, yb_ffn, yb_crs, yb_att, zb_ffn, zb_crs, zb_att,
+    att_v, crs_v, up_v, dn_v, a_v, b_v, o_v, do_v, mid_v, late_v, s_v, g_v, c_v, ta, tb, tc,
+    send_v, recv_v, kx, qx, vx, gx, kt_v, lse_v, gain_v, gain_in_v, gain_buf, out_st, dw_st, sum_st,
+    x_sem, x_sent, y0_sent, c_sem, zw_got, zw_sent, yw_got, yw_sent,
+    row_got, row_sent, fwd_sem, cot_got, gain_sem, copy_sem, ex_got, ex_sent, mem_got, mem_sent, mf_got, mf_sent,
+    dm_got, dm_sent, df_got, df_sent, y_got, y_sent, z_got, z_sent, home_got, home_sent,
+    blk_got, blk_sent, gr_got, gr_sent, gr_hop_got, gr_hop_sent, sum_sem, dw_sem,
+):
+    at = Place(planes)
+    c, z, t, y, r = at.c, at.z, at.t, at.y, at.r
+    rows = x_in.shape[1]
+    slot = s_v.shape[0]
+    tiles = slot // BLOCK
+    depth = up_in.shape[0]
+    side = crs_in.shape[1]
+    relay = at.relays
+    other = jnp.logical_not(relay)
+    vmem = {"att": att_v, "crs": crs_v, "up": up_v, "dn": dn_v}
+    shard = {"att": self_in, "up": up_in, "dn": dn_in}
+    here = pl.ds(pl.multiple_of(z * depth, depth), depth)
+    dw = {"ffn": dw_ffn, "crs": dw_crs, "att": dw_att}
+    yb = {"ffn": yb_ffn, "crs": yb_crs, "att": yb_att}
+    zb = {"ffn": zb_ffn, "crs": zb_crs, "att": zb_att}
+    home = {"ffn": home_ffn, "crs": home_crs, "att": home_att}
+    names = {}
+
+    def copying(name, source, goal):
+        index = names.setdefault(name, len(names))
+        return pltpu.make_async_copy(source, goal, copy_sem.at[index])
+
+    def half_of(core):
+        return pl.ds(pl.multiple_of(core * 2 * rows, 2 * rows), 2 * rows)
+
+    at.meet()
+
+    relay_dev = (y, z, 2 * y + c)
+    over_dev = (y, z, 2 * (1 - y) + c)
+    stays = both(c == y, r == c)
+
+    def launch(g):
+        i = GROUPS.index(g)
+        goal = vmem[g].at[r, here, :]
+
+        @pl.when(stays)
+        def _():
+            pltpu.make_async_copy(shard[g], goal, x_sem.at[i, r]).start()
+
+        @pl.when(jnp.logical_not(stays))
+        def _():
+            push(shard[g], goal, x_sent.at[i], x_sem.at[i, r], relay_dev).start()
+
+    def launch_over(g):
+        i = GROUPS.index(g)
+        return push(shard[g], vmem[g].at[r, here, :], y0_sent.at[i], yw_got.at[i, 0, r], over_dev)
+
+    crs_dev = (y, z, 2 * y + 1)
+    crs_stays = both(c == y, r == 1)
+
+    def crs_goal(block, section):
+        return crs_v.at[block, here, pl.ds(pl.multiple_of((1 - section) * side, side), side)]
+
+    def launch_crs():
+        @pl.when(crs_stays)
+        def _():
+            pltpu.make_async_copy(crs_in, crs_goal(r, c), c_sem.at[r, c]).start()
+
+        @pl.when(jnp.logical_not(crs_stays))
+        def _():
+            push(crs_in, crs_goal(r, c), x_sent.at[1], c_sem.at[r, c], crs_dev).start()
+
+    row_goal = s_v.at[strip(t, rows), :]
+    cot_goal = cot.at[strip(t, rows), :]
+
+    def row_stays(s):
+        return both(both(c == y, r == c), y == s)
+
+    def launch_rows(s):
+        dev = (y, z, 2 * s + c)
+
+        @pl.when(row_stays(s))
+        def _():
+            pltpu.make_async_copy(x_in.at[s], row_goal, row_got.at[r]).start()
+
+        @pl.when(jnp.logical_not(row_stays(s)))
+        def _():
+            push(x_in.at[s], row_goal, row_sent.at[s], row_got.at[r], dev).start()
+
+    def launch_cot():
+        dev = (y, z, 2 * c + 1)
+
+        @pl.when(crs_stays)
+        def _():
+            pltpu.make_async_copy(cot_in.at[c], cot_goal, cot_got.at[r]).start()
+
+        @pl.when(jnp.logical_not(crs_stays))
+        def _():
+            push(cot_in.at[c], cot_goal, row_sent.at[2], cot_got.at[r], dev).start()
+
+    gain_copy = push(gain_in, gain_in_v.at[c], gain_sem.at[0], gain_sem.at[1], at.twin)
+    gain_copy.start()
+    launch("att")
+    launch_over("att").start()
+    launch_rows(0)
+    launch_rows(1)
+    launch("up")
+    launch_over("up").start()
+    launch_crs()
+    launch("dn")
+    launch_cot()
+
+    def piece(g, k, b):
+        j = lax.rem(z - k + planes, planes)
+        return vmem[g].at[b, pl.ds(pl.multiple_of(j * depth, depth), depth), :]
+
+    def ring(g, k, b):
+        i = GROUPS.index(g)
+        return push(
+            piece(g, k - 1, b), piece(g, k - 1, b), zw_sent.at[i, k - 1, b], zw_got.at[i, k - 1, b], at.above
+        )
+
+    def ring_in(g, k, b):
+        i = GROUPS.index(g)
+        return push(piece(g, k, b), piece(g, k, b), zw_sent.at[i, k - 1, b], zw_got.at[i, k - 1, b], at.above)
+
+    def cross_over(g, k, b):
+        i = GROUPS.index(g)
+        return push(piece(g, k, b), piece(g, k, b), yw_sent.at[i, k, b], yw_got.at[i, k, b], at.across)
+
+    def arrive(g, k, b):
+        if k:
+            ring_in(g, k, b).wait_recv()
+        elif g == "crs":
+            for section in range(2):
+                goal = crs_goal(b, section)
+                push(goal, goal, x_sent.at[1], c_sem.at[b, section], at.twin).wait_recv()
+        else:
+            i = GROUPS.index(g)
+            goal = vmem[g].at[b, here, :]
+            push(goal, goal, x_sent.at[i], x_sem.at[i, b], at.twin).wait_recv()
+
+    def passing(g, k, up=True, over=True):
+        def run():
+            for b in range(2):
+                if up:
+                    arrive(g, k, b)
+                    if k + 1 < planes:
+                        ring(g, k + 1, b).start()
+                if over and not (k == 0 and g in DIRECT):
+                    cross_over(g, k, b).start()
+
+        return run
+
+    def schedule(order):
+        events = []
+        for n, g in enumerate(order):
+            for k in range(planes):
+                if k == 0 and n == 0:
+                    events.append(passing(g, 0))
+                elif k:
+                    events.append(passing(g, k))
+                if n + 1 < len(order):
+                    if k == planes - 2:
+                        events[-1] = chained(events[-1], passing(order[n + 1], 0, True, False))
+                    if k == planes - 1:
+                        events[-1] = chained(events[-1], passing(order[n + 1], 0, False, True))
+        return events
+
+    def chained(one, two):
+        def run():
+            one()
+            two()
+
+        return run
+
+    enc_events = schedule(("att", "up", "dn"))
+    dec_events = schedule(("att", "crs", "up", "dn"))
+
+    def pump_enc(count):
+        for _ in range(min(count, len(enc_events))):
+            pl.when(both(relay, at.encodes))(enc_events.pop(0))
+
+    def pump_dec(count):
+        for _ in range(min(count, len(dec_events))):
+            pl.when(both(relay, at.decodes))(dec_events.pop(0))
+
+    def pump(count):
+        pump_enc(count)
+        pump_dec(count)
+
+    def settle(g):
+        listens = both(other, at.decodes) if g == "crs" else other
+
+        @pl.when(listens)
+        def _():
+            for k in range(planes):
+                for b in range(2):
+                    cross_over(g, k, b).wait_recv()
+
+    def exchange(e, i):
+        q = strip(i, BLOCK)
+        k = e % 2
+        return push(send_v.at[k, q, :], recv_v.at[k, q, :], ex_sent.at[e, i], ex_got.at[e, i], at.twin)
+
+    def joined(e, i):
+        q = strip(i, BLOCK)
+        exchange(e, i).wait_recv()
+        return send_v[e % 2, q, :].astype(WIDE) + recv_v[e % 2, q, :].astype(WIDE)
+
+    def sent(e):
+        each(tiles, lambda i: exchange(e, i).wait_send())
+
+    pump(1)
+    for k in range(2):
+        goal = s_v.at[strip(2 * c + k, rows), :]
+        push(goal, goal, row_sent.at[0], row_got.at[k], at.twin).wait_recv()
+    half, far_half = half_of(c), half_of(1 - c)
+    rows_on = push(s_v.at[half, :], s_v.at[half, :], fwd_sem.at[0], fwd_sem.at[1], at.twin)
+    rows_on.start()
+    pump(1)
+    push(gain_in, gain_in_v.at[1 - c], gain_sem.at[0], gain_sem.at[1], at.twin).wait_recv()
+    gain_here = pltpu.make_async_copy(gain_in, gain_in_v.at[c], gain_sem.at[2])
+    gain_here.start()
+    gain_here.wait()
+    gains = gain_in_v.at[r]
+    g0, g1, g2 = gains[0:1, :], gains[1:2, :], gains[2:3, :]
+    gain_v[...] = jnp.zeros_like(gain_v)
+    push(s_v.at[far_half, :], s_v.at[far_half, :], fwd_sem.at[0], fwd_sem.at[1], at.twin).wait_recv()
+    x_put = copying("x", s_v, x_k)
+    x_put.start()
+
+    def enter(i):
+        q = strip(i, BLOCK)
+        c_v[q, :] = (center(s_v[q, :].astype(WIDE))[0] * g0).astype(LOW)
+
+    each(tiles, enter)
+    first_put = copying("first", c_v, first_k)
+    first_put.start()
+    pump(2)
+    settle("att")
+
+    def project(source, weights, part):
+        def project_rows(i):
+            q = strip(i, BLOCK)
+            for b in range(2):
+                if part != "kv":
+                    a_v[b, q, 0:256] = mm(source[q, :], weights[b, :, 0:256]).astype(LOW)
+                if part != "q":
+                    a_v[b, q, 256:640] = mm(source[q, :], weights[b, :, 384:768]).astype(LOW)
+
+        each(tiles, project_rows)
+
+    packed_v = a_v.at[:, :, 0:640]
+    project(c_v, att_v, "all")
+    p_put = copying("p", packed_v, p_k)
+    p_put.start()
+    o_v[...] = jnp.zeros_like(o_v)
+    lse_v[...] = jnp.zeros_like(lse_v)
+    pump(1)
+
+    def attend_heads(bias, causal, hooks):
+        def head_forward(n):
+            b = lax.div(n, 3)
+            attend_block(lax.rem(n, 3), a_v.at[b], o_v.at[b], lse_v, n, bias, kx, qx, kt_v, causal)
+            for when, event in hooks:
+                pl.when(both(n == when, relay))(event)
+
+        each(6, head_forward)
+
+    enc_hooks = [(2, enc_events.pop(0)), (5, enc_events.pop(0))]
+    dec_hooks = [(2, dec_events.pop(0)), (5, dec_events.pop(0))]
+    pl.when(at.encodes)(lambda: attend_heads(bias_self, False, enc_hooks))
+    pl.when(at.decodes)(lambda: attend_heads(bias_self, True, dec_hooks))
+    o_put, lse_put = copying("o", o_v, o_k), copying("lse", lse_v, lse_k)
+    o_put.start()
+    lse_put.start()
+
+    def out_project(e, weights):
+        def out_rows(i):
+            q = strip(i, BLOCK)
+            part = mm_nt(o_v[0, q, :], weights[0, :, 128:384]) + mm_nt(o_v[1, q, :], weights[1, :, 128:384])
+            send_v[e % 2, q, :] = part.astype(LOW)
+            exchange(e, i).start()
+
+        each(tiles, out_rows)
+
+    out_project(0, att_v)
+    pump(1)
+    x_put.wait()
+    rows_on.wait_send()
+
+    def middle(i):
+        q = strip(i, BLOCK)
+        value = s_v[q, :].astype(WIDE) + joined(0, i)
+        mid_v[q, :] = value
+        s_v[q, :] = (center(value)[0] * g1).astype(LOW)
+
+    each(tiles, middle)
+    first_put.wait()
+    p_put.wait()
+    o_put.wait()
+    lse_put.wait()
+
+    def mem_send(i):
+        q = pl.ds(pl.multiple_of((2 * c + i) * BLOCK, BLOCK), BLOCK)
+        return push(g_v.at[q, :], g_v.at[q, :], mem_sent.at[i], mem_got.at[i], at.beside)
+
+    def mem_forward(i, core):
+        q = pl.ds(pl.multiple_of((2 * core + i) * BLOCK, BLOCK), BLOCK)
+        return push(g_v.at[q, :], g_v.at[q, :], mf_sent.at[i], mf_got.at[i], at.twin)
+
+    def row_home(k, source, goal, sent_by, got):
+        dev = (r, z, 2 * c + k)
+        keeps = both(both(c == r, y == c), r == k)
+        return keeps, source, goal.at[y], sent_by.at[k], got.at[y], dev
+
+    def go_home(*spec):
+        keeps, source, goal, sent_by, got, dev = row_home(*spec)
+
+        @pl.when(keeps)
+        def _():
+            pltpu.make_async_copy(source, goal, got).start()
+
+        @pl.when(jnp.logical_not(keeps))
+        def _():
+            push(source, goal, sent_by, got, dev).start()
+
+    def went_home(*spec):
+        keeps, source, goal, sent_by, got, dev = row_home(*spec)
+
+        @pl.when(jnp.logical_not(keeps))
+        def _():
+            push(source, goal, sent_by, got, dev).wait_send()
+
+    def memory_home(k):
+        return k, memory_k.at[strip(2 * c + k, rows), :], block_out, blk_sent, blk_got
+
+    settle_up = lambda: settle("up")
+    pl.when(at.encodes)(settle_up)
+
+    @pl.when(at.encodes)
+    def _():
+        def up_rows(i):
+            q = strip(i, BLOCK)
+            for b in range(2):
+                value, grade = gelu_parts(mm(s_v[q, :], up_v[b]))
+                a_v[b, q, :] = value.astype(LOW)
+                b_v[b, q, :] = grade.astype(LOW)
+
+        each(tiles, up_rows)
+
+    pump_enc(9)
+
+    @pl.when(at.encodes)
+    def _():
+        settle("dn")
+
+        def down_rows(i):
+            q = strip(i, BLOCK)
+            part = mm_nt(a_v[0, q, :], dn_v[0]) + mm_nt(a_v[1, q, :], dn_v[1])
+            send_v[1, q, :] = part.astype(LOW)
+            exchange(1, i).start()
+
+        each(tiles, down_rows)
+
+        def finish(n):
+            i = lax.rem(n + 2 * c, 4)
+            q = strip(i, BLOCK)
+            value = mid_v[q, :] + joined(1, i)
+            late_v[q, :] = value
+            g_v[q, :] = (center(value)[0] * g2).astype(LOW)
+
+            @pl.when(n < 2)
+            def _():
+                mem_send(n).start()
+
+        each(tiles, finish)
+        keep = copying("memory", g_v, memory_k)
+        keep.start()
+        keep.wait()
+        for k in range(2):
+            go_home(*memory_home(k))
+        sent(0)
+
+    def norm_grad(values, gain, grad, gain_row, counted):
+        normal, scale = center(values)
+        scaled = grad * gain
+        one = jnp.mean(scaled, axis=-1, keepdims=True)
+        two = jnp.mean(scaled * normal, axis=-1, keepdims=True)
+        total = jnp.sum(grad * normal, axis=0, keepdims=True)
+        gain_v[gain_row : gain_row + 1, :] += jnp.where(counted, total, 0.0)
+        return (scaled - one - normal * two) * scale
+
+    def ours(i):
+        return lax.div(i, 2) == c
+
+    @pl.when(at.decodes)
+    def _():
+        second_put = copying("second", s_v, second_k)
+        second_put.start()
+        for k in range(2):
+            goal = cot.at[strip(2 * c + k, rows), :]
+            push(goal, goal, row_sent.at[2], cot_got.at[k], at.twin).wait_recv()
+        cot_on = push(cot.at[half, :], cot.at[half, :], fwd_sem.at[2], fwd_sem.at[3], at.twin)
+        cot_on.start()
+        for _ in range(len(dec_events) - 3):
+            pl.when(relay)(dec_events.pop(0))
+        settle("crs")
+        project(s_v, crs_v, "q")
+        for _ in range(len(dec_events)):
+            pl.when(relay)(dec_events.pop(0))
+        push(cot.at[far_half, :], cot.at[far_half, :], fwd_sem.at[2], fwd_sem.at[3], at.twin).wait_recv()
+        cot_in_v = copying("cot", cot, c_v)
+        cot_in_v.start()
+        o_v[...] = jnp.zeros_like(o_v)
+        lse_v[...] = jnp.zeros_like(lse_v)
+        for i in range(2):
+            mem_send(i).wait_recv()
+            mem_forward(i, c).start()
+        for i in range(2):
+            mem_forward(i, 1 - c).wait_recv()
+        project(g_v, crs_v, "kv")
+        puts = [copying("pc", packed_v, pc_k), copying("memory", g_v, memory_k)]
+        for copy in puts:
+            copy.start()
+        attend_heads(bias_cross, False, [])
+        puts += [copying("oc", o_v, oc_k), copying("lsec", lse_v, lsec_k)]
+        for copy in puts[2:]:
+            copy.start()
+        out_project(1, crs_v)
+        second_put.wait()
+
+        def finish(i):
+            q = strip(i, BLOCK)
+            value = mid_v[q, :] + joined(1, i)
+            late_v[q, :] = value
+            s_v[q, :] = (center(value)[0] * g2).astype(LOW)
+
+        each(tiles, finish)
+        late_put = copying("late", late_v, late_k)
+        late_put.start()
+        settle("up")
+        settle("dn")
+        cot_in_v.wait()
+        sent(0)
+        for copy in puts:
+            copy.wait()
+
+        def feed_rows(i):
+            q = strip(i, BLOCK)
+            part = None
+            for b in range(2):
+                value, grade = gelu_parts(mm(s_v[q, :], up_v[b]))
+                a_v[b, q, :] = value.astype(LOW)
+                d_pre = (mm(c_v[q, :], dn_v[b]) * grade).astype(LOW)
+                b_v[b, q, :] = d_pre
+                term = mm_nt(d_pre, up_v[b])
+                part = term if part is None else part + term
+            send_v[0, q, :] = part.astype(LOW)
+            exchange(2, i).start()
+
+        each(tiles, feed_rows)
+        copying("act", a_v, act_k).start()
+        late_put.wait()
+        cot_on.wait_send()
+        each(2, lambda i: mem_forward(i, c).wait_send())
+
+    def block_of(k):
+        return lax.rem(z - 1 - k + 2 * planes, planes)
+
+    def y_hop(g, k):
+        i = SUMS.index(g)
+        return push(dw[g].at[k], yb[g].at[k], y_sent.at[i, k], y_got.at[i, k], at.across)
+
+    def z_hop(g, k):
+        i = SUMS.index(g)
+        return push(dw[g].at[k], zb[g].at[k], z_sent.at[i, k], z_got.at[i, k], at.above)
+
+    def emit(g, compute):
+        columns = dw[g].shape[3]
+
+        def put(k, s):
+            return pltpu.make_async_copy(dw_st.at[s, :, :, 0:columns], dw[g].at[k], dw_sem.at[s])
+
+        def run(k):
+            s = lax.rem(k, 2)
+            j = block_of(k)
+            compute(s, pl.ds(pl.multiple_of(j * depth, depth), depth))
+            put(k, s).start()
+
+            @pl.when(k >= 1)
+            def _():
+                put(k - 1, 1 - s).wait()
+                pl.when(other)(lambda: y_hop(g, k - 1).start())
+
+        each(planes, run, "emit_" + g)
+        put(planes - 1, (planes - 1) % 2).wait()
+        pl.when(other)(lambda: y_hop(g, planes - 1).start())
+
+    def homes(g):
+        columns = dw[g].shape[3]
+        source = dw[g].at[planes - 1]
+        result = []
+        for b in range(2):
+            if g == "crs":
+                for section in range(2):
+                    cut = pl.ds((1 - section) * (columns // 2), columns // 2)
+                    result.append(
+                        (both(c == section, r == b), source.at[b, :, cut], (section, z, 2 * y + b), 2 * b + section)
+                    )
+            else:
+                result.append((both(c == r, r == b), source.at[b], (r, z, 2 * y + b), b))
+        return result
+
+    def summing(g, k):
+        i = SUMS.index(g)
+        columns = dw[g].shape[3]
+
+        def run():
+            y_hop(g, k).wait_recv()
+            parts = [dw[g].at[k], yb[g].at[k]]
+            if k:
+                z_hop(g, k - 1).wait_recv()
+                parts.append(zb[g].at[k - 1])
+            copies = [
+                pltpu.make_async_copy(part, sum_st.at[n, :, :, 0:columns], sum_sem.at[n])
+                for n, part in enumerate(parts)
+            ]
+            for copy in copies:
+                copy.start()
+            for copy in copies:
+                copy.wait()
+            for b in range(2):
+                total = sum_st[0, b, :, 0:columns].astype(WIDE) + sum_st[1, b, :, 0:columns].astype(WIDE)
+                if k:
+                    total = total + sum_st[2, b, :, 0:columns].astype(WIDE)
+                sum_st[0, b, :, 0:columns] = total.astype(LOW)
+            back = pltpu.make_async_copy(sum_st.at[0, :, :, 0:columns], dw[g].at[k], sum_sem.at[0])
+            back.start()
+            back.wait()
+            if k + 1 < planes:
+                z_hop(g, k).start()
+            else:
+                for keeps, source, dev, n in homes(g):
+
+                    @pl.when(keeps)
+                    def _():
+                        pltpu.make_async_copy(source, home[g], home_got.at[i]).start()
+
+                    @pl.when(jnp.logical_not(keeps))
+                    def _():
+                        push(source, home[g], home_sent.at[i, n], home_got.at[i], dev).start()
+
+        return run
+
+    enc_sums = [summing(g, k) for g in ("ffn", "att") for k in range(planes)]
+    dec_sums = [summing(g, k) for g in ("ffn", "crs", "att") for k in range(planes)]
+
+    def add_enc(count):
+        for _ in range(min(count, len(enc_sums))):
+            pl.when(both(relay, at.encodes))(enc_sums.pop(0))
+
+    def add_dec(count):
+        for _ in range(min(count, len(dec_sums))):
+            pl.when(both(relay, at.decodes))(dec_sums.pop(0))
+
+    def turn(source, goal):
+        def run(i):
+            q = strip(i, BLOCK)
+            goal[:, q] = source[q, :].astype(WIDE).T.astype(LOW)
+
+        each(tiles, run, "turn")
+
+    def dm_hop(n, source):
+        q = pl.ds(pl.multiple_of((2 * c + n) * BLOCK, BLOCK), BLOCK)
+        return push(source.at[q, :], c_v.at[q, :], dm_sent.at[n], dm_got.at[n], at.beside)
+
+    def df_hop(n, core):
+        q = pl.ds(pl.multiple_of((2 * core + n) * BLOCK, BLOCK), BLOCK)
+        return push(c_v.at[q, :], c_v.at[q, :], df_sent.at[n], df_got.at[n], at.twin)
+
+    @pl.when(at.encodes)
+    def _():
+        def back_rows(m):
+            n = lax.div(m, 2)
+            own = lax.rem(m, 2) == 0
+            i = jnp.where(own, 2 * c + n, 2 * (1 - c) + n)
+            q = strip(i, BLOCK)
+
+            @pl.when(own)
+            def _():
+                dm_hop(n, c_v).wait_recv()
+                df_hop(n, c).start()
+
+            @pl.when(jnp.logical_not(own))
+            def _():
+                df_hop(n, 1 - c).wait_recv()
+
+            grad = norm_grad(late_v[q, :], g2, c_v[q, :].astype(WIDE), 2, ours(i))
+            late_v[q, :] = grad
+            low = grad.astype(LOW)
+            part = None
+            for b in range(2):
+                d_pre = (mm(low, dn_v[b]) * b_v[b, q, :].astype(WIDE)).astype(LOW)
+                b_v[b, q, :] = d_pre
+                term = mm_nt(d_pre, up_v[b])
+                part = term if part is None else part + term
+            send_v[0, q, :] = part.astype(LOW)
+
+            @pl.when(own)
+            def _():
+                df_hop(n, c).wait_send()
+
+            c_v[q, :] = low
+            exchange(2, i).start()
+
+        each(tiles, back_rows)
+
+    turn(s_v, ta)
+    turn(c_v, tb)
+
+    def ffn_block(s, j):
+        for b in range(2):
+            dw_st[s, b, :, 0:768] = mm(ta[j, :], b_v[b]).astype(LOW)
+            dw_st[s, b, :, 768:1536] = mm(tb[j, :], a_v[b]).astype(LOW)
+
+    emit("ffn", ffn_block)
+
+    @pl.when(at.decodes)
+    def _():
+        copying("act", a_v, act_k).wait()
+        packed = copying("pc", pc_k, packed_v)
+        small = [copying("oc", oc_k, o_v), copying("lsec", lsec_k, lse_v), copying("second", second_k, s_v)]
+        packed.start()
+        for copy in small:
+            copy.start()
+
+        def late_rows(i):
+            q = strip(i, BLOCK)
+            grad = c_v[q, :].astype(WIDE) + norm_grad(late_v[q, :], g2, joined(2, i), 2, ours(i))
+            late_v[q, :] = grad
+            g_v[q, :] = grad.astype(LOW)
+
+        each(tiles, late_rows)
+
+        def cross_out(i):
+            q = strip(i, BLOCK)
+            for b in range(2):
+                do_v[b, q, :] = mm(g_v[q, :], crs_v[b, :, 128:384]).astype(LOW)
+
+        each(tiles, cross_out)
+        for copy in small:
+            copy.wait()
+        packed.wait()
+        b_v[...] = jnp.zeros_like(b_v)
+
+        def cross_head(n):
+            b = lax.div(n, 3)
+            attend_back_block(
+                lax.rem(n, 3), a_v.at[b], o_v.at[b], do_v.at[b], b_v.at[b], lse_v, n, bias_cross,
+                kx, qx, vx, gx, kt_v, False,
+            )
+
+        each(6, cross_head)
+        sent(1)
+
+        def to_memory(q):
+            return mm_nt(b_v[0, q, 256:640], crs_v[0, :, 384:768]) + mm_nt(b_v[1, q, 256:640], crs_v[1, :, 384:768])
+
+        def far(n):
+            i = 2 * (1 - c) + n
+            q = strip(i, BLOCK)
+            send_v[1, q, :] = to_memory(q).astype(LOW)
+            exchange(3, i).start()
+
+        each(2, far)
+
+        def near(n):
+            i = 2 * c + n
+            q = strip(i, BLOCK)
+            part = to_memory(q)
+            exchange(3, i).wait_recv()
+            send_v[1, q, :] = (part + recv_v[1, q, :].astype(WIDE)).astype(LOW)
+            dm_hop(n, send_v.at[1]).start()
+
+        each(2, near)
+
+        def to_query(i):
+            q = strip(i, BLOCK)
+            part = mm_nt(b_v[0, q, 0:256], crs_v[0, :, 0:256]) + mm_nt(b_v[1, q, 0:256], crs_v[1, :, 0:256])
+            send_v[0, q, :] = part.astype(LOW)
+            exchange(4, i).start()
+
+        sent(2)
+        each(tiles, to_query)
+        add_dec(1)
+        turn(s_v, ta)
+        stage_in = copying("memory", memory_k, s_v)
+        stage_in.start()
+        turn(g_v, tc)
+        stage_in.wait()
+        turn(s_v, tb)
+        copying("first", first_k, s_v).start()
+
+        def crs_block(s, j):
+            for b in range(2):
+                left = mm(ta[j, :], b_v[b, :, 0:256])
+                out = mm(tc[j, :], o_v[b])
+                dw_st[s, b, :, 0:128] = left[:, 0:128].astype(LOW)
+                dw_st[s, b, :, 128:256] = (left[:, 128:256] + out[:, 0:128]).astype(LOW)
+                dw_st[s, b, :, 256:384] = out[:, 128:256].astype(LOW)
+                dw_st[s, b, :, 384:768] = mm(tb[j, :], b_v[b, :, 256:640]).astype(LOW)
+
+        emit("crs", crs_block)
+        add_dec(1)
+
+        def below(i):
+            q = strip(i, BLOCK)
+            grad = late_v[q, :] + norm_grad(mid_v[q, :], g1, joined(4, i), 1, ours(i))
+            late_v[q, :] = grad
+            g_v[q, :] = grad.astype(LOW)
+
+        each(tiles, below)
+        copying("first", first_k, s_v).wait()
+
+        def gone(n):
+            exchange(3, 2 * (1 - c) + n).wait_send()
+            dm_hop(n, send_v.at[1]).wait_send()
+
+        each(2, gone)
+
+    @pl.when(at.encodes)
+    def _():
+        copying("first", first_k, s_v).start()
+        each(2, lambda i: mem_send(i).wait_send())
+
+        def below(i):
+            q = strip(i, BLOCK)
+            grad = late_v[q, :] + norm_grad(mid_v[q, :], g1, joined(2, i), 1, ours(i))
+            late_v[q, :] = grad
+            g_v[q, :] = grad.astype(LOW)
+
+        each(tiles, below)
+        copying("first", first_k, s_v).wait()
+        sent(1)
+
+    packed = copying("p", p_k, packed_v)
+    small = [copying("o", o_k, o_v), copying("lse", lse_k, lse_v)]
+    packed.start()
+    for copy in small:
+        copy.start()
+
+    def self_out(i):
+        q = strip(i, BLOCK)
+        for b in range(2):
+            do_v[b, q, :] = mm(g_v[q, :], att_v[b, :, 128:384]).astype(LOW)
+
+    each(tiles, self_out)
+    b_v[...] = jnp.zeros_like(b_v)
+    for copy in small:
+        copy.wait()
+    packed.wait()
+
+    def self_heads(causal, hooks):
+        def self_head(n):
+            b = lax.div(n, 3)
+            attend_back_block(
+                lax.rem(n, 3), a_v.at[b], o_v.at[b], do_v.at[b], b_v.at[b], lse_v, n, bias_self,
+                kx, qx, vx, gx, kt_v, causal,
+            )
+            for when, event in hooks:
+                pl.when(both(n == when, relay))(event)
+
+        each(6, self_head)
+
+    enc_back = [(1, enc_sums.pop(0))]
+    dec_back = [(2, dec_sums.pop(0)), (5, dec_sums.pop(0))]
+    pl.when(at.encodes)(lambda: self_heads(False, enc_back))
+    pl.when(at.decodes)(lambda: self_heads(True, dec_back))
+
+    def to_rows(q):
+        part = None
+        for b in range(2):
+            term = mm_nt(b_v[b, q, 0:256], att_v[b, :, 0:256]) + mm_nt(b_v[b, q, 256:640], att_v[b, :, 384:768])
+            part = term if part is None else part + term
+        return part
+
+    def far_rows(n):
+        i = 2 * (1 - c) + n
+        q = strip(i, BLOCK)
+        send_v[1, q, :] = to_rows(q).astype(LOW)
+        exchange(5, i).start()
+
+    each(2, far_rows)
+    turn(s_v, ta)
+    x_in_v = copying("x", x_k, s_v)
+    x_in_v.start()
+    turn(g_v, tc)
+
+    def att_block(s, j):
+        for b in range(2):
+            left = mm(ta[j, :], b_v[b, :, 0:256])
+            out = mm(tc[j, :], o_v[b])
+            dw_st[s, b, :, 0:128] = left[:, 0:128].astype(LOW)
+            dw_st[s, b, :, 128:256] = (left[:, 128:256] + out[:, 0:128]).astype(LOW)
+            dw_st[s, b, :, 256:384] = out[:, 128:256].astype(LOW)
+            dw_st[s, b, :, 384:768] = mm(ta[j, :], b_v[b, :, 256:640]).astype(LOW)
+
+    emit("att", att_block)
+    add_enc(1)
+    x_in_v.wait()
+
+    def near_rows(n):
+        i = 2 * c + n
+        q = strip(i, BLOCK)
+        part = to_rows(q)
+        exchange(5, i).wait_recv()
+        grad = part + recv_v[1, q, :].astype(WIDE)
+        value = late_v[q, :] + norm_grad(s_v[q, :].astype(WIDE), g0, grad, 0, True)
+        out_st[strip(n, BLOCK), :] = value.astype(LOW)
+
+    each(2, near_rows)
+    out_put = copying("out", out_st, grad_k)
+    out_put.start()
+    out_put.wait()
+
+    def grad_home(k):
+        return k, grad_k.at[strip(k, rows), :], grad_out, gr_sent, gr_got
+
+    for k in range(2):
+        go_home(*grad_home(k))
+
+    def gain_hop(n, source, device):
+        return push(source, gain_buf.at[n], gr_hop_sent.at[n], gr_hop_got.at[n], device)
+
+    gain_buf[0] = gain_v[...]
+    twin_hop = gain_hop(1, gain_buf.at[0], at.twin)
+    twin_hop.start()
+    twin_hop.wait()
+    peer_hop = gain_hop(3, gain_buf.at[2], (1 - c, z, lax.rem(t + 2, 4)))
+    last = 4 + planes
+
+    @pl.when(relay)
+    def _():
+        gain_buf[2] = gain_buf[0] + gain_buf[1]
+        peer_hop.start()
+
+    def ring_hop(n):
+        return gain_hop(5 + n, gain_buf.at[4 + n], at.above)
+
+    def gain_step(n):
+        @pl.when(relay)
+        def _():
+            if n == 0:
+                peer_hop.wait()
+                gain_buf[4] = gain_buf[2] + gain_buf[3]
+            else:
+                ring_hop(n - 1).wait()
+            if n < planes - 1:
+                ring_hop(n).start()
+            else:
+                total = None
+                for j in range(planes):
+                    held = gain_buf[jnp.where(z == j, 4, 5 + lax.rem(z - 1 - j + planes, planes))]
+                    total = held if total is None else total + held
+                gain_buf[last] = total
+                for b in range(2):
+                    keeps = both(c == r, r == b)
+
+                    @pl.when(keeps)
+                    def _():
+                        pltpu.make_async_copy(gain_buf.at[last], gain_buf.at[last + 1], gr_hop_got.at[last + 1]).start()
+
+                    @pl.when(jnp.logical_not(keeps))
+                    def _():
+                        final_hop(b).start()
+
+    def final_hop(b):
+        return push(
+            gain_buf.at[last], gain_buf.at[last + 1], gr_hop_sent.at[last + b], gr_hop_got.at[last + 1],
+            (r, z, 2 * y + b),
+        )
+
+    def y3_home(k):
+        return k, y3_k.at[strip(k, rows), :], block_out, blk_sent, blk_got
+
+    @pl.when(at.decodes)
+    def _():
+        copies = [copying("act", act_k, a_v), copying("late", late_k, mid_v)]
+        for copy in copies:
+            copy.start()
+        sent(4)
+        for copy in copies:
+            copy.wait()
+
+        def to_out(q):
+            return mm_nt(a_v[0, q, :], dn_v[0]) + mm_nt(a_v[1, q, :], dn_v[1])
+
+        def far_out(n):
+            i = 2 * (1 - c) + n
+            q = strip(i, BLOCK)
+            send_v[0, q, :] = to_out(q).astype(LOW)
+            exchange(6, i).start()
+
+        each(2, far_out)
+
+        def near_out(n):
+            i = 2 * c + n
+            q = strip(i, BLOCK)
+            part = to_out(q)
+            exchange(6, i).wait_recv()
+            out_st[strip(n, BLOCK), :] = (mid_v[q, :] + part + recv_v[0, q, :].astype(WIDE)).astype(LOW)
+
+        each(2, near_out)
+        y3_put = copying("out", out_st, y3_k)
+        y3_put.start()
+        y3_put.wait()
+        for k in range(2):
+            go_home(*y3_home(k))
+
+    for n in range(planes):
+        add_enc(1)
+        add_dec(2)
+        gain_step(n)
+    add_enc(9)
+    add_dec(99)
+
+    for s in range(2):
+        for goal, got in ((block_out, blk_got), (grad_out, gr_got)):
+            push(goal.at[s], goal.at[s], blk_sent.at[0], got.at[s], at.twin).wait_recv()
+    push(gain_buf.at[last], gain_buf.at[last + 1], gr_hop_sent.at[last], gr_hop_got.at[last + 1], at.twin).wait_recv()
+    gains_home = copying("gains", gain_buf.at[last + 1], gain_out)
+    gains_home.start()
+    gains_home.wait()
+    for i, g in enumerate(SUMS):
+        push(home[g], home[g], home_sent.at[i, 0], home_got.at[i], at.twin).wait_recv()
+    for k in range(2):
+        went_home(*grad_home(k))
+
+    @pl.when(at.encodes)
+    def _():
+        for k in range(2):
+            went_home(*memory_home(k))
+        sent(2)
+
+    @pl.when(at.decodes)
+    def _():
+        for k in range(2):
+            went_home(*y3_home(k))
+        each(2, lambda n: exchange(6, 2 * (1 - c) + n).wait_send())
+
+    each(2, lambda n: exchange(5, 2 * (1 - c) + n).wait_send())
+
+    @pl.when(relay)
+    def _():
+        for b in range(2):
+            pl.when(jnp.logical_not(both(c == r, r == b)))(lambda: final_hop(b).wait_send())
+
+    for g in SUMS:
+        there = at.decodes if g == "crs" else jnp.logical_or(at.decodes, at.encodes)
+
+        @pl.when(both(other, there))
+        def _():
+            for k in range(planes):
+                y_hop(g, k).wait_send()
+
+        @pl.when(both(relay, there))
+        def _():
+            for k in range(planes - 1):
+                z_hop(g, k).wait_send()
+            for keeps, source, dev, n in homes(g):
+
+                @pl.when(jnp.logical_not(keeps))
+                def _():
+                    i = SUMS.index(g)
+                    push(source, home[g], home_sent.at[i, n], home_got.at[i], dev).wait_send()
+
+    gain_copy.wait_send()
+    for g in DIRECT:
+        launch_over(g).wait_send()
+
+    @pl.when(jnp.logical_not(stays))
+    def _():
+        for g in ("att", "up", "dn"):
+            push(shard[g], vmem[g].at[r, here, :], x_sent.at[GROUPS.index(g)], x_sem.at[0, 0], relay_dev).wait_send()
+
+    @pl.when(jnp.logical_not(crs_stays))
+    def _():
+        push(crs_in, crs_goal(r, c), x_sent.at[1], c_sem.at[0, 0], crs_dev).wait_send()
+        push(cot_in.at[c], cot_goal, row_sent.at[2], cot_got.at[r], at.twin).wait_send()
+
+    for s in range(2):
+
+        @pl.when(jnp.logical_not(row_stays(s)))
+        def _():
+            push(x_in.at[s], row_goal, row_sent.at[s], row_got.at[r], at.twin).wait_send()
+
+    for g in GROUPS:
+        member = both(relay, at.decodes) if g == "crs" else relay
+
+        @pl.when(member)
+        def _():
+            for k in range(planes):
+                for b in range(2):
+                    if k:
+                        ring(g, k, b).wait_send()
+                    if k or g not in DIRECT:
+                        cross_over(g, k, b).wait_send()
+
+
+def block_call(planes, slot, width, hidden, depth, args):
+    shape = jax.ShapeDtypeStruct
+    rows = slot // 4
+    square = (slot, width)
+    wides = {"ffn": 2 * hidden, "crs": width, "att": width}
+    packed, outs, logs, acts = (2, slot, 640), (2, slot, 256), (8, slot), (2, slot, hidden)
+    out_shape = (
+        [shape((2, rows, width), LOW)] * 2
+        + [shape((depth, 2 * hidden), LOW), shape((depth, width // 2), LOW), shape((depth, width), LOW)]
+        + [shape((8, width), WIDE)]
+        + [shape(square, LOW)] * 4
+        + [shape(square, WIDE), shape(square, LOW)]
+        + [shape(packed, LOW), shape(outs, LOW), shape(logs, WIDE)] * 2
+        + [shape(acts, LOW)]
+        + [shape((2 * rows, width), LOW)] * 2
+        + [shape((planes, 2, depth, wides[g]), LOW) for g in SUMS] * 3
+    )
+    dma = pltpu.SemaphoreType.DMA
+    v = pltpu.VMEM
+    groups = len(GROUPS)
+    scratch = (
+        [v((2, width, width), LOW)] * 2
+        + [v((2, width, hidden), LOW)] * 2
+        + [v(acts, LOW)] * 2
+        + [v(outs, LOW)] * 2
+        + [v(square, WIDE)] * 2
+        + [v(square, LOW)] * 3
+        + [v((width, slot), LOW)] * 3
+        + [v((2,) + square, LOW)] * 2
+        + [v((slot, TILE), LOW)] * 4
+        + [v((TILE, slot), LOW), v(logs, WIDE), v((8, width), WIDE), v((2, 8, width), WIDE)]
+        + [v((planes + 6, 8, width), WIDE)]
+        + [v((2 * rows, width), LOW), v((2, 2, depth, 2 * hidden), LOW), v((3, 2, depth, 2 * hidden), LOW)]
+        + [dma((groups, 2)), dma((groups,)), dma((groups,)), dma((2, 2))]
+        + [dma((groups, planes, 2))] * 4
+        + [dma((2,)), dma((3,)), dma((4,)), dma((2,)), dma((3,)), dma((24,)), dma((7, 4)), dma((7, 4))]
+        + [dma((2,))] * 8
+        + [dma((3, planes))] * 4
+        + [dma((3,)), dma((3, 4))]
+        + [dma((2,))] * 4
+        + [dma((planes + 6,))] * 2
+        + [dma((3,)), dma((2,))]
+    )
+    any_spec = pl.BlockSpec(memory_space=pl.ANY)
+    vmem_spec = pl.BlockSpec(memory_space=pltpu.VMEM)
+    return pl.pallas_call(
+        functools.partial(block_kernel, planes),
+        out_shape=out_shape,
+        in_specs=[any_spec] * 6 + [vmem_spec] * 3,
+        out_specs=[any_spec] * len(out_shape),
+        scratch_shapes=scratch,
+        compiler_params=pltpu.CompilerParams(collective_id=0, has_side_effects=True, vmem_limit_bytes=VMEM_BYTES),
+    )(*args)
+
+
 def ring_gather(lay, shard):
     planes = lay.planes
     rows = shard.shape[1]
+    if planes > 4:
+        piece = lax.all_gather(shard, "dp", axis=1, tiled=True)
+        across = lay.route(piece, lambda c, z, t: (c, z, (t + 2) % 4) if c == t // 2 else None)
+        return jnp.where(lay.relays, piece, across)
     relay = lambda c, z, t: (c, (z + 1) % planes, t) if c == t // 2 else None
     whole = jnp.zeros((shard.shape[0], planes * rows, shard.shape[2]), shard.dtype)
     piece = shard
@@ -148,6 +1385,8 @@
         low, lambda c, z, t: (c, z, (t + 2) % 4) if (c != t // 2 and t % 2 == holder) else None
     )
     summed = low.astype(WIDE) + across.astype(WIDE)
+    if planes > 4:
+        return lax.psum_scatter(summed.astype(LOW), "dp", scatter_dimension=1, tiled=True)
     relay = lambda c, z, t: (c, (z + 1) % planes, t) if (c == t // 2 and t % 2 == holder) else None
     take = lambda j: lax.dynamic_slice_in_dim(summed, (j % planes) * rows, rows, 1)
     running = take(lay.plane - 1)
@@ -166,7 +1405,7 @@
     return same.astype(WIDE) + beside.astype(WIDE)
 
 
-def body(block_input, w_self, w_self_out, w_cross, w_up, w_down, norm_gains, lengths, task_mask, out_grad):
+def general_body(block_input, w_self, w_self_out, w_cross, w_up, w_down, norm_gains, lengths, task_mask, out_grad):
     lay = Layout()
     seqs, rows, width = block_input.shape[1:]
     slot = rows * lay.chips
@@ -382,6 +1621,77 @@
     )
 
 
+def body(block_input, w_self, w_self_out, w_cross, w_up, w_down, norm_gains, lengths, task_mask, out_grad):
+    lay = Layout()
+    seqs, rows, width = block_input.shape[1:]
+    slot = rows * lay.chips
+    sec = lay.core
+    item = lay.item
+
+    if lay.planes != 4:
+        return general_body(
+            block_input, w_self, w_self_out, w_cross, w_up, w_down, norm_gains, lengths, task_mask, out_grad
+        )
+
+    depth = w_self.shape[1]
+    wide = w_self.shape[3]
+    hidden = w_up.shape[2]
+    self_block = pack_heads(
+        {"q": w_self[0, :, 0], "k": w_self[0, :, 1], "v": w_self[0, :, 2], "o": w_self_out[0].T}
+    )
+    pair = {"q": w_cross[0, :, 0], "o": w_cross[0, :, 1], "k": w_cross[0, :, 0], "v": w_cross[0, :, 1]}
+    pieces = [pair[n][:, HEAD * h : HEAD * (h + 1)] for n, h in ORDER]
+    cross_block = jnp.where(
+        sec == 1, jnp.concatenate(pieces[:6], axis=1), jnp.concatenate(pieces[6:], axis=1)
+    )
+    gain_block = jnp.concatenate([norm_gains[0].astype(WIDE), jnp.zeros((5, width), WIDE)], axis=0)
+
+    positions = jnp.arange(slot)
+    own_length = jnp.where(lay.is_decoder, lengths[1, item], lengths[0, item])
+
+    def key_bias(allowed):
+        return jnp.broadcast_to(jnp.where(allowed, 0.0, NEG_FILL)[:, None], (slot, TILE)).astype(LOW)
+
+    biases = (
+        key_bias(positions < own_length),
+        key_bias((positions < lengths[0, item]) & (task_mask[item] == 1)),
+    )
+    block_output, input_grad, home_feed, home_cross, home_self, gain_total = block_call(
+        lay.planes,
+        slot,
+        width,
+        hidden,
+        depth,
+        (self_block, cross_block, w_up[0], w_down[0].T, block_input[0], out_grad, gain_block) + biases,
+    )[:6]
+    home_self, home_feed, home_cross = (v.astype(WIDE) for v in (home_self, home_feed, home_cross))
+    g_self = jnp.stack([unpack_heads(home_self, n) for n in "qkv"], axis=1)[None]
+    g_self_out = unpack_heads(home_self, "o").T[None]
+    halves = (ORDER[:6], ORDER[6:])
+    take = lambda order, name: jnp.concatenate(
+        [home_cross[:, HEAD * order.index((name, h)) : HEAD * (order.index((name, h)) + 1)] for h in range(3)], axis=1
+    )
+    g_cross = jnp.where(
+        sec == 1,
+        jnp.stack([take(halves[0], "q"), take(halves[0], "o")], axis=1),
+        jnp.stack([take(halves[1], "k"), take(halves[1], "v")], axis=1),
+    )[None]
+    g_up = home_feed[:, :hidden][None]
+    g_down = home_feed[:, hidden:].T[None]
+    gain_total = gain_total[None]
+    return (
+        block_output[None],
+        input_grad.astype(WIDE)[None],
+        g_self,
+        g_self_out,
+        g_cross,
+        g_up,
+        g_down,
+        gain_total[:, :2],
+        gain_total[:, 2],
+    )
+
+
 def solution(mesh):
     placed = (
         P("section", "dp", "tensor", None),

time: 866 us -> 378 us (0.44)
  the two profiles are of different devices: /device:TPU:2 before, /device:TPU:1 now
where the time goes in v4:
time: 378 us; the launch traced here: 371 us
  Pallas kernels  346 us (92%)
  local copies, waits for them, and re-layouts  14.9 us (4%)
  other arithmetic  6.9 us (2%)
    pallas_call x1, Pallas kernels, block_call(): pl.pallas_call(functools.partial(block_kernel, planes), out_shape=out_sha...  346 us

profile of v4, /device:TPU:1, one launch (start us, length us, event | category | flops | bytes accessed | tf_op | source)
XLA Modules:
  0.0 370.6 jit_solution(16507362485924756255)
XLA Ops:
  0.7 0.8 compare_reduce_fusion
  1.5 1.3 constant_dynamic-slice_fusion
  4.1 0.7 select_convert_fusion
  4.8 1.3 pad_convert_fusion.gain_in
  6.1 1.0 copy.19
  7.1 0.9 broadcast_in_dim.50.bias_self
  8.0 0.9 broadcast_in_dim.51.bias_cross
  8.9 1.0 slice_bitcast_fusion.4
  10.0 0.8 concatenate.58.self_in
  10.8 0.3 fusion.3
  11.2 0.8 maximum_select_fusion.1.crs_in
  12.0 346.3 %shard_map.169 = (bf16[2,256,768]{2,1,0:T(8,128)(2,1)}, bf16[2,256,768]{2,1,0:T(8,128)(2,1)}, bf16[192,1536]{1,0:T(8,128)(2,1)}, bf16[192,384]{1,0:T(8,128)(2,1)...) custom-call(bf16[192,768]{1,0:T(8,128)(2,1)} %concatenate.58.self_in, ...), custom_call_target="tpu_custom_call" | custom-call | tf_op jit(solution)/shard_map/pallas_call | solution.py:1351
  358.3 1.4 slice_bitcast_fusion.7
  359.7 1.3 slice.200
  361.0 0.9 convert_element_type.24
  362.0 1.0 fusion.2
  362.9 0.9 fusion.1
  363.9 0.8 copy.22
  364.8 0.9 maximum_bitcast_fusion
  365.9 1.1 copy.23
  367.0 0.1 convert_element_type.25
  367.1 1.1 slice_bitcast_fusion
  368.2 1.3 bitcast_convert_fusion
  369.5 0.9 copy.29
  (36 shorter events, 0.5 us)
Async XLA Ops:
  0.6 10.2 %copy-start.3 = (bf16[1,192,2,192]{3,2,1,0:T(2,128)(2,1)S(1)}, bf16[1,192,2,192]{3,2,1,0:T(2,128)(2,1)}, u32[]{:S(2)}) copy-start(bf16[1,192,2,192]{3,2,1,0:T(2,128)(2,1)} %param.13) | copy-start | bytes 442372
  358.3 6.4 %copy-start.1 = (bf16[192,768]{1,0:T(8,128)(2,1)S(1)}, bf16[192,768]{1,0:T(8,128)(2,1)}, u32[]{:S(2)}) copy-start(bf16[192,768]{1,0:T(8,128)(2,1)} %get-tuple-element.17) | copy-start | bytes 884740
  362.9 2.7 copy-start
  365.7 1.3 copy-start.5
  365.9 2.3 copy-start.4
  367.1 2.4 copy-start.2
